TPU v7x, 32 devices: a whole 2x2x4 slice. The times are simulated.
32 devices in a mesh: section: 2 (over core), dp: 16 (over z, y, x).
Axes of the slice: x: 2, y: 2, z: 4, core: 2. Of those that a mesh axis runs over, the one named last changes fastest.
Arguments:
- tokens: bfloat16 [128, 256, 512], P('dp'), may hold values from -6 to 6
- out_cotangent: bfloat16 [128, 256, 512], P('dp'), may hold values from -8 to 8
- speaker: int32 [128], P('dp'), may hold values from 0 to 2559
- valid: int32 [128], P('dp'), may hold values 0 or 1
- conv_weight: float32 [2, 7, 512], P('section'), may hold values from -2 to 2
- conv_bias: float32 [2, 512], P('section'), may hold values from -3 to 3
- scale_table: float32 [2, 2560, 512], P('section'), may hold values from 0.1 to 1.9
- shift_table: float32 [2, 2560, 512], P('section'), may hold values from -3 to 3
- up_weight: bfloat16 [2, 512, 1536], P('section'), may hold values from -0.25 to 0.25
- up_bias: float32 [2, 1536], P('section'), may hold values from -3 to 3
- down_weight: bfloat16 [2, 1536, 512], P('section'), may hold values from -0.15625 to 0.15625
- down_bias: float32 [2, 512], P('section'), may hold values from -3 to 3
- layer_scale: float32 [2, 512], P('section'), may hold values from 0.5 to 1.5
Outputs:
- block_outputs: bfloat16 [2, 128, 256, 512], P('section', 'dp')
- input_grads: bfloat16 [2, 128, 256, 512], P('section', 'dp')
- grad_conv_weight: float32 [2, 7, 512], P('section', None, 'dp')
- grad_conv_bias: float32 [2, 512], P('section', 'dp')
- grad_scale_table: float32 [2, 2560, 512], P('section', 'dp')
- grad_shift_table: float32 [2, 2560, 512], P('section', 'dp')
- grad_up_weight: float32 [2, 512, 1536], P('section', 'dp')
- grad_up_bias: float32 [2, 1536], P('section', 'dp')
- grad_down_weight: float32 [2, 1536, 512], P('section', 'dp')
- grad_down_bias: float32 [2, 512], P('section', 'dp')
- grad_layer_scale: float32 [2, 512], P('section', 'dp')
All inputs are finite; a program needn't handle non-finite values. No bound on the sum of `valid` on one device may be relied on, other than what follows from the above.
Results may differ from a plain program's by a relative error of at most 0.0074.
Values may be sent and summed in bfloat16 or wider, within the bound.
No kernel may reach another device: no remote copies, remote signals or barrier semaphores. Data moves between devices by JAX's collectives and lax.ppermute only.
A program may use at most 192 MiB of HBM per device.

v0:
```python
import jax
import jax.numpy as jnp
from jax import lax
from jax.sharding import PartitionSpec as P

MICRO = 4


highest = lax.Precision.HIGHEST


def shifted(block, axis, distance):
    devices = range(lax.axis_size(axis))
    route = [(i - distance, i) for i in devices if i - distance in devices]
    return lax.ppermute(block, axis, route)


def prepare(inputs, kernel_taps, conv_shift, scale_rows, shift_rows):
    frames = inputs.shape[1]
    padded = jnp.pad(inputs, ((0, 0), (3, 3), (0, 0)))
    conv = conv_shift + padded[:, 0:frames, :] * kernel_taps[0]
    for offset in range(1, kernel_taps.shape[0]):
        conv = conv + padded[:, offset : offset + frames, :] * kernel_taps[offset]
    centred = conv - jnp.mean(conv, axis=-1, keepdims=True)
    normed = centred * lax.rsqrt(jnp.mean(centred * centred, axis=-1, keepdims=True) + 1e-06)
    return normed * scale_rows[:, None, :] + shift_rows[:, None, :]


def gelu_exact(values):
    return jax.nn.gelu(values, approximate=False)


def local(
    tokens,
    out_cotangent,
    speaker,
    valid,
    conv_weight,
    conv_bias,
    scale_table,
    shift_table,
    up_weight,
    up_bias,
    down_weight,
    down_bias,
    layer_scale,
):
    section = lax.axis_index("section")
    first_section = section == 0
    clips, frames, width = tokens.shape
    hidden_width = up_weight.shape[2]
    table_size = scale_table.shape[1]
    slots = clips // MICRO
    rows = slots * frames
    kernel_taps = conv_weight[0]
    conv_shift = conv_bias[0]
    up_mat = up_weight[0]
    up_shift = up_bias[0]
    down_mat = down_weight[0]
    down_shift = down_bias[0]
    gains = layer_scale[0]
    owners = (speaker[:, None] == jnp.arange(table_size, dtype=jnp.int32)[None, :]).astype(
        jnp.float32
    )
    scale_rows_all = jnp.dot(owners, scale_table[0], precision=highest)
    shift_rows_all = jnp.dot(owners, shift_table[0], precision=highest)
    clip_weights = valid.astype(jnp.float32)
    inputs_all = tokens
    outputs_all = jnp.zeros_like(tokens)
    saved_pre = jnp.zeros((MICRO, rows, hidden_width), jnp.float32)
    saved_branch = jnp.zeros((MICRO, rows, width), jnp.float32)
    received = jnp.zeros((slots, frames, width), jnp.bfloat16)
    for moment in range(MICRO + 1):
        index = moment - section
        active = (index >= 0) & (index < MICRO)
        place = jnp.clip(index, 0, MICRO - 1)
        first_row = place * slots
        own_inputs = lax.dynamic_slice_in_dim(tokens, first_row, slots, 0)
        inputs_now = jnp.where(first_section, own_inputs, received)
        scale_part = lax.dynamic_slice_in_dim(scale_rows_all, first_row, slots, 0)
        shift_part = lax.dynamic_slice_in_dim(shift_rows_all, first_row, slots, 0)
        inputs_float = inputs_now.astype(jnp.float32)
        adapted = prepare(inputs_float, kernel_taps, conv_shift, scale_part, shift_part)
        adapted_low = adapted.reshape(rows, width).astype(jnp.bfloat16)
        hidden_pre = jnp.dot(adapted_low, up_mat, preferred_element_type=jnp.float32) + up_shift
        activated_low = gelu_exact(hidden_pre).astype(jnp.bfloat16)
        branch = jnp.dot(activated_low, down_mat, preferred_element_type=jnp.float32) + down_shift
        result = (inputs_float + gains * branch.reshape(slots, frames, width)).astype(jnp.bfloat16)
        old_inputs = lax.dynamic_slice_in_dim(inputs_all, first_row, slots, 0)
        inputs_all = lax.dynamic_update_slice_in_dim(
            inputs_all, jnp.where(active, inputs_now, old_inputs), first_row, 0
        )
        old_outputs = lax.dynamic_slice_in_dim(outputs_all, first_row, slots, 0)
        outputs_all = lax.dynamic_update_slice_in_dim(
            outputs_all, jnp.where(active, result, old_outputs), first_row, 0
        )
        old_pre = lax.dynamic_index_in_dim(saved_pre, place, 0, keepdims=False)
        saved_pre = lax.dynamic_update_index_in_dim(
            saved_pre, jnp.where(active, hidden_pre, old_pre), place, 0
        )
        old_branch = lax.dynamic_index_in_dim(saved_branch, place, 0, keepdims=False)
        saved_branch = lax.dynamic_update_index_in_dim(
            saved_branch, jnp.where(active, branch, old_branch), place, 0
        )
        if moment < MICRO:
            received = shifted(result, "section", 1)
    grad_in_all = jnp.zeros_like(tokens)
    clip_rows = jnp.zeros((clips, 2 * width), jnp.float32)
    sum_taps = jnp.zeros_like(kernel_taps)
    sum_conv = jnp.zeros_like(conv_shift)
    sum_up = jnp.zeros((width, hidden_width), jnp.float32)
    sum_up_shift = jnp.zeros((hidden_width,), jnp.float32)
    sum_down = jnp.zeros((hidden_width, width), jnp.float32)
    sum_down_shift = jnp.zeros((width,), jnp.float32)
    sum_gains = jnp.zeros((width,), jnp.float32)
    back_received = jnp.zeros((slots, frames, width), jnp.bfloat16)
    for moment in range(MICRO + 1):
        index = moment - 1 + section
        active = (index >= 0) & (index < MICRO)
        place = jnp.clip(index, 0, MICRO - 1)
        first_row = place * slots
        inputs_now = lax.dynamic_slice_in_dim(inputs_all, first_row, slots, 0)
        cot_part = lax.dynamic_slice_in_dim(out_cotangent, first_row, slots, 0).astype(jnp.float32)
        weight_part = lax.dynamic_slice_in_dim(clip_weights, first_row, slots, 0) * active.astype(
            jnp.float32
        )
        grad_out = jnp.where(
            first_section, back_received.astype(jnp.float32), cot_part * weight_part[:, None, None]
        )
        scale_part = lax.dynamic_slice_in_dim(scale_rows_all, first_row, slots, 0)
        shift_part = lax.dynamic_slice_in_dim(shift_rows_all, first_row, slots, 0)
        adapted, pull_prepare = jax.vjp(
            prepare, inputs_now.astype(jnp.float32), kernel_taps, conv_shift, scale_part, shift_part
        )
        adapted_low = adapted.reshape(rows, width).astype(jnp.bfloat16)
        hidden_pre = lax.dynamic_index_in_dim(saved_pre, place, 0, keepdims=False)
        activated, pull_gelu = jax.vjp(gelu_exact, hidden_pre)
        activated_low = activated.astype(jnp.bfloat16)
        branch = lax.dynamic_index_in_dim(saved_branch, place, 0, keepdims=False)
        grad_flat = grad_out.reshape(rows, width)
        grad_branch = (grad_flat * gains).astype(jnp.bfloat16)
        grad_act = jnp.einsum(
            "td,hd->th", grad_branch, down_mat, preferred_element_type=jnp.float32
        )
        grad_pre = pull_gelu(grad_act)[0].astype(jnp.bfloat16)
        grad_adapted = jnp.einsum("th,dh->td", grad_pre, up_mat, preferred_element_type=jnp.float32)
        grad_inputs, grad_taps, grad_conv, grad_scale, grad_shift = pull_prepare(
            grad_adapted.reshape(slots, frames, width)
        )
        grad_total = (grad_out + grad_inputs).astype(jnp.bfloat16)
        if moment < MICRO:
            back_received = shifted(grad_total, "section", -1)
        old_grads = lax.dynamic_slice_in_dim(grad_in_all, first_row, slots, 0)
        grad_in_all = lax.dynamic_update_slice_in_dim(
            grad_in_all, jnp.where(active, grad_total, old_grads), first_row, 0
        )
        new_rows = jnp.concatenate([grad_scale, grad_shift], axis=1)
        old_rows = lax.dynamic_slice_in_dim(clip_rows, first_row, slots, 0)
        clip_rows = lax.dynamic_update_slice_in_dim(
            clip_rows, jnp.where(active, new_rows, old_rows), first_row, 0
        )
        sum_taps = sum_taps + grad_taps
        sum_conv = sum_conv + grad_conv
        sum_gains = sum_gains + jnp.sum(grad_flat * branch, axis=0)
        sum_down_shift = sum_down_shift + jnp.sum(grad_branch.astype(jnp.float32), axis=0)
        sum_down = sum_down + jnp.einsum(
            "th,td->hd", activated_low, grad_branch, preferred_element_type=jnp.float32
        )
        sum_up_shift = sum_up_shift + jnp.sum(grad_pre.astype(jnp.float32), axis=0)
        sum_up = sum_up + jnp.einsum(
            "td,th->dh", adapted_low, grad_pre, preferred_element_type=jnp.float32
        )
    table_scale = jnp.einsum("ce,cd->ed", owners, clip_rows[:, :width], precision=highest)
    table_shift = jnp.einsum("ce,cd->ed", owners, clip_rows[:, width:], precision=highest)
    shares = (
        lax.psum_scatter(sum_taps, "dp", scatter_dimension=1, tiled=True),
        lax.psum_scatter(sum_conv, "dp", scatter_dimension=0, tiled=True),
        lax.psum_scatter(table_scale, "dp", scatter_dimension=0, tiled=True),
        lax.psum_scatter(table_shift, "dp", scatter_dimension=0, tiled=True),
        lax.psum_scatter(sum_up, "dp", scatter_dimension=0, tiled=True),
        lax.psum_scatter(sum_up_shift, "dp", scatter_dimension=0, tiled=True),
        lax.psum_scatter(sum_down, "dp", scatter_dimension=0, tiled=True),
        lax.psum_scatter(sum_down_shift, "dp", scatter_dimension=0, tiled=True),
        lax.psum_scatter(sum_gains, "dp", scatter_dimension=0, tiled=True),
    )
    (
        share_taps,
        share_conv,
        share_scale,
        share_shift,
        share_up,
        share_up_shift,
        share_down,
        share_down_shift,
        share_gains,
    ) = shares
    return (
        outputs_all[None],
        grad_in_all[None],
        share_taps[None],
        share_conv[None],
        share_scale[None],
        share_shift[None],
        share_up[None],
        share_up_shift[None],
        share_down[None],
        share_down_shift[None],
        share_gains[None],
    )


def solution(mesh):
    placed = (
        P("dp", None, None),
        P("dp", None, None),
        P("dp"),
        P("dp"),
        P("section", None, None),
        P("section", None),
        P("section", None, None),
        P("section", None, None),
        P("section", None, None),
        P("section", None),
        P("section", None, None),
        P("section", None),
        P("section", None),
    )
    return jax.shard_map(
        local,
        mesh=mesh,
        in_specs=placed,
        out_specs=(
            P("section", "dp", None, None),
            P("section", "dp", None, None),
            P("section", None, "dp"),
            P("section", "dp"),
            P("section", "dp", None),
            P("section", "dp", None),
            P("section", "dp", None),
            P("section", "dp"),
            P("section", "dp", None),
            P("section", "dp"),
            P("section", "dp"),
        ),
        check_vma=False,
    )
```

profile of v0, /device:TPU:0, one launch (start us, length us, event | category | flops | bytes accessed | tf_op | source)
XLA Modules:
  0.0 870.3 jit_solution(15676582953614913422)
XLA Ops:
  8.2 4.8 fusion
  22.3 2.5 broadcast_in_dim.324
  24.8 7.8 bitcast_dynamic-update-slice_fusion.9
  34.1 2.3 select_dynamic-update-slice_fusion.11
  36.4 2.6 collective-permute-start
  42.5 2.2 select_dynamic-update-slice_fusion.7
  46.4 2.7 bitcast_dynamic-update-slice_fusion.3
  49.1 7.7 bitcast_dynamic-update-slice_fusion.8
  68.0 2.7 bitcast_dynamic-update-slice_fusion.2
  70.7 7.8 bitcast_dynamic-update-slice_fusion.7
  90.3 2.6 bitcast_dynamic-update-slice_fusion.1
  92.9 7.7 bitcast_dynamic-update-slice_fusion.6
  106.8 2.3 constant_dynamic-slice_fusion.32
  111.2 2.2 select_dynamic-update-slice_fusion.4
  113.4 4.0 dynamic-slice_convert_fusion
  118.6 11.3 %fusion.802 = (f32[2,256]{1,0:T(2,128)S(1)}, f32[2,256,512]{2,1,0:T(8,128)S(1)}, f32[2,256]{1,0:T(2,128)S(1)}, f32[2,256,512]{2,1,0:T(8,128)S(1)}, f32[2,256]{1,...) fusion(f32[512]{0:T(512)S(1)} %bitcast.701, ...), kind=kLoop, calls=%fused_computation.1240 | loop fusion | flops 19658240 | bytes 10512384 | tf_op jit(solution)/shard_map/jvp()/reduce_sum | solution.py:24
  130.5 3.6 bitcast_dynamic-update-slice_fusion
  134.2 10.2 %convert_reduce_fusion.4 = (f32[1536]{0:T(1024)}, bf16[512,1536]{1,0:T(8,128)(2,1)S(1)}) fusion(bf16[512,512]{1,0:T(8,128)(2,1)S(1)} %bitcast.663, bf16[1,1536,512]{2,1,0:T(8,128)(2,1)S(1)} %copy-done.103, f32[4,512,1536]{2,1,0:T(8,128)} %get-tuple-element.253, s32[]{:T(128)S(6)} %min.36), kind=kOutput, calls=%fused_computation.210 | convolution fusion | flops 863500800 | bytes 6821892 | tf_op jit(solution)/shard_map/td,hd->th/dot_general | solution.py:142
  144.4 8.7 fusion.213
  153.4 2.6 multiply_reduce_fusion.9
  162.8 9.7 %bitcast_dynamic-update-slice_fusion.5 = (f32[4,512,512]{2,1,0:T(8,128)}, f32[512,512]{1,0:T(8,128)}) fusion(f32[4,512,512]{2,1,0:T(8,128)} %get-tuple-element.264, s32[]{:T(128)S(6)} %min.35, f32[1,512,512]{2,1,0:T(8,128)S(1)} %copy-done.39, pred[]{:T(512)S(6)} %and.35, f32[512]{0:T(512)S(1)} %bitcast.798, bf16[1,1536,512]{2,1,0:T(8,128)(2,1)S(1)} %copy-done.104, ...), kind=kOutput, calls=%fused_computation.592 | convolution fusion | flops 856948736 | bytes 7866373 | tf_op jit(solution)/shard_map/dot_general | solution.py:87
  172.5 4.5 constant_dynamic-slice_fusion.17
  179.8 9.0 %convert_reduce_fusion.3 = (f32[1536]{0:T(1024)}, bf16[512,1536]{1,0:T(8,128)(2,1)S(1)}) fusion(bf16[512,512]{1,0:T(8,128)(2,1)S(1)} %bitcast.661, bf16[1,1536,512]{2,1,0:T(8,128)(2,1)S(1)} %copy-done.105, f32[4,512,1536]{2,1,0:T(8,128)S(1)} %copy-done.2, s32[]{:T(128)S(6)} %min.37), kind=kOutput, calls=%fused_computation.209 | convolution fusion | flops 863500800 | bytes 6821892 | tf_op jit(solution)/shard_map/td,hd->th/dot_general | solution.py:142
  188.8 2.6 multiply_reduce_fusion.8
  195.8 10.2 %convolution_add_fusion.3 = f32[1536,512]{1,0:T(8,128)} fusion(f32[1536,512]{1,0:T(8,128)} %fusion.213, bf16[512,512]{1,0:T(8,128)(2,1)S(1)} %bitcast.662, f32[4,512,1536]{2,1,0:T(8,128)S(1)} %copy-done.2, s32[]{:T(128)S(6)} %min.37), kind=kOutput, calls=%fused_computation.22 | convolution fusion | flops 857210880 | bytes 9961476 | tf_op jit(solution)/shard_map/th,td->hd/dot_general | solution.py:166
  208.0 9.0 %convert_reduce_fusion.2 = (f32[1536]{0:T(1024)}, bf16[512,1536]{1,0:T(8,128)(2,1)S(1)}) fusion(bf16[512,512]{1,0:T(8,128)(2,1)S(1)} %bitcast.656, bf16[1,1536,512]{2,1,0:T(8,128)(2,1)S(1)} %copy-done.106, f32[4,512,1536]{2,1,0:T(8,128)S(1)} %copy-done.2, s32[]{:T(128)S(6)} %min.38), kind=kOutput, calls=%fused_computation.208 | convolution fusion | flops 863500800 | bytes 6821892 | tf_op jit(solution)/shard_map/td,hd->th/dot_general | solution.py:142
  218.2 2.6 multiply_reduce_fusion.7
  222.4 3.9 multiply_reduce_fusion.30
  226.3 4.4 select_dynamic-update-slice_fusion.1
  232.3 2.3 collective-permute-done.6
  236.2 8.6 convert_reduce_fusion.1
  244.9 2.6 multiply_reduce_fusion.6
  254.1 2.7 convolution_add_fusion.5
  257.4 8.4 convert_reduce_fusion
  268.5 2.5 multiply_reduce_fusion.16
  271.0 3.9 multiply_reduce_fusion.41
  276.2 5.1 convolution_add_fusion.4
  282.3 9.3 %convolution_add_fusion.2 = f32[1536,512]{1,0:T(8,128)S(1)} fusion(f32[1536,512]{1,0:T(8,128)} %convolution_add_fusion.3, bf16[512,512]{1,0:T(8,128)(2,1)S(1)} %bitcast.657, f32[4,512,1536]{2,1,0:T(8,128)} %get-tuple-element.253, s32[]{:T(128)S(6)} %min.38), kind=kOutput, calls=%fused_computation.21 | convolution fusion | flops 857210880 | bytes 9961476 | tf_op jit(solution)/shard_map/th,td->hd/dot_general | solution.py:166
  291.7 9.0 %convolution_add_fusion.1 = f32[1536,512]{1,0:T(8,128)S(1)} fusion(f32[1536,512]{1,0:T(8,128)S(1)} %convolution_add_fusion.2, bf16[512,512]{1,0:T(8,128)(2,1)S(1)} %bitcast.659, f32[4,512,1536]{2,1,0:T(8,128)} %get-tuple-element.253, s32[]{:T(128)S(6)} %min.39), kind=kOutput, calls=%fused_computation.20 | convolution fusion | flops 857210880 | bytes 9961476 | tf_op jit(solution)/shard_map/th,td->hd/dot_general | solution.py:166
  300.7 10.0 %convolution_add_fusion = f32[1536,512]{1,0:T(8,128)} fusion(f32[1536,512]{1,0:T(8,128)S(1)} %convolution_add_fusion.1, bf16[512,512]{1,0:T(8,128)(2,1)S(1)} %bitcast.666, f32[4,512,1536]{2,1,0:T(8,128)} %get-tuple-element.253, s32[]{:T(128)S(6)} %min.40), kind=kOutput, calls=%fused_computation.19 | convolution fusion | flops 857210880 | bytes 9961476 | tf_op jit(solution)/shard_map/th,td->hd/dot_general | solution.py:166
  311.5 4.6 fusion.480
  316.2 4.7 fusion.479
  328.8 78.4 %all-reduce.84 = (f32[512]{0:T(512)S(1)}, f32[1536]{0:T(1024)S(1)}, f32[512]{0:T(512)S(1)}, f32[512]{0:T(512)S(1)}) all-reduce(f32[512]{0:T(512)S(1)} %add_add_fusion.9, f32[1536]{0:T(1024)S(1)} %add_add_fusion.6, f32[512]{0:T(512)S(1)} %add_add_fusion.8, f32[512]{0:T(512)S(1)} %add_add_fusion.7), channel_id=3, replica_groups=mesh['section'=2,'dp'=16] {'dp'}, use_global_device_ids=true, to_apply=%region_71.72.clone | all-reduce | flops 3072 | bytes 24576
  409.5 5.0 bitcast_dynamic-update-slice_fusion.10
  415.9 74.1 %reduce-scatter.12.cloned.1.call-done = f32[32,1536]{1,0:T(8,128)} async-done(((f32[512,1536]{1,0:T(8,128)}), f32[32,1536]{1,0:T(8,128)}) %reduce-scatter.12.cloned.1.call-update) | async-done | bytes 196624 | tf_op jit(solution)/shard_map/reduce_scatter | solution.py:180
  490.1 136.6 %reduce-scatter.14.cloned.1.call-done = f32[96,512]{1,0:T(8,128)} async-done(((f32[1536,512]{1,0:T(8,128)}), f32[96,512]{1,0:T(8,128)}) %reduce-scatter.14.cloned.1.call-update) | async-done | bytes 196624 | tf_op jit(solution)/shard_map/reduce_scatter | solution.py:182
  626.7 117.4 %reduce-scatter.8.cloned.1.call-done = f32[160,512]{1,0:T(8,128)} async-done(((f32[2560,512]{1,0:T(8,128)}), f32[160,512]{1,0:T(8,128)}) %reduce-scatter.8.cloned.1.call-update) | async-done | bytes 327696 | tf_op jit(solution)/shard_map/reduce_scatter | solution.py:178
  744.1 119.3 %reduce-scatter.10.cloned.1.call-done = f32[160,512]{1,0:T(8,128)} async-done(((f32[2560,512]{1,0:T(8,128)}), f32[160,512]{1,0:T(8,128)}) %reduce-scatter.10.cloned.1.call-update) | async-done | bytes 327696 | tf_op jit(solution)/shard_map/reduce_scatter | solution.py:179
  (368 shorter events, 94.3 us)
Async XLA Ops:
  7.2 14.1 %copy-start = (bf16[1,512,1536]{2,1,0:T(8,128)(2,1)S(1)}, bf16[1,512,1536]{2,1,0:T(8,128)(2,1)}, u32[]{:S(2)}) copy-start(bf16[1,512,1536]{2,1,0:T(8,128)(2,1)} %param.21) | copy-start | bytes 4718596
  7.2 5.9 copy-start.81
  7.2 407.4 %reduce-scatter.16.cloned.1.call-start = ((), (), s32[]{:S(2)}) async-start(), calls=%async_computation.9 | async-start | bytes 278528
  7.3 5.8 copy-start.16
  22.3 10.3 %copy-start.1 = (f32[4,512,1536]{2,1,0:T(8,128)}, f32[4,512,1536]{2,1,0:T(8,128)S(1)}, u32[]{:S(2)}) copy-start(f32[4,512,1536]{2,1,0:T(8,128)S(1)} %get-tuple-element.245) | copy-start | bytes 37748740
  24.8 9.3 %copy-start.50 = (f32[1,512]{1,0:T(1,128)S(1)}, f32[1,512]{1,0:T(1,128)}, u32[]{:S(2)}) copy-start(f32[1,512]{1,0:T(1,128)} %param.25) | copy-start | bytes 6148
  36.4 6.0 collective-permute-start
  59.0 5.0 collective-permute-start.1
  80.6 5.8 collective-permute-start.2
  102.8 8.4 collective-permute-start.3
  117.4 12.6 %copy-start.7 = (f32[2,256,512]{2,1,0:T(8,128)}, f32[2,256,512]{2,1,0:T(8,128)S(1)}, u32[]{:S(2)}) copy-start(f32[2,256,512]{2,1,0:T(8,128)S(1)} %get-tuple-element.157) | copy-start | bytes 3145732
  130.0 47.0 %copy-start.9 = (f32[2,256,512]{2,1,0:T(8,128)}, f32[2,256,512]{2,1,0:T(8,128)S(1)}, u32[]{:S(2)}) copy-start(f32[2,256,512]{2,1,0:T(8,128)S(1)} %get-tuple-element.98) | copy-start | bytes 3145732
  134.2 10.2 %copy-start.2 = (f32[4,512,1536]{2,1,0:T(8,128)S(1)}, f32[4,512,1536]{2,1,0:T(8,128)}, u32[]{:S(2)}) copy-start(f32[4,512,1536]{2,1,0:T(8,128)} %get-tuple-element.253) | copy-start | bytes 37748740
  144.4 8.9 %copy-start.27 = (bf16[512,1536]{1,0:T(8,128)(2,1)}, bf16[512,1536]{1,0:T(8,128)(2,1)S(1)}, u32[]{:S(2)}) copy-start(bf16[512,1536]{1,0:T(8,128)(2,1)S(1)} %get-tuple-element.277) | copy-start | bytes 4718596
  144.4 8.9 %copy-start.63 = (f32[2,512]{1,0:T(2,128)S(1)}, f32[2,512]{1,0:T(2,128)}, u32[]{:S(2)}) copy-start(f32[2,512]{1,0:T(2,128)} %get-tuple-element.285) | copy-start | bytes 12292
  144.4 9.0 %copy-start.98 = (f32[2,512]{1,0:T(2,128)S(1)}, f32[2,512]{1,0:T(2,128)}, u32[]{:S(2)}) copy-start(f32[2,512]{1,0:T(2,128)} %get-tuple-element.207) | copy-start | bytes 12292
  161.2 17.6 %collective-permute-start.4 = (bf16[2,256,512]{2,1,0:T(8,128)(2,1)}, bf16[2,256,512]{2,1,0:T(8,128)(2,1)S(1)}, u32[]{:S(2)}, u32[]{:S(2)}) collective-permute-start(bf16[2,256,512]{2,1,0:T(8,128)(2,1)} %get-tuple-element.118), channel_id=1, source_target_pairs={{16,0},{17,1},{18,2},{19,3},{20,4},{21,5},{22,6},{23,7},{24,8},{25... | collective-permute-start | bytes 1572872 | tf_op jit(solution)/shard_map/ppermute | solution.py:15
  179.7 9.1 %copy-start.46 = (bf16[2,256,512]{2,1,0:T(8,128)(2,1)}, bf16[2,256,512]{2,1,0:T(8,128)(2,1)S(1)}, u32[]{:S(2)}) copy-start(bf16[2,256,512]{2,1,0:T(8,128)(2,1)S(1)} %get-tuple-element.86) | copy-start | bytes 1572868
  179.7 9.1 %copy-start.62 = (f32[2,512]{1,0:T(2,128)S(1)}, f32[2,512]{1,0:T(2,128)}, u32[]{:S(2)}) copy-start(f32[2,512]{1,0:T(2,128)} %get-tuple-element.286) | copy-start | bytes 12292
  179.8 9.1 %copy-start.97 = (f32[2,512]{1,0:T(2,128)S(1)}, f32[2,512]{1,0:T(2,128)}, u32[]{:S(2)}) copy-start(f32[2,512]{1,0:T(2,128)} %get-tuple-element.206) | copy-start | bytes 12292
  194.3 11.7 %copy-start.35 = (bf16[512,1536]{1,0:T(8,128)(2,1)S(1)}, bf16[512,1536]{1,0:T(8,128)(2,1)}, u32[]{:S(2)}) copy-start(bf16[512,1536]{1,0:T(8,128)(2,1)} %copy-done.34) | copy-start | bytes 4718596
  194.4 11.7 %copy-start.38 = (bf16[2,256,512]{2,1,0:T(8,128)(2,1)S(1)}, bf16[2,256,512]{2,1,0:T(8,128)(2,1)}, u32[]{:S(2)}) copy-start(bf16[2,256,512]{2,1,0:T(8,128)(2,1)} %get-tuple-element.166) | copy-start | bytes 1572868
  194.4 12.7 %collective-permute-start.5 = (bf16[2,256,512]{2,1,0:T(8,128)(2,1)S(1)}, bf16[2,256,512]{2,1,0:T(8,128)(2,1)S(1)}, u32[]{:S(2)}, u32[]{:S(2)}) collective-permute-start(bf16[2,256,512]{2,1,0:T(8,128)(2,1)S(1)} %get-tuple-element.112), channel_id=1, source_target_pairs={{16,0},{17,1},{18,2},{19,3},{20,4},{21,5},{22,6},{23,7},{24,8},{25... | collective-permute-start | bytes 1572872 | tf_op jit(solution)/shard_map/ppermute | solution.py:15
  208.0 9.1 %copy-start.41 = (bf16[2,256,512]{2,1,0:T(8,128)(2,1)}, bf16[2,256,512]{2,1,0:T(8,128)(2,1)S(1)}, u32[]{:S(2)}) copy-start(bf16[2,256,512]{2,1,0:T(8,128)(2,1)S(1)} %get-tuple-element.90) | copy-start | bytes 1572868
  208.0 10.2 %copy-start.61 = (f32[2,512]{1,0:T(2,128)S(1)}, f32[2,512]{1,0:T(2,128)}, u32[]{:S(2)}) copy-start(f32[2,512]{1,0:T(2,128)} %get-tuple-element.287) | copy-start | bytes 12292
  208.0 10.2 %copy-start.96 = (f32[2,512]{1,0:T(2,128)S(1)}, f32[2,512]{1,0:T(2,128)}, u32[]{:S(2)}) copy-start(f32[2,512]{1,0:T(2,128)} %get-tuple-element.205) | copy-start | bytes 12292
  226.3 8.3 copy-start.19
  226.3 8.3 copy-start.20
  226.3 8.3 copy-start.85
  230.7 3.9 collective-permute-start.6
  236.2 8.6 copy-start.43
  236.2 8.7 copy-start.60
  236.2 8.7 copy-start.95
  251.3 5.6 collective-permute-start.7
  256.9 8.9 %copy-start.23 = (bf16[2,256,512]{2,1,0:T(8,128)(2,1)}, bf16[2,256,512]{2,1,0:T(8,128)(2,1)S(1)}, u32[]{:S(2)}) copy-start(bf16[2,256,512]{2,1,0:T(8,128)(2,1)S(1)} %collective-permute-done.7) | copy-start | bytes 1572868
  257.3 8.5 copy-start.48
  257.3 8.5 copy-start.10
  257.3 8.5 copy-start.54
  257.3 8.5 copy-start.59
  257.4 8.5 copy-start.65
  257.4 8.5 copy-start.94
  276.0 214.1 %reduce-scatter.12.cloned.1.call-start = ((), (), s32[]{:S(2)}) async-start(), calls=%async_computation.7 | async-start | bytes 3342336 | tf_op jit(solution)/shard_map/reduce_scatter | solution.py:180
  281.3 345.4 %reduce-scatter.14.cloned.1.call-start = ((), (), s32[]{:S(2)}) async-start(), calls=%async_computation.8 | async-start | bytes 3342336 | tf_op jit(solution)/shard_map/reduce_scatter | solution.py:182
  282.3 9.3 %copy-start.44 = (bf16[2,256,512]{2,1,0:T(8,128)(2,1)S(1)}, bf16[2,256,512]{2,1,0:T(8,128)(2,1)}, u32[]{:S(2)}) copy-start(bf16[2,256,512]{2,1,0:T(8,128)(2,1)} %copy-done.43) | copy-start | bytes 1572868
  291.7 9.0 %copy-start.49 = (bf16[2,256,512]{2,1,0:T(8,128)(2,1)S(1)}, bf16[2,256,512]{2,1,0:T(8,128)(2,1)}, u32[]{:S(2)}) copy-start(bf16[2,256,512]{2,1,0:T(8,128)(2,1)} %copy-done.48) | copy-start | bytes 1572868
  310.7 433.4 %reduce-scatter.8.cloned.1.call-start = ((), (), s32[]{:S(2)}) async-start(), calls=%async_computation.5 | async-start | bytes 5570560 | tf_op jit(solution)/shard_map/reduce_scatter | solution.py:178
  316.2 547.2 %reduce-scatter.10.cloned.1.call-start = ((), (), s32[]{:S(2)}) async-start(), calls=%async_computation.6 | async-start | bytes 5570560 | tf_op jit(solution)/shard_map/reduce_scatter | solution.py:179
  326.7 82.9 %copy-start.24 = (bf16[2,256,512]{2,1,0:T(8,128)(2,1)S(1)}, bf16[2,256,512]{2,1,0:T(8,128)(2,1)}, u32[]{:S(2)}) copy-start(bf16[2,256,512]{2,1,0:T(8,128)(2,1)} %copy-done.23) | copy-start | bytes 1572868
  (77 other events, 188.4 us)
Sparse Core Ops, SparseCore 0:
  276.1 79.9 reduce-scatter.15
  361.6 128.3 reduce-scatter.11
  495.6 131.0 reduce-scatter.13
  629.4 114.6 reduce-scatter.7
  746.8 116.5 reduce-scatter.9
where the time goes:
time: 880 us; the launch traced here: 870 us
  waiting for transfers between devices  450 us (51%)
  matrix products  184 us (21%)
  other arithmetic  83.7 us (10%)
  blocking collectives  78.4 us (9%)
  local copies, waits for them, and re-layouts  42.9 us (5%)
  between operations  17.1 us (2%)
  starting transfers between devices  14 us (2%)
    reduce_scatter x1, waiting for transfers between devices, local(): lax.psum_scatter(sum_down, 'dp', scatter_dimension=0, tiled=True)  137 us
    reduce_scatter x1, waiting for transfers between devices, local(): lax.psum_scatter(table_shift, 'dp', scatter_dimension=0, tiled=True)  119 us
    reduce_scatter x1, waiting for transfers between devices, local(): lax.psum_scatter(table_scale, 'dp', scatter_dimension=0, tiled=True)  117 us
    unnamed x1, blocking collectives  78.4 us
    reduce_scatter x1, waiting for transfers between devices, local(): lax.psum_scatter(sum_up, 'dp', scatter_dimension=0, tiled=True)  74.1 us
    dot_general x5, matrix products, local(): jnp.einsum('th,td->hd', activated_low, grad_branch, preferred_element_typ...  47.1 us
    dot_general x5, matrix products, local(): jnp.einsum('td,hd->th', grad_branch, down_mat, preferred_element_type=jnp...  45.3 us
    dot_general x5, matrix products, local(): jnp.dot(activated_low, down_mat, preferred_element_type=jnp.float32)  40.7 us
  transfers between devices with their start and end apart: 13, of which 5 were waited for; matrix products, arithmetic and copies ran while one was open for 12% of the time, Pallas kernels for 0%

commit v1 on v0

v1 whole, which is shorter than its diff:
```python
import functools

import jax
import jax.numpy as jnp
from jax import lax
from jax.experimental import pallas as pl
from jax.experimental.pallas import tpu as pltpu
from jax.sharding import PartitionSpec as P

F32 = jnp.float32
BF16 = jnp.bfloat16
PAIR = ("section", "dp")
TILE = 512
HALF_ROOT = 0.7071067811865476
DENSITY = 0.3989422804014327
BLOCKS = 16
ORDERS = ((0, 1, 2, 3), (2, 0, 1, 3))
ANY = pl.BlockSpec(memory_space=pltpu.HBM)
VMEM = pl.BlockSpec(memory_space=pltpu.VMEM)
SMEM = pl.BlockSpec(memory_space=pltpu.SMEM)

TAPS, CONV, UPB, DOWNB, GAIN, SCALE, SHIFT, SMALL = 0, 7, 8, 11, 12, 16, 20, 24


def position(block, order):
    place = 0
    for bit in order:
        place = 2 * place + ((block >> bit) & 1)
    return place


def dot(a, b, dims):
    return lax.dot_general(a, b, (dims, ((), ())), preferred_element_type=F32)


NN = ((1,), (0,))
NT = ((1,), (1,))
TN = ((0,), (0,))


def shifted(x, offset):
    if offset == 0:
        return x
    frames = x.shape[0]
    rows = lax.broadcasted_iota(jnp.int32, (frames, 1), 0)
    rolled = pltpu.roll(x, (-offset) % frames, 0)
    kept = rows < frames - offset if offset > 0 else rows >= -offset
    return jnp.where(kept, rolled, 0.0)


def wide(x, width):
    return jnp.concatenate([x] * (width // 128), axis=1)


def rowsum(x):
    return jnp.sum(x, axis=0, keepdims=True)


def normalize(x, small, clip):
    conv = small[CONV : CONV + 1] + x * small[3:4]
    for k in range(7):
        if k != 3:
            conv = conv + shifted(x, k - 3) * small[k : k + 1]
    centred = conv - jnp.mean(conv, axis=-1, keepdims=True)
    inv = lax.rsqrt(jnp.mean(centred * centred, axis=-1, keepdims=True) + 1e-06)
    normed = centred * inv
    scale = small[pl.ds(SCALE + clip, 1)]
    shift = small[pl.ds(SHIFT + clip, 1)]
    adapted = (normed * scale + shift).astype(BF16)
    return adapted, normed.astype(BF16), jnp.broadcast_to(inv, (x.shape[0], 128))


def prep_body(sec, speaker, taps, conv, upb, downb, gain, scale_hbm, shift_hbm, own, other, sems):
    width = own.shape[1]
    half = SMALL - SHIFT
    copies = []
    for side, out in enumerate((own, other)):
        first = (sec[0] if side == 0 else 1 - sec[0]) * half
        for clip in range(half):
            row = speaker[first + clip]
            for kind, table in enumerate((scale_hbm, shift_hbm)):
                copies.append(
                    pltpu.make_async_copy(
                        table.at[0, pl.ds(row, 1)],
                        out.at[pl.ds((SCALE, SHIFT)[kind] + clip, 1)],
                        sems.at[side, kind, clip],
                    )
                )
    for copy in copies:
        copy.start()
    for out in (own, other):
        for k in range(7):
            out[TAPS + k : TAPS + k + 1] = taps[k]
        out[CONV : CONV + 1] = conv[...]
        for k in range(DOWNB - UPB):
            out[UPB + k : UPB + k + 1] = upb[:, k * width : (k + 1) * width]
        out[DOWNB : DOWNB + 1] = downb[...]
        out[GAIN : GAIN + 1] = gain[...]
        out[GAIN + 1 : SCALE] = jnp.zeros((SCALE - GAIN - 1, width), F32)
    for copy in copies:
        copy.wait()


def first_norm_body(sec, tokens, small, adapted, normed, inv):
    clip = pl.program_id(0)
    a, n, r = normalize(tokens[0].astype(F32), small, clip)
    adapted[...] = a
    normed[...] = n
    inv[...] = r


def forward_tiles(adapted, up, down, small, act, slope, acc):
    clips = acc.shape[0] // 256
    for j in range(3):
        bias = small[UPB + j : UPB + j + 1]
        for r in range(clips):
            rows = slice(r * 256, (r + 1) * 256)
            pre = dot(adapted[rows], up[:, j * TILE : (j + 1) * TILE], NN) + bias
            phi = 0.5 * lax.erf(pre * HALF_ROOT) + 0.5
            low = (pre * phi).astype(BF16)
            act[j, rows] = low
            slope[j, rows] = (phi + pre * (DENSITY * jnp.exp(-0.5 * pre * pre))).astype(BF16)
            part = dot(low, down[j * TILE : (j + 1) * TILE], NN)
            if j == 0:
                acc[rows] = part
            else:
                acc[rows] = acc[rows] + part


def activation_tile(j, gb, down, slope, sums):
    total = jnp.zeros((1, TILE), F32)
    for r in range(gb.shape[0] // 256):
        rows = slice(r * 256, (r + 1) * 256)
        gact = dot(gb[rows], down[j * TILE : (j + 1) * TILE], NT)
        gpre = (gact * slope[j, rows].astype(F32)).astype(BF16)
        slope[j, rows] = gpre
        total = total + rowsum(gpre.astype(F32))
    sums[UPB + j : UPB + j + 1] = total


def weight_tile(j, gb, adapted, act, gpre, upd, dnd):
    gup = dot(adapted[...], gpre, TN).astype(BF16)
    share = TILE // BLOCKS
    for i in range(BLOCKS):
        upd[position(i, ORDERS[0]), j * share : (j + 1) * share] = gup[i * share : (i + 1) * share]
    gdn = dot(act, gb[...], TN).astype(BF16)
    share = 3 * TILE // BLOCKS
    at = j * TILE
    while at < (j + 1) * TILE:
        stop = min((at // share + 1) * share, (j + 1) * TILE)
        first = at % share
        dnd[position(at // share, ORDERS[1]), first : first + stop - at] = gdn[
            at - j * TILE : stop - j * TILE
        ]
        at = stop


def norm_backward(gad, normed, inv, small, clip, grad_out, v):
    n = normed.astype(F32)
    width = n.shape[1]
    scale = small[pl.ds(SCALE + clip, 1)]
    g_shift = rowsum(gad)
    g_scale = rowsum(gad * n)
    gn = gad * scale
    m1 = jnp.mean(gn, axis=-1, keepdims=True)
    m2 = jnp.mean(gn * n, axis=-1, keepdims=True)
    gc = (gn - m1 - n * m2) * wide(inv, width)
    g_conv = rowsum(gc)
    total = grad_out
    g_taps = []
    for k in range(7):
        moved = shifted(gc, 3 - k)
        total = total + moved * small[k : k + 1]
        g_taps.append(rowsum(moved * v))
    return total.astype(BF16), jnp.concatenate(g_taps + [g_conv], axis=0), g_scale, g_shift


def place_weights(sec, block, up_own, up_got, down_own, down_got, up, down, sems, start):
    def go(up_from, down_from):
        for source, target, sem in ((up_from, up, sems.at[0]), (down_from, down, sems.at[1])):
            copy = pltpu.make_async_copy(source, target, sem)
            copy.start() if start else copy.wait()

    if not start:
        go(up_own, down_own)
        return

    @pl.when(sec[0] == block)
    def _():
        go(up_own, down_own)

    @pl.when(sec[0] != block)
    def _():
        go(up_got, down_got)


def route(sec, upd, dnd, keep, send, sems, start):
    def go(kept, sent):
        for source, target, sem in ((kept, keep, sems.at[0]), (sent, send, sems.at[1])):
            copy = pltpu.make_async_copy(source, target, sem)
            copy.start() if start else copy.wait()

    if not start:
        go(upd, dnd)
        return

    @pl.when(sec[0] == 0)
    def _():
        go(upd, dnd)

    @pl.when(sec[0] != 0)
    def _():
        go(dnd, upd)


def main_body(
    sec, valid, adapted0, tokens, cot, small0, small1, up_own, up_got, down_own, down_got,
    gin1, gb0, sums0, sums1, out_own, out_send, act_hbm, gpre_hbm, keep, send,
    up0, down0, up1, down1, act0, slope0, act1, slope1, acc, adapted1, normed1, inv1, branch0, gb1,
    out0, out1, upd, dnd, sems,
):
    clips = acc.shape[0] // 256
    weights = (up_own, up_got, down_own, down_got)
    place_weights(sec, 0, *weights, up0, down0, sems.at[0], True)
    place_weights(sec, 1, *weights, up1, down1, sems.at[1], True)
    place_weights(sec, 0, *weights, up0, down0, sems.at[0], False)
    forward_tiles(adapted0, up0, down0, small0, act0, slope0, acc)
    save_act = pltpu.make_async_copy(act0, act_hbm, sems.at[2, 0])
    save_act.start()

    def between(r):
        rows = pl.ds(pl.multiple_of(r * 256, 256), 256)
        branch = acc[rows] + small0[DOWNB : DOWNB + 1]
        branch0[rows] = branch
        result = (tokens[r].astype(F32) + small0[GAIN : GAIN + 1] * branch).astype(BF16)
        out0[r] = result
        a, n, i = normalize(result.astype(F32), small1, r)
        adapted1[rows] = a
        normed1[rows] = n
        inv1[rows] = i

    pl.loop(0, clips)(between)
    place_weights(sec, 1, *weights, up1, down1, sems.at[1], False)
    forward_tiles(adapted1, up1, down1, small1, act1, slope1, acc)
    sums0[...] = jnp.zeros_like(sums0)
    sums1[...] = jnp.zeros_like(sums1)

    def top(r):
        rows = pl.ds(pl.multiple_of(r * 256, 256), 256)
        branch = acc[rows] + small1[DOWNB : DOWNB + 1]
        gain = small1[GAIN : GAIN + 1]
        out1[r] = (out0[r].astype(F32) + gain * branch).astype(BF16)
        grad = cot[r].astype(F32) * valid[sec[0] * clips + r].astype(F32)
        low = (grad * gain).astype(BF16)
        gb1[rows] = low
        sums1[GAIN : GAIN + 1] += rowsum(grad * branch)
        sums1[DOWNB : DOWNB + 1] += rowsum(low.astype(F32))

    pl.loop(0, clips)(top)
    half_own = out_own.at[pl.ds(sec[0] * clips, clips)]
    route(sec, out0, out1, half_own, out_send, sems.at[4], True)
    for j in range(3):
        activation_tile(j, gb1, down1, slope1, sums1)
        for r in range(clips):
            rows = slice(r * 256, (r + 1) * 256)
            part = dot(slope1[j, rows], up1[:, j * TILE : (j + 1) * TILE], NT)
            acc[rows] = part if j == 0 else acc[rows] + part
        weight_tile(j, gb1, adapted1, act1[j], slope1[j], upd, dnd)
    route(sec, upd, dnd, keep, send, sems.at[3], True)

    def under(r):
        rows = pl.ds(pl.multiple_of(r * 256, 256), 256)
        grad = cot[r].astype(F32) * valid[sec[0] * clips + r].astype(F32)
        gin, smalls, g_scale, g_shift = norm_backward(
            acc[rows], normed1[rows], inv1[rows], small1, r, grad, out0[r].astype(F32)
        )
        gin1[r] = gin
        sums1[TAPS : TAPS + 8] += smalls
        sums1[pl.ds(SCALE + r, 1)] = g_scale
        sums1[pl.ds(SHIFT + r, 1)] = g_shift
        grad0 = gin.astype(F32)
        low = (grad0 * small0[GAIN : GAIN + 1]).astype(BF16)
        gb0[rows] = low
        sums0[GAIN : GAIN + 1] += rowsum(grad0 * branch0[rows])
        sums0[DOWNB : DOWNB + 1] += rowsum(low.astype(F32))

    pl.loop(0, clips)(under)
    saves = []
    for j in range(3):
        activation_tile(j, gb0, down0, slope0, sums0)
        saves.append(pltpu.make_async_copy(slope0.at[j], gpre_hbm.at[j], sems.at[5 + j // 2, j % 2]))
        saves[-1].start()
    save_act.wait()
    route(sec, out0, out1, half_own, out_send, sems.at[4], False)
    route(sec, upd, dnd, keep, send, sems.at[3], False)
    for copy in saves:
        copy.wait()


def weights_body(sec, gb, adapted, act, gpre, keep, send, upd, dnd, sems):
    step = pl.program_id(0)
    for j in range(3):

        @pl.when(step == j)
        def _():
            weight_tile(j, gb, adapted, act[0], gpre[0], upd, dnd)

    @pl.when(step == 2)
    def _():
        route(sec, upd, dnd, keep, send, sems, True)
        route(sec, upd, dnd, keep, send, sems, False)


def last_body(
    first, sec, gpre, up_own, up_got, normed, inv, small, grad_out, tokens, sums_in, *rest
):
    gin, away, sums, up, sem = rest[-5:]
    step = pl.program_id(0)
    clip = first + step

    @pl.when(step == 0)
    def _():
        sums[...] = sums_in[...]

        @pl.when(sec[0] == 0)
        def _():
            pltpu.make_async_copy(up_own, up, sem).start()

        @pl.when(sec[0] != 0)
        def _():
            pltpu.make_async_copy(up_got, up, sem).start()

        pltpu.make_async_copy(up_own, up, sem).wait()

    gad = dot(gpre[0], up[:, :TILE], NT)
    for j in range(1, 3):
        gad = gad + dot(gpre[j], up[:, j * TILE : (j + 1) * TILE], NT)
    above = grad_out[0]
    out, smalls, g_scale, g_shift = norm_backward(
        gad, normed[...], inv[...], small, clip, above.astype(F32), tokens[0].astype(F32)
    )
    gin[0] = jnp.where(sec[0] == 0, out, above)
    away[0] = jnp.where(sec[0] == 0, above, out)
    sums[TAPS : TAPS + 8] += smalls
    sums[pl.ds(SCALE + clip, 1)] = g_scale
    sums[pl.ds(SHIFT + clip, 1)] = g_shift


def pick(first, a, b):
    return jnp.where(first, a, b)


def bit_of(spot, step):
    low, high = ORDERS[0][step], ORDERS[1][step]
    return (spot[1] >> (low if low == high else pick(spot[0] == 0, low, high))) & 1


def region(spot, level, step):
    start = 0
    for i in range(level, min(step, 4)):
        start = start + bit_of(spot, i) * (8 >> i)
    if step < 4:
        start = start + (1 - bit_of(spot, step)) * (8 >> step)
    return start


GATHER = (1, 2, 3, 0)


def gather_slot(spot):
    slot = 0
    for i, step in enumerate(GATHER):
        slot = slot + bit_of(spot, step) * (1 << i)
    return slot


def fetch(copies, source, first, rows, target, sem):
    copies.append(pltpu.make_async_copy(source.at[pl.ds(first, rows)], target, sem))
    copies[-1].start()


def add_up(buffers, rows):
    total = buffers[0][:rows].astype(F32)
    for buffer in buffers[1:]:
        total = total + buffer[:rows].astype(F32)
    return total


def pack_body(step, blocks, bases, share, extras, spot, speaker, *refs):
    levels = step + 2
    sources = [refs[b * levels : (b + 1) * levels] for b in range(blocks)]
    refs = refs[blocks * levels :]
    count = 1 if step == 4 else 8 >> step
    rows = count * share
    extra_in, refs = refs[: 3 * extras], refs[3 * extras :]
    packet, refs = (refs[0], refs[1:]) if step < 4 or extras else (None, refs)
    if extras:
        smalls_out, refs = refs[0], refs[1:]
    if step == 4:
        mine, away, refs = refs[0], refs[1], refs[2:]
    buffers, tail, sems = refs
    copies = []
    for b in range(blocks):
        for n in range(levels):
            level = max(n - 1, 0)
            base = bases[b][level]
            first = pl.multiple_of((region(spot, level, step)) * share + base, 32)
            fetch(copies, sources[b][n], first, rows, buffers.at[b, n], sems.at[b, n])
    head = blocks * rows if step < 4 else 0
    if extras and step == 1:
        sums0, sums1, got = extra_in
        own = pick(spot[0] == 0, sums0[...], sums1[...])
        other = got[...]
        low = pick(spot[0] == 0, own[SCALE:], other[SCALE:])
        high = pick(spot[0] == 0, other[SCALE:], own[SCALE:])
        packet[head : head + 16] = jnp.concatenate([low, high], axis=0).astype(BF16)
        width = own.shape[1]
        lane = lax.broadcasted_iota(jnp.int32, (1, width), 1)
        mine_lane = (lane >> 4) == gather_slot(spot)
        which = ((lane >> 3) & 1) * 4 + (lane & 3)
        code = jnp.zeros((1, width), jnp.int32)
        for c in range(8):
            code = jnp.where(mine_lane & (which == c), speaker[c], code)
        smalls_out[...] = own[:SCALE] + other[:SCALE]
        smalls_out[13:14] = (code >> 6).astype(F32)
        smalls_out[14:15] = (code & 63).astype(F32)
        packet[head + 16 : head + 32] = smalls_out[...].astype(BF16)
    elif extras:
        before, after, smalls_in = extra_in
        size = 16 << (step - 2)
        old_head = blocks * (8 >> (step - 1)) * share
        bit = bit_of(spot, GATHER[step - 2])
        for n, (source, spot_bit) in enumerate(((before, bit), (after, 1 - bit))):
            target = packet.at[pl.ds(pl.multiple_of(head + spot_bit * size, 16), size)]
            fetch(copies, source, old_head, size, target, sems.at[2, n])
        fetch(copies, after, old_head + size, 16, tail, sems.at[2, 2])
    for b in range(blocks):
        for n in range(levels):
            copies[b * levels + n].wait()
        total = add_up([buffers.at[b, n] for n in range(levels)], rows)
        if step < 4:
            packet[b * rows : (b + 1) * rows] = total.astype(BF16)
        else:
            @pl.when(spot[0] == b)
            def _():
                mine[...] = total

            @pl.when(spot[0] != b)
            def _():
                away[...] = total
    if extras and step > 1:
        for copy in copies[blocks * levels :]:
            copy.wait()
        smalls_out[...] = smalls_in[...] + tail[...].astype(F32)
        packet[head + 2 * size : head + 2 * size + 16] = smalls_out[...].astype(BF16)


def finish_body(
    spot, before, after, smalls_in, mine, got, scale, shift, up, down, smalls, rows_of, tail, sems
):
    size = rows_of.shape[0] // 2
    bit = bit_of(spot, GATHER[3])
    copies = []
    for n, (source, spot_bit) in enumerate(((before, bit), (after, 1 - bit))):
        target = rows_of.at[pl.ds(pl.multiple_of(spot_bit * size, 16), size)]
        fetch(copies, source, 0, size, target, sems.at[n])
    fetch(copies, after, size, 16, tail, sems.at[2])
    first = spot[0] == 0
    one, two = mine[...], got[...]
    up_rows = up.shape[0]
    ups = pick(first, one, two)
    for j in range(3):
        up[:, j * TILE : (j + 1) * TILE] = ups[j * up_rows : (j + 1) * up_rows]
    down[...] = pick(first, two, one)
    for copy in copies:
        copy.wait()
    total = smalls_in[...] + tail[...].astype(F32)
    smalls[...] = total
    owned = scale.shape[0]
    count = 2 * size
    who = total[13:14, :count] * 64.0 + total[14:15, :count]
    wanted = lax.broadcasted_iota(jnp.int32, (owned, count), 0) + spot[1] * owned
    hit = who == wanted.astype(F32)
    kind = (lax.broadcasted_iota(jnp.int32, (owned, count), 1) >> 2) & 1
    for k, out in enumerate((scale, shift)):
        out[...] = dot(jnp.where(hit & (kind == k), 1.0, 0.0).astype(BF16), rows_of[...], NN)


def struct(shape, dtype):
    return jax.ShapeDtypeStruct(shape, dtype)


def params(limit=60):
    return pltpu.CompilerParams(vmem_limit_bytes=limit * 1024 * 1024)


def local(
    tokens, out_cotangent, speaker, valid, conv_weight, conv_bias, scale_table, shift_table,
    up_weight, up_bias, down_weight, down_bias, layer_scale,
):
    section = lax.axis_index("section").astype(jnp.int32)
    place = lax.axis_index("dp").astype(jnp.int32)
    devices = lax.axis_size("dp")
    first_section = section == 0
    clips, frames, width = tokens.shape
    hidden = up_weight.shape[2]
    table_rows = scale_table.shape[1]
    half = clips // 2
    rows = half * frames
    sec = section[None]
    spot = jnp.stack([section, place])
    swap = [(0, 1), (1, 0)]

    own_small, other_small = pl.pallas_call(
        prep_body,
        out_shape=[struct((SMALL, width), F32)] * 2,
        in_specs=[SMEM, SMEM] + [VMEM] * 5 + [ANY] * 2,
        out_specs=[VMEM] * 2,
        scratch_shapes=[pltpu.SemaphoreType.DMA((2, 2, half))],
        name="prep",
    )(
        sec, speaker, conv_weight.transpose(1, 0, 2), conv_bias, up_bias, down_bias, layer_scale,
        scale_table, shift_table,
    )
    got_small = lax.ppermute(other_small, "section", swap)
    up_own, down_own = up_weight[0], down_weight[0]
    up_got = lax.ppermute(up_own, "section", swap)
    down_got = lax.ppermute(down_own, "section", swap)
    small0 = jnp.where(first_section, own_small, got_small)
    small1 = jnp.where(first_section, got_small, own_small)

    clip_block = (1, frames, width)
    mine = pl.BlockSpec(clip_block, lambda c, sec: (sec[0] * half + c, 0, 0))
    whole_small = pl.BlockSpec((SMALL, width), lambda c, sec: (0, 0))
    flat = pl.BlockSpec((frames, width), lambda c, sec: (c, 0))
    flat_inv = pl.BlockSpec((frames, 128), lambda c, sec: (c, 0))
    adapted0, normed0, inv0 = pl.pallas_call(
        first_norm_body,
        grid_spec=pltpu.PrefetchScalarGridSpec(
            num_scalar_prefetch=1,
            grid=(half,),
            in_specs=[mine, whole_small],
            out_specs=[flat, flat, flat_inv],
        ),
        out_shape=[
            struct((rows, width), BF16), struct((rows, width), BF16), struct((rows, 128), F32)
        ],
        name="first_norm",
    )(sec, tokens, small0)

    half_struct = struct((half, frames, width), BF16)
    whole_struct = struct((clips, frames, width), BF16)
    small_struct = struct((SMALL, width), F32)
    tiles = hidden // TILE
    tiled = (tiles, rows, TILE)
    share = hidden // BLOCKS
    gradient = (BLOCKS, share, width)
    gradient_struct = struct(gradient, BF16)
    half_spec = pl.BlockSpec((half, frames, width), lambda i, sec, valid: (sec[0], 0, 0))

    def full(*shape):
        return pl.BlockSpec(shape, lambda i, *_: (0,) * len(shape))

    gin1, gb0, sums0, sums1, out_own, out_send, act0, gpre0, keep1, send1 = pl.pallas_call(
        main_body,
        grid_spec=pltpu.PrefetchScalarGridSpec(
            num_scalar_prefetch=2,
            grid=(1,),
            in_specs=[full(rows, width), half_spec, half_spec, full(SMALL, width), full(SMALL, width)]
            + [ANY] * 4,
            out_specs=[full(half, frames, width), full(rows, width)]
            + [full(SMALL, width)] * 2
            + [ANY] * 6,
            scratch_shapes=[
                pltpu.VMEM((width, hidden), BF16),
                pltpu.VMEM((hidden, width), BF16),
                pltpu.VMEM((width, hidden), BF16),
                pltpu.VMEM((hidden, width), BF16),
                pltpu.VMEM(tiled, BF16),
                pltpu.VMEM(tiled, BF16),
                pltpu.VMEM(tiled, BF16),
                pltpu.VMEM(tiled, BF16),
                pltpu.VMEM((rows, width), F32),
                pltpu.VMEM((rows, width), BF16),
                pltpu.VMEM((rows, width), BF16),
                pltpu.VMEM((rows, 128), F32),
                pltpu.VMEM((rows, width), F32),
                pltpu.VMEM((rows, width), BF16),
                pltpu.VMEM((half, frames, width), BF16),
                pltpu.VMEM((half, frames, width), BF16),
                pltpu.VMEM(gradient, BF16),
                pltpu.VMEM(gradient, BF16),
                pltpu.SemaphoreType.DMA((7, 2)),
            ],
        ),
        out_shape=[
            half_struct, struct((rows, width), BF16), small_struct, small_struct,
            whole_struct, half_struct, struct(tiled, BF16), struct(tiled, BF16),
            gradient_struct, gradient_struct,
        ],
        compiler_params=params(),
        name="main",
    )(
        sec, valid, adapted0, tokens, out_cotangent, small0, small1, up_own, up_got, down_own, down_got
    )
    got1 = lax.ppermute(send1, "section", swap)
    got_out = lax.ppermute(out_send, "section", swap)

    tile_spec = pl.BlockSpec((1, rows, TILE), lambda j, *_: (j, 0, 0))
    keep0, send0 = pl.pallas_call(
        weights_body,
        grid_spec=pltpu.PrefetchScalarGridSpec(
            num_scalar_prefetch=1,
            grid=(tiles,),
            in_specs=[full(rows, width), full(rows, width), tile_spec, tile_spec],
            out_specs=[ANY, ANY],
            scratch_shapes=[
                pltpu.VMEM(gradient, BF16),
                pltpu.VMEM(gradient, BF16),
                pltpu.SemaphoreType.DMA((2,)),
            ],
        ),
        out_shape=[gradient_struct, gradient_struct],
        compiler_params=params(),
        name="weights",
    )(sec, gb0, adapted0, act0, gpre0)
    got0 = lax.ppermute(send0, "section", swap)

    def last(first, count, sums, *others):
        def at(c):
            return first + c

        return pl.pallas_call(
            functools.partial(last_body, first),
            grid_spec=pltpu.PrefetchScalarGridSpec(
                num_scalar_prefetch=1,
                grid=(count,),
                in_specs=[
                    pl.BlockSpec((tiles, frames, TILE), lambda c, sec: (0, at(c), 0)),
                    ANY,
                    ANY,
                    pl.BlockSpec((frames, width), lambda c, sec: (at(c), 0)),
                    pl.BlockSpec((frames, 128), lambda c, sec: (at(c), 0)),
                    whole_small,
                    pl.BlockSpec(clip_block, lambda c, sec: (at(c), 0, 0)),
                    pl.BlockSpec(clip_block, lambda c, sec: (sec[0] * half + at(c), 0, 0)),
                    whole_small,
                ]
                + [ANY] * len(others),
                out_specs=[
                    pl.BlockSpec(clip_block, lambda c, sec: (sec[0] * half + at(c), 0, 0)),
                    pl.BlockSpec(clip_block, lambda c, sec: (at(c), 0, 0)),
                    whole_small,
                ],
                scratch_shapes=[pltpu.VMEM((width, hidden), BF16), pltpu.SemaphoreType.DMA],
            ),
            out_shape=[whole_struct, half_struct, small_struct],
            input_output_aliases={10 + i: i for i in range(len(others))},
            compiler_params=params(),
            name="last",
        )(sec, gpre0, up_own, up_got, normed0, inv0, small0, gin1, tokens, sums, *others)

    gin_own, gin_send, sums0 = last(0, half, sums0)
    got_gin = lax.ppermute(gin_send, "section", swap)
    got_sums = lax.ppermute(pick(first_section, sums1, sums0), "section", swap)

    def joined(whole, got):
        return lax.dynamic_update_slice(whole, got, ((1 - section) * half, 0, 0))[None]

    block_outputs = joined(out_own, got_out)
    input_grads = joined(gin_own, got_gin)
    pairs = [[keep0, got0], [keep1, got1]]
    if devices == BLOCKS:
        outs = halved(spot, speaker, pairs, sums0, sums1, got_sums, table_rows)
    else:
        outs = scattered(section, place, devices, speaker, pairs, sums0, sums1, got_sums, table_rows)
    up_share, down_share, table_scale, table_shift, smalls = outs
    lanes = width // devices
    own_lanes = lax.dynamic_slice_in_dim(smalls, place * lanes, lanes, 1)
    up_bias_share = lax.dynamic_slice_in_dim(
        smalls[UPB : UPB + 3].reshape(-1), place * (hidden // devices), hidden // devices, 0
    )
    return (
        block_outputs,
        input_grads,
        own_lanes[TAPS : TAPS + 7][None],
        own_lanes[CONV : CONV + 1],
        table_scale[None],
        table_shift[None],
        up_share[None],
        up_bias_share[None],
        down_share[None],
        own_lanes[DOWNB : DOWNB + 1],
        own_lanes[GAIN : GAIN + 1],
    )


def exchanged(packet, step):
    devices = lax.axis_size("dp")
    moves = [
        (s * devices + i, s * devices + (i ^ (1 << ORDERS[s][step])))
        for s in range(2)
        for i in range(devices)
    ]
    return lax.ppermute(packet, PAIR, moves)


def halved(spot, speaker, pairs, sums0, sums1, got_sums, table_rows):
    _, share, width = pairs[0][0].shape
    pairs = [[piece.reshape(-1, width) for piece in pair] for pair in pairs]

    def pack(step, block_sources, bases, extra_in, name):
        blocks = len(block_sources)
        levels = step + 2
        count = 1 if step == 4 else 8 >> step
        rows = count * share
        extras = len(extra_in) > 0
        outs, specs = [], []
        size = (8 << step) if extras else 0
        length = (blocks * rows if step < 4 else 0) + (size + 16 if extras else 0)
        outs.append(struct((length, width), BF16))
        if extras:
            outs.append(struct((SCALE, width), F32))
        if step == 4:
            outs += [struct((share, width), F32)] * 2
        if extras and step == 1:
            extra_specs = [VMEM] * 3
        elif extras:
            extra_specs = [ANY, ANY, VMEM]
        else:
            extra_specs = []
        return pl.pallas_call(
            functools.partial(pack_body, step, blocks, bases, share, int(extras)),
            out_shape=outs,
            in_specs=[SMEM, SMEM] + [ANY] * (blocks * levels) + extra_specs,
            out_specs=[VMEM] * len(outs),
            scratch_shapes=[
                pltpu.VMEM((blocks, levels, rows, width), BF16),
                pltpu.VMEM((16, width), BF16),
                pltpu.SemaphoreType.DMA((3, max(levels, 3))),
            ],
            compiler_params=params(),
            name=name,
        )(spot, speaker, *[x for sources in block_sources for x in sources], *extra_in)

    for b in (1, 0):
        (packet,) = pack(0, [pairs[b]], [[0]], [], f"pack0_{b}")
        pairs[b].append(exchanged(packet, 0))
    bases = [[0, 0], [0, 0]]
    extra_in = [sums0, sums1, got_sums]
    for step in range(1, 4):
        packet, smalls = pack(step, pairs, bases, extra_in, f"pack{step}")
        got = exchanged(packet, step)
        rows = (8 >> step) * share
        for b in range(2):
            pairs[b].append(got)
            bases[b].append(b * rows)
        bases = [list(x) for x in bases]
        extra_in = [packet, got, smalls]
    packet, smalls, mine, away = pack(4, pairs, bases, extra_in, "pack4")
    got = exchanged(packet, 0)
    got_share = lax.ppermute(away, "section", [(0, 1), (1, 0)])
    owned = table_rows // BLOCKS
    up_rows = width // BLOCKS
    scale, shift, up, down, smalls = pl.pallas_call(
        finish_body,
        out_shape=[
            struct((owned, width), F32),
            struct((owned, width), F32),
            struct((up_rows, 3 * TILE), F32),
            struct((share, width), F32),
            struct((SCALE, width), F32),
        ],
        in_specs=[SMEM, ANY, ANY, VMEM, VMEM, VMEM],
        out_specs=[VMEM] * 5,
        scratch_shapes=[
            pltpu.VMEM((16 * BLOCKS, width), BF16),
            pltpu.VMEM((16, width), BF16),
            pltpu.SemaphoreType.DMA((3,)),
        ],
        name="finish",
    )(spot, packet, got, smalls, mine, got_share)
    return up, down, scale, shift, smalls


def scattered(section, place, devices, speaker, pairs, sums0, sums1, got_sums, table_rows):
    first_section = section == 0
    own_sums = pick(first_section, sums0, sums1)
    smalls = lax.psum(own_sums[:SCALE] + got_sums[:SCALE], "dp")
    clip_rows = jnp.stack([own_sums[SCALE:], got_sums[SCALE:]])
    clip_rows = pick(first_section, clip_rows, clip_rows[::-1]).astype(BF16)
    clips = speaker.shape[0]
    width = clip_rows.shape[-1]
    clip_rows = clip_rows.reshape(2, 2, clips // 2, width).transpose(1, 0, 2, 3).reshape(2, clips, width)
    gathered = lax.all_gather(clip_rows, "dp", axis=1, tiled=True)
    who = lax.all_gather(speaker, "dp", tiled=True)
    owned = table_rows // devices
    wanted = place * owned + jnp.arange(owned, dtype=jnp.int32)
    chosen = (who[None, :] == wanted[:, None]).astype(BF16)
    tables = [jnp.dot(chosen, gathered[k], preferred_element_type=F32) for k in range(2)]
    natural = []
    for order in ORDERS:
        natural.append(
            jnp.stack(
                [
                    jnp.stack([pair[0][position(i, order)].astype(F32) + pair[1][position(i, order)].astype(F32) for i in range(BLOCKS)])
                    for pair in pairs
                ]
            )
        )
    blocks, _, rows, width = natural[0].shape
    tiles = rows * BLOCKS // TILE
    up = natural[0].reshape(blocks, BLOCKS, tiles, rows // tiles, TILE).transpose(0, 1, 3, 2, 4)
    flat = pick(
        first_section, up.reshape(blocks, devices, -1), natural[1].reshape(blocks, devices, -1)
    )
    share = lax.psum_scatter(flat, "dp", scatter_dimension=1, tiled=True)[:, 0]
    own_share = lax.dynamic_index_in_dim(share, section, 0, keepdims=False)
    got_share = lax.ppermute(
        lax.dynamic_index_in_dim(share, 1 - section, 0, keepdims=False), "section", [(0, 1), (1, 0)]
    )
    up_share = pick(first_section, own_share, got_share).reshape(width // devices, -1)
    down_share = pick(first_section, got_share, own_share).reshape(-1, width)
    return up_share, down_share, tables[0], tables[1], smalls


def solution(mesh):
    placed = (
        P("dp", None, None),
        P("dp", None, None),
        P("dp"),
        P("dp"),
        P("section", None, None),
        P("section", None),
        P("section", None, None),
        P("section", None, None),
        P("section", None, None),
        P("section", None),
        P("section", None, None),
        P("section", None),
        P("section", None),
    )
    return jax.shard_map(
        local,
        mesh=mesh,
        in_specs=placed,
        out_specs=(
            P("section", "dp", None, None),
            P("section", "dp", None, None),
            P("section", None, "dp"),
            P("section", "dp"),
            P("section", "dp", None),
            P("section", "dp", None),
            P("section", "dp", None),
            P("section", "dp"),
            P("section", "dp", None),
            P("section", "dp"),
            P("section", "dp"),
        ),
        check_vma=False,
    )
```

time: 880 us -> 158 us (0.18); the launches traced: 870 us -> 157 us
  waiting for transfers between devices: 450 us -> 37.7 us
  matrix products: 184 us -> 0 us
  Pallas kernels: 0 us -> 88.3 us
  other arithmetic: 83.7 us -> 2.05 us
  blocking collectives: 78.4 us -> 0 us
  local copies, waits for them, and re-layouts: 42.9 us -> 12.9 us
  between operations: 17.1 us -> 0.82 us
    reduce_scatter x4 -> x0, waiting for transfers between devices: 447 us -> none  [the longest x1 137 us: local(): lax.psum_scatter(sum_down, 'dp', scatter_dimension=0, tiled=True)]
    dot_general x34 -> x0, matrix products: 184 us -> none  [the longest x5 47.1 us: local(): jnp.einsum('th,td->hd', activated_low, grad_branch, preferred_element_typ...]
    pallas_call x0 -> x12, Pallas kernels: none -> 88.3 us  [the longest x1 39.5 us: local(): pl.pallas_call(main_body, grid_spec=pltpu.PrefetchScalarGridSpec(num_scal...]
    unnamed x1 -> x0, blocking collectives: 78.4 us -> none
    reduce_sum x31 -> x0, other arithmetic: 40.9 us -> none  [the longest x10 17.7 us: prepare(): centred = conv - jnp.mean(conv, axis=-1, keepdims=True)]
    ppermute x8 -> x15, waiting for transfers between devices: 2.29 us -> 37.7 us  [the longest x6 31.7 us: exchanged(): return lax.ppermute(packet, PAIR, moves)]
    dynamic_update_slice x19 -> x0, other arithmetic: 33.4 us -> none  [the longest x5 14.4 us: local(): lax.dynamic_update_slice_in_dim(grad_in_all, jnp.where(active, grad_total...]
    dynamic_slice x10 -> x0, local copies, waits for them, and re-layouts: 19.8 us -> none  [the longest x4 8.39 us: local(): old_pre = lax.dynamic_index_in_dim(saved_pre, place, 0, keepdims=False)]
  transfers between devices with their start and end apart: 13 -> 15, of which waited for: 5 -> 8; matrix products, arithmetic and copies ran while one was open for 12% -> 3% of each run, Pallas kernels for 0% -> 22%
where the time goes in v1:
time: 158 us; the launch traced here: 157 us
  Pallas kernels  88.3 us (56%)
  waiting for transfers between devices  37.7 us (24%)
  starting transfers between devices  15.4 us (10%)
  local copies, waits for them, and re-layouts  12.9 us (8%)
  other arithmetic  2.05 us (1%)
    pallas_call x1, Pallas kernels, local(): pl.pallas_call(main_body, grid_spec=pltpu.PrefetchScalarGridSpec(num_scal...  39.5 us
    ppermute x6, waiting for transfers between devices, exchanged(): return lax.ppermute(packet, PAIR, moves)  31.7 us
    pallas_call x6, Pallas kernels, pack(): pl.pallas_call(functools.partial(pack_body, step, blocks, bases, share, i...  19.4 us
    ppermute x6, starting transfers between devices, exchanged(): return lax.ppermute(packet, PAIR, moves)  11.7 us
    pallas_call x1, Pallas kernels, last(): pl.pallas_call(functools.partial(last_body, first), grid_spec=pltpu.Prefe...  10.7 us
    pallas_call x1, Pallas kernels, local(): pl.pallas_call(weights_body, grid_spec=pltpu.PrefetchScalarGridSpec(num_s...  7.81 us
    unnamed x27, local copies, waits for them, and re-layouts  7.37 us
    pallas_call x1, Pallas kernels, local(): pl.pallas_call(first_norm_body, grid_spec=pltpu.PrefetchScalarGridSpec(nu...  5.28 us
  transfers between devices with their start and end apart: 15, of which 8 were waited for; matrix products, arithmetic and copies ran while one was open for 3% of the time, Pallas kernels for 22%

profile of v1, /device:TPU:0, one launch (start us, length us, event | category | flops | bytes accessed | tf_op | source)
XLA Modules:
  0.0 157.2 jit_solution(16748832471779209815)
XLA Ops:
  0.6 0.6 collective-permute-start.1
  1.3 2.4 %prep.1 = (f32[24,512]{1,0:T(8,128)}, f32[24,512]{1,0:T(8,128)}) custom-call(s32[1]{0:T(128)} %bitcast.sec, s32[8]{0:T(128)} %speaker.13, f32[7,1,512]{2,1,0:T(1,128)} %bitcast.43, f32[1,512]{1,0:T(1,128)} %conv.1, f32[1,1536]{1,0:T(1,128)} %upb.1, f32[1,512]{1,0:T(1,128)} %downb.1, f32[1,512]{1,0:T(1,128)} %gain.1, f32[1,2560,512]{2,1,0:T(8,128)} %scale_hbm.1, ...), custom_call_target="tpu_custom_call" | custom-call | tf_op jit(solution)/shard_map/prep/pallas_call | solution.py:514
  3.7 0.5 collective-permute-start
  4.2 2.5 %collective-permute-done = f32[24,512]{1,0:T(8,128)S(1)} collective-permute-done((f32[24,512]{1,0:T(8,128)}, f32[24,512]{1,0:T(8,128)S(1)}, u32[]{:S(2)}, u32[]{:S(2)}) %collective-permute-start) | collective-permute-done | bytes 49184 | tf_op jit(solution)/shard_map/ppermute | solution.py:525
  6.8 1.4 broadcast_select_fusion.1
  8.2 5.3 %first_norm.1 = (bf16[1024,512]{1,0:T(8,128)(2,1)}, bf16[1024,512]{1,0:T(8,128)(2,1)}, f32[1024,128]{1,0:T(8,128)}) custom-call(s32[1]{0:T(128)} %bitcast.sec, bf16[8,256,512]{2,1,0:T(8,128)(2,1)} %tokens.5, f32[24,512]{1,0:T(8,128)} %get-tuple-element.93.small.small0), custom_call_target="tpu_custom_call" | custom-call | tf_op jit(solution)/shard_map/first_norm/pallas_call | solution.py:537
  13.5 1.1 copy-done.5
  14.6 0.5 copy-done.7
  15.2 39.5 %main.1 = (bf16[4,256,512]{2,1,0:T(8,128)(2,1)}, bf16[1024,512]{1,0:T(8,128)(2,1)}, f32[24,512]{1,0:T(8,128)}, f32[24,512]{1,0:T(8,128)}, bf16[8,256,512]{2,1,0:...) custom-call(s32[1]{0:T(128)} %bitcast.sec, ...), custom_call_target="tpu_custom_call" | custom-call | tf_op jit(solution)/shard_map/main/pallas_call | solution.py:564
  54.7 7.8 %weights.1 = (bf16[16,96,512]{2,1,0:T(8,128)(2,1)}, bf16[16,96,512]{2,1,0:T(8,128)(2,1)}) custom-call(s32[1]{0:T(128)} %bitcast.sec, bf16[1024,512]{1,0:T(8,128)(2,1)} %get-tuple-element.58.gb, bf16[1024,512]{1,0:T(8,128)(2,1)} %get-tuple-element.48.adapted0.adapted, bf16[3,1024,512]{2,1,0:T(8,128)(2,1)} %get-tuple-element.59.act, ...), custom_call_target="tpu_custom_call" | custom-call | tf_op jit(solution)/shard_map/weights/pallas_call | solution.py:610
  62.5 1.0 collective-permute-start.5
  63.5 0.6 pad_add_fusion.spot
  64.1 2.6 %collective-permute-done.5 = bf16[16,96,512]{2,1,0:T(8,128)(2,1)S(1)} collective-permute-done((bf16[16,96,512]{2,1,0:T(8,128)(2,1)}, bf16[16,96,512]{2,1,0:T(8,128)(2,1)S(1)}, u32[]{:S(2)}, u32[]{:S(2)}) %collective-permute-start.5) | collective-permute-done | bytes 1572896 | tf_op jit(solution)/shard_map/ppermute | solution.py:627
  66.7 1.1 copy-done.1
  67.8 3.2 %pack0_0.1 = bf16[768,512]{1,0:T(8,128)(2,1)} custom-call(s32[2]{0:T(128)} %pad_add_fusion.spot, s32[8]{0:T(128)} %speaker.13, bf16[1536,512]{1,0:T(8,128)(2,1)} %bitcast.28, bf16[1536,512]{1,0:T(8,128)(2,1)} %bitcast.33), custom_call_target="tpu_custom_call" | custom-call | tf_op jit(solution)/shard_map/pack0_0/pallas_call | solution.py:732
  71.0 2.7 %collective-permute-start.6 = (bf16[768,512]{1,0:T(8,128)(2,1)}, bf16[768,512]{1,0:T(8,128)(2,1)S(1)}, u32[]{:S(2)}, u32[]{:S(2)}) collective-permute-start(bf16[768,512]{1,0:T(8,128)(2,1)} %pack0_0.1), channel_id=1, source_target_pairs={{0,1},{1,0},{2,3},{3,2},{4,5},{5,4},{6,7},{7,6},{8,9},{9,8},{10,11... | collective-permute-start | bytes 2359304 | tf_op jit(solution)/shard_map/ppermute | solution.py:705
  73.7 3.2 %pack0_1.1 = bf16[768,512]{1,0:T(8,128)(2,1)} custom-call(s32[2]{0:T(128)} %pad_add_fusion.spot, s32[8]{0:T(128)} %speaker.13, bf16[1536,512]{1,0:T(8,128)(2,1)} %bitcast.23, bf16[1536,512]{1,0:T(8,128)(2,1)} %bitcast.12.refs_1_.refs_4_.refs_5_.refs_6_.refs_7_), custom_call_target="tpu_custom_call" | custom-call | tf_op jit(solution)/shard_map/pack0_1/pallas_call | solution.py:732
  76.9 0.1 collective-permute-start.8
  77.0 10.7 %last.1 = (bf16[8,256,512]{2,1,0:T(8,128)(2,1)}, bf16[4,256,512]{2,1,0:T(8,128)(2,1)}, f32[24,512]{1,0:T(8,128)}) custom-call(s32[1]{0:T(128)} %bitcast.sec, bf16[3,1024,512]{2,1,0:T(8,128)(2,1)} %get-tuple-element.51.gpre, bf16[512,1536]{1,0:T(8,128)(2,1)} %bitcast.40, bf16[512,1536]{1,0:T(8,128)(2,1)} %copy-done.5, ...), custom_call_target="tpu_custom_call" | custom-call | tf_op jit(solution)/shard_map/last/pallas_call | solution.py:633
  87.8 1.0 collective-permute-start.9
  88.8 0.9 collective-permute-done.9.refs_8_
  89.6 2.7 %collective-permute-done.8.refs_5_.refs_6_.refs_7_.refs_8_ = bf16[768,512]{1,0:T(8,128)(2,1)S(1)} collective-permute-done((bf16[768,512]{1,0:T(8,128)(2,1)}, bf16[768,512]{1,0:T(8,128)(2,1)S(1)}, u32[]{:S(2)}, u32[]{:S(2)}) %collective-permute-start.8) | collective-permute-done | bytes 786464 | tf_op jit(solution)/shard_map/ppermute | solution.py:705
  92.3 0.9 copy-done.3
  93.2 3.6 %pack1.1 = (bf16[800,512]{1,0:T(8,128)(2,1)}, f32[16,512]{1,0:T(8,128)}) custom-call(s32[2]{0:T(128)} %pad_add_fusion.spot, s32[8]{0:T(128)} %speaker.13, bf16[1536,512]{1,0:T(8,128)(2,1)} %bitcast.29, bf16[1536,512]{1,0:T(8,128)(2,1)} %bitcast.34, bf16[768,512]{1,0:T(8,128)(2,1)} %copy-done.2, bf16[1536,512]{1,0:T(8,128)(2,1)} %bitcast.24, ...), custom_call_target="tpu_custom_call" | custom-call | tf_op jit(solution)/shard_map/pack1/pallas_call | solution.py:732
  96.8 2.1 %collective-permute-start.10 = (bf16[800,512]{1,0:T(8,128)(2,1)}, bf16[800,512]{1,0:T(8,128)(2,1)S(1)}, u32[]{:S(2)}, u32[]{:S(2)}) collective-permute-start(bf16[800,512]{1,0:T(8,128)(2,1)} %get-tuple-element.66.refs_8_), channel_id=1, source_target_pairs={{0,2},{1,3},{2,0},{3,1},{4,6},{5,7},{6,4},{7,5},{8,10},{9,11},{10,... | collective-permute-start | bytes 2457608 | tf_op jit(solution)/shard_map/ppermute | solution.py:705
  98.9 0.5 collective-permute-start.4
  99.4 10.0 %collective-permute-done.10.refs_3_.refs_7_.refs_9_.refs_8_ = bf16[800,512]{1,0:T(8,128)(2,1)S(1)} collective-permute-done((bf16[800,512]{1,0:T(8,128)(2,1)}, bf16[800,512]{1,0:T(8,128)(2,1)S(1)}, u32[]{:S(2)}, u32[]{:S(2)}) %collective-permute-start.10) | collective-permute-done | bytes 819232 | tf_op jit(solution)/shard_map/ppermute | solution.py:705
  109.4 0.9 copy-done
  110.3 3.2 %pack2.1 = (bf16[432,512]{1,0:T(8,128)(2,1)}, f32[16,512]{1,0:T(8,128)}) custom-call(s32[2]{0:T(128)} %pad_add_fusion.spot, s32[8]{0:T(128)} %speaker.13, bf16[1536,512]{1,0:T(8,128)(2,1)} %bitcast.30, bf16[1536,512]{1,0:T(8,128)(2,1)} %bitcast.35, bf16[768,512]{1,0:T(8,128)(2,1)} %copy-done.2, bf16[800,512]{1,0:T(8,128)(2,1)} %copy-done, ...), custom_call_target="tpu_custom_call" | custom-call | tf_op jit(solution)/shard_map/pack2/pallas_call | solution.py:732
  113.6 2.1 %collective-permute-start.11 = (bf16[432,512]{1,0:T(8,128)(2,1)}, bf16[432,512]{1,0:T(8,128)(2,1)S(1)}, u32[]{:S(2)}, u32[]{:S(2)}) collective-permute-start(bf16[432,512]{1,0:T(8,128)(2,1)} %get-tuple-element.68.refs_10_), channel_id=1, source_target_pairs={{0,4},{1,5},{2,6},{3,7},{4,0},{5,1},{6,2},{7,3},{8,12},{9,13},{10,... | collective-permute-start | bytes 1327112 | tf_op jit(solution)/shard_map/ppermute | solution.py:705
  115.7 6.5 %collective-permute-done.11.refs_4_.refs_9_.refs_11_.refs_10_ = bf16[432,512]{1,0:T(8,128)(2,1)S(1)} collective-permute-done((bf16[432,512]{1,0:T(8,128)(2,1)}, bf16[432,512]{1,0:T(8,128)(2,1)S(1)}, u32[]{:S(2)}, u32[]{:S(2)}) %collective-permute-start.11) | collective-permute-done | bytes 442400 | tf_op jit(solution)/shard_map/ppermute | solution.py:705
  122.2 0.8 copy-done.4
  123.0 3.0 %pack3.1 = (bf16[272,512]{1,0:T(8,128)(2,1)}, f32[16,512]{1,0:T(8,128)}) custom-call(s32[2]{0:T(128)} %pad_add_fusion.spot, s32[8]{0:T(128)} %speaker.13, bf16[1536,512]{1,0:T(8,128)(2,1)} %bitcast.31, bf16[1536,512]{1,0:T(8,128)(2,1)} %bitcast.36, bf16[768,512]{1,0:T(8,128)(2,1)} %copy-done.2, bf16[800,512]{1,0:T(8,128)(2,1)} %copy-done, ...), custom_call_target="tpu_custom_call" | custom-call | tf_op jit(solution)/shard_map/pack3/pallas_call | solution.py:732
  126.0 3.1 %collective-permute-start.12 = (bf16[272,512]{1,0:T(8,128)(2,1)}, bf16[272,512]{1,0:T(8,128)(2,1)S(1)}, u32[]{:S(2)}, u32[]{:S(2)}) collective-permute-start(bf16[272,512]{1,0:T(8,128)(2,1)} %get-tuple-element.70.refs_12_), channel_id=1, source_target_pairs={{0,8},{1,9},{2,10},{3,11},{4,12},{5,13},{6,14},{7,15},{8,0},{9,1},... | collective-permute-start | bytes 835592 | tf_op jit(solution)/shard_map/ppermute | solution.py:705
  129.1 1.0 bitcast_dynamic-update-slice_fusion.1
  130.2 9.8 %collective-permute-done.12.refs_5_.refs_11_.refs_13_ = bf16[272,512]{1,0:T(8,128)(2,1)S(1)} collective-permute-done((bf16[272,512]{1,0:T(8,128)(2,1)}, bf16[272,512]{1,0:T(8,128)(2,1)S(1)}, u32[]{:S(2)}, u32[]{:S(2)}) %collective-permute-start.12) | collective-permute-done | bytes 278560 | tf_op jit(solution)/shard_map/ppermute | solution.py:705
  139.9 0.7 copy-done.6
  140.6 3.2 %pack4.1 = (bf16[144,512]{1,0:T(8,128)(2,1)}, f32[16,512]{1,0:T(8,128)}, f32[96,512]{1,0:T(8,128)}, f32[96,512]{1,0:T(8,128)}) custom-call(s32[2]{0:T(128)} %pad_add_fusion.spot, s32[8]{0:T(128)} %speaker.13, bf16[1536,512]{1,0:T(8,128)(2,1)} %bitcast.32, bf16[1536,512]{1,0:T(8,128)(2,1)} %bitcast.37, bf16[768,512]{1,0:T(8,128)(2,1)} %copy-done.2, ...), custom_call_target="tpu_custom_call" | custom-call | tf_op jit(solution)/shard_map/pack4/pallas_call | solution.py:732
  143.9 1.6 %collective-permute-start.13 = (bf16[144,512]{1,0:T(8,128)(2,1)}, bf16[144,512]{1,0:T(8,128)(2,1)S(1)}, u32[]{:S(2)}, u32[]{:S(2)}) collective-permute-start(bf16[144,512]{1,0:T(8,128)(2,1)} %get-tuple-element.72.before), channel_id=1, source_target_pairs={{0,1},{1,0},{2,3},{3,2},{4,5},{5,4},{6,7},{7,6},{8,9},{9,8},{10,11... | collective-permute-start | bytes 442376 | tf_op jit(solution)/shard_map/ppermute | solution.py:705
  145.5 1.0 bitcast_dynamic-update-slice_fusion
  146.5 2.8 %collective-permute-done.13.after = bf16[144,512]{1,0:T(8,128)(2,1)S(1)} collective-permute-done((bf16[144,512]{1,0:T(8,128)(2,1)}, bf16[144,512]{1,0:T(8,128)(2,1)S(1)}, u32[]{:S(2)}, u32[]{:S(2)}) %collective-permute-start.13) | collective-permute-done | bytes 147488 | tf_op jit(solution)/shard_map/ppermute | solution.py:705
  149.3 0.6 copy-done.10
  150.0 3.1 %finish.1 = (f32[160,512]{1,0:T(8,128)}, f32[160,512]{1,0:T(8,128)}, f32[32,1536]{1,0:T(8,128)}, f32[96,512]{1,0:T(8,128)}, f32[16,512]{1,0:T(8,128)}) custom-call(s32[2]{0:T(128)} %pad_add_fusion.spot, bf16[144,512]{1,0:T(8,128)(2,1)} %get-tuple-element.72.before, bf16[144,512]{1,0:T(8,128)(2,1)} %copy-done.10, f32[16,512]{1,0:T(8,128)} %get-tuple-element.73.smalls_in, ...), custom_call_target="tpu_custom_call" | custom-call | tf_op jit(solution)/shard_map/finish/pallas_call | solution.py:765
  153.2 0.7 slice.17
  153.9 0.7 dynamic-slice_bitcast_fusion
  154.6 0.6 copy.24
  155.2 0.6 dynamic-slice_bitcast_fusion.1
  155.8 1.4 fusion
  (31 shorter events, 0.3 us)
Async XLA Ops:
  0.6 12.9 %collective-permute-start.1 = (bf16[512,1536]{1,0:T(8,128)(2,1)}, bf16[512,1536]{1,0:T(8,128)(2,1)S(1)}, u32[]{:S(2)}, u32[]{:S(2)}) collective-permute-start(bf16[512,1536]{1,0:T(8,128)(2,1)} %bitcast.38), channel_id=1, source_target_pairs={{0,16},{16,0},{1,17},{17,1},{2,18},{18,2},{3,19},{19,3},{4,20},{20... | collective-permute-start | bytes 4718600 | tf_op jit(solution)/shard_map/ppermute | solution.py:527
  1.2 12.3 %collective-permute-start.2 = (bf16[1536,512]{1,0:T(8,128)(2,1)}, bf16[1536,512]{1,0:T(8,128)(2,1)S(1)}, u32[]{:S(2)}, u32[]{:S(2)}) collective-permute-start(bf16[1536,512]{1,0:T(8,128)(2,1)} %bitcast.41), channel_id=1, source_target_pairs={{0,16},{16,0},{1,17},{17,1},{2,18},{18,2},{3,19},{19,3},{4,20},{20... | collective-permute-start | bytes 4718600 | tf_op jit(solution)/shard_map/ppermute | solution.py:528
  3.7 3.0 %collective-permute-start = (f32[24,512]{1,0:T(8,128)}, f32[24,512]{1,0:T(8,128)S(1)}, u32[]{:S(2)}, u32[]{:S(2)}) collective-permute-start(f32[24,512]{1,0:T(8,128)} %get-tuple-element.47), channel_id=1, source_target_pairs={{0,16},{16,0},{1,17},{17,1},{2,18},{18,2},{3,19},{19,3},{4,20},{20... | collective-permute-start | bytes 147464 | tf_op jit(solution)/shard_map/ppermute | solution.py:525
  13.5 1.1 copy-start.5
  13.5 1.6 %copy-start.7 = (bf16[1536,512]{1,0:T(8,128)(2,1)}, bf16[1536,512]{1,0:T(8,128)(2,1)S(1)}, u32[]{:S(2)}) copy-start(bf16[1536,512]{1,0:T(8,128)(2,1)S(1)} %collective-permute-done.2.down_got) | copy-start | bytes 4718596
  54.6 8.8 %copy-start.12 = (bf16[16,96,512]{2,1,0:T(8,128)(2,1)S(1)}, bf16[16,96,512]{2,1,0:T(8,128)(2,1)}, u32[]{:S(2)}) copy-start(bf16[16,96,512]{2,1,0:T(8,128)(2,1)} %get-tuple-element.63) | copy-start | bytes 4718596
  62.5 4.2 %collective-permute-start.5 = (bf16[16,96,512]{2,1,0:T(8,128)(2,1)}, bf16[16,96,512]{2,1,0:T(8,128)(2,1)S(1)}, u32[]{:S(2)}, u32[]{:S(2)}) collective-permute-start(bf16[16,96,512]{2,1,0:T(8,128)(2,1)} %get-tuple-element.61), channel_id=1, source_target_pairs={{0,16},{16,0},{1,17},{17,1},{2,18},{18,2},{3,19},{19,3},{4,20},{20... | collective-permute-start | bytes 4718600 | tf_op jit(solution)/shard_map/ppermute | solution.py:627
  63.4 10.3 %collective-permute-start.7 = (bf16[16,96,512]{2,1,0:T(8,128)(2,1)S(1)}, bf16[16,96,512]{2,1,0:T(8,128)(2,1)}, u32[]{:S(2)}, u32[]{:S(2)}) collective-permute-start(bf16[16,96,512]{2,1,0:T(8,128)(2,1)S(1)} %copy-done.12), channel_id=1, source_target_pairs={{0,16},{16,0},{1,17},{17,1},{2,18},{18,2},{3,19},{19,3},{4,20},{20... | collective-permute-start | bytes 4718600 | tf_op jit(solution)/shard_map/ppermute | solution.py:606
  66.7 1.1 copy-start.1
  71.0 18.6 %collective-permute-start.6 = (bf16[768,512]{1,0:T(8,128)(2,1)}, bf16[768,512]{1,0:T(8,128)(2,1)S(1)}, u32[]{:S(2)}, u32[]{:S(2)}) collective-permute-start(bf16[768,512]{1,0:T(8,128)(2,1)} %pack0_0.1), channel_id=1, source_target_pairs={{0,1},{1,0},{2,3},{3,2},{4,5},{5,4},{6,7},{7,6},{8,9},{9,8},{10,11... | collective-permute-start | bytes 2359304 | tf_op jit(solution)/shard_map/ppermute | solution.py:705
  76.9 15.4 %collective-permute-start.8 = (bf16[768,512]{1,0:T(8,128)(2,1)}, bf16[768,512]{1,0:T(8,128)(2,1)S(1)}, u32[]{:S(2)}, u32[]{:S(2)}) collective-permute-start(bf16[768,512]{1,0:T(8,128)(2,1)} %pack0_1.1), channel_id=1, source_target_pairs={{0,1},{1,0},{2,3},{3,2},{4,5},{5,4},{6,7},{7,6},{8,9},{9,8},{10,11... | collective-permute-start | bytes 2359304 | tf_op jit(solution)/shard_map/ppermute | solution.py:705
  77.0 10.8 %copy-start.8 = (f32[24,512]{1,0:T(8,128)S(1)}, f32[24,512]{1,0:T(8,128)}, u32[]{:S(2)}) copy-start(f32[24,512]{1,0:T(8,128)} %get-tuple-element.65.refs_7_) | copy-start | bytes 147460
  87.8 1.9 %collective-permute-start.9 = (f32[24,512]{1,0:T(8,128)S(1)}, f32[24,512]{1,0:T(8,128)S(1)}, u32[]{:S(2)}, u32[]{:S(2)}) collective-permute-start(f32[24,512]{1,0:T(8,128)S(1)} %broadcast_select_fusion), channel_id=1, source_target_pairs={{0,16},{16,0},{1,17},{17,1},{2,18},{18,2},{3,19},{19,3},{4,20},{20... | collective-permute-start | bytes 147464 | tf_op jit(solution)/shard_map/ppermute | solution.py:665
  89.6 2.7 %copy-start.11 = (f32[24,512]{1,0:T(8,128)}, f32[24,512]{1,0:T(8,128)S(1)}, u32[]{:S(2)}) copy-start(f32[24,512]{1,0:T(8,128)S(1)} %collective-permute-done.9.refs_8_) | copy-start | bytes 147460
  89.6 2.7 %copy-start.2 = (bf16[768,512]{1,0:T(8,128)(2,1)}, bf16[768,512]{1,0:T(8,128)(2,1)S(1)}, u32[]{:S(2)}) copy-start(bf16[768,512]{1,0:T(8,128)(2,1)S(1)} %collective-permute-done.6.refs_2_) | copy-start | bytes 2359300
  92.3 0.9 copy-start.3
  96.8 12.7 %collective-permute-start.10 = (bf16[800,512]{1,0:T(8,128)(2,1)}, bf16[800,512]{1,0:T(8,128)(2,1)S(1)}, u32[]{:S(2)}, u32[]{:S(2)}) collective-permute-start(bf16[800,512]{1,0:T(8,128)(2,1)} %get-tuple-element.66.refs_8_), channel_id=1, source_target_pairs={{0,2},{1,3},{2,0},{3,1},{4,6},{5,7},{6,4},{7,5},{8,10},{9,11},{10,... | collective-permute-start | bytes 2457608 | tf_op jit(solution)/shard_map/ppermute | solution.py:705
  98.9 30.2 %collective-permute-start.3 = (bf16[4,256,512]{2,1,0:T(8,128)(2,1)}, bf16[4,256,512]{2,1,0:T(8,128)(2,1)S(1)}, u32[]{:S(2)}, u32[]{:S(2)}) collective-permute-start(bf16[4,256,512]{2,1,0:T(8,128)(2,1)} %get-tuple-element.50), channel_id=1, source_target_pairs={{0,16},{16,0},{1,17},{17,1},{2,18},{18,2},{3,19},{19,3},{4,20},{20... | collective-permute-start | bytes 3145736 | tf_op jit(solution)/shard_map/ppermute | solution.py:607
  98.9 46.6 %collective-permute-start.4 = (bf16[4,256,512]{2,1,0:T(8,128)(2,1)}, bf16[4,256,512]{2,1,0:T(8,128)(2,1)S(1)}, u32[]{:S(2)}, u32[]{:S(2)}) collective-permute-start(bf16[4,256,512]{2,1,0:T(8,128)(2,1)} %get-tuple-element.57), channel_id=1, source_target_pairs={{0,16},{16,0},{1,17},{17,1},{2,18},{18,2},{3,19},{19,3},{4,20},{20... | collective-permute-start | bytes 3145736 | tf_op jit(solution)/shard_map/ppermute | solution.py:664
  109.4 0.9 copy-start
  113.6 8.6 %collective-permute-start.11 = (bf16[432,512]{1,0:T(8,128)(2,1)}, bf16[432,512]{1,0:T(8,128)(2,1)S(1)}, u32[]{:S(2)}, u32[]{:S(2)}) collective-permute-start(bf16[432,512]{1,0:T(8,128)(2,1)} %get-tuple-element.68.refs_10_), channel_id=1, source_target_pairs={{0,4},{1,5},{2,6},{3,7},{4,0},{5,1},{6,2},{7,3},{8,12},{9,13},{10,... | collective-permute-start | bytes 1327112 | tf_op jit(solution)/shard_map/ppermute | solution.py:705
  122.2 0.8 copy-start.4
  126.0 13.9 %collective-permute-start.12 = (bf16[272,512]{1,0:T(8,128)(2,1)}, bf16[272,512]{1,0:T(8,128)(2,1)S(1)}, u32[]{:S(2)}, u32[]{:S(2)}) collective-permute-start(bf16[272,512]{1,0:T(8,128)(2,1)} %get-tuple-element.70.refs_12_), channel_id=1, source_target_pairs={{0,8},{1,9},{2,10},{3,11},{4,12},{5,13},{6,14},{7,15},{8,0},{9,1},... | collective-permute-start | bytes 835592 | tf_op jit(solution)/shard_map/ppermute | solution.py:705
  139.9 0.7 copy-start.6
  143.9 5.4 %collective-permute-start.13 = (bf16[144,512]{1,0:T(8,128)(2,1)}, bf16[144,512]{1,0:T(8,128)(2,1)S(1)}, u32[]{:S(2)}, u32[]{:S(2)}) collective-permute-start(bf16[144,512]{1,0:T(8,128)(2,1)} %get-tuple-element.72.before), channel_id=1, source_target_pairs={{0,1},{1,0},{2,3},{3,2},{4,5},{5,4},{6,7},{7,6},{8,9},{9,8},{10,11... | collective-permute-start | bytes 442376 | tf_op jit(solution)/shard_map/ppermute | solution.py:705
  145.5 3.8 %collective-permute-start.14 = (f32[96,512]{1,0:T(8,128)}, f32[96,512]{1,0:T(8,128)S(1)}, u32[]{:S(2)}, u32[]{:S(2)}) collective-permute-start(f32[96,512]{1,0:T(8,128)} %get-tuple-element.75), channel_id=1, source_target_pairs={{0,16},{16,0},{1,17},{17,1},{2,18},{18,2},{3,19},{19,3},{4,20},{20... | collective-permute-start | bytes 589832 | tf_op jit(solution)/shard_map/ppermute | solution.py:762
  149.3 0.7 copy-start.10
  149.3 0.7 copy-start.9

commit v2 on v1

--- a/solution.py
+++ b/solution.py
@@ -6,6 +6,7 @@
 from jax.experimental import pallas as pl
 from jax.experimental.pallas import tpu as pltpu
 from jax.sharding import PartitionSpec as P
+
 
 F32 = jnp.float32
 BF16 = jnp.bfloat16
@@ -15,7 +16,7 @@
 DENSITY = 0.3989422804014327
 BLOCKS = 16
 ORDERS = ((0, 1, 2, 3), (2, 0, 1, 3))
-ANY = pl.BlockSpec(memory_space=pltpu.HBM)
+ANY = pl.BlockSpec(memory_space=pl.ANY)
 VMEM = pl.BlockSpec(memory_space=pltpu.VMEM)
 SMEM = pl.BlockSpec(memory_space=pltpu.SMEM)
 
@@ -101,14 +102,6 @@
         copy.wait()
 
 
-def first_norm_body(sec, tokens, small, adapted, normed, inv):
-    clip = pl.program_id(0)
-    a, n, r = normalize(tokens[0].astype(F32), small, clip)
-    adapted[...] = a
-    normed[...] = n
-    inv[...] = r
-
-
 def forward_tiles(adapted, up, down, small, act, slope, acc):
     clips = acc.shape[0] // 256
     for j in range(3):
@@ -214,87 +207,124 @@
 
 
 def main_body(
-    sec, valid, adapted0, tokens, cot, small0, small1, up_own, up_got, down_own, down_got,
-    gin1, gb0, sums0, sums1, out_own, out_send, act_hbm, gpre_hbm, keep, send,
-    up0, down0, up1, down1, act0, slope0, act1, slope1, acc, adapted1, normed1, inv1, branch0, gb1,
-    out0, out1, upd, dnd, sems,
+    sec, valid, own_small, got_small, tokens, cot, up_own, up_got, down_own, down_got,
+    sums0, sums1, gin1, gb0_hbm, adapted_hbm, normed_hbm, inv_hbm, out_own, out_send, act_hbm,
+    gpre_hbm, keep, send, small0_out,
+    up0, down0, up1, down1, act0, slope0, act1, slope1, acc, adapted0, normed, inv, adapted1, branch0,
+    gb, v, grad, out0, out1, small0, small1, upd, dnd, sems, pieces,
 ):
     clips = acc.shape[0] // 256
+    mine = pl.ds(sec[0] * clips, clips)
+    loads = (
+        pltpu.make_async_copy(tokens.at[mine], v, sems.at[6, 0]),
+        pltpu.make_async_copy(cot.at[mine], grad, sems.at[6, 1]),
+    )
+    loads[0].start()
     weights = (up_own, up_got, down_own, down_got)
     place_weights(sec, 0, *weights, up0, down0, sems.at[0], True)
     place_weights(sec, 1, *weights, up1, down1, sems.at[1], True)
+    loads[1].start()
+    first = sec[0] == 0
+    small0[...] = pick(first, own_small[...], got_small[...])
+    small1[...] = pick(first, got_small[...], own_small[...])
+    small0_out[...] = small0[...]
+    sums0[...] = jnp.zeros_like(sums0)
+    sums1[...] = jnp.zeros_like(sums1)
+    loads[0].wait()
+
+    def begin(r):
+        rows = pl.ds(pl.multiple_of(r * 256, 256), 256)
+        adapted0[rows], normed[rows], inv[rows] = normalize(v[r].astype(F32), small0, r)
+
+    pl.loop(0, clips)(begin)
+    saves = [
+        pltpu.make_async_copy(source, target, sems.at[7 + n // 2, n % 2])
+        for n, (source, target) in enumerate(
+            ((normed, normed_hbm), (inv, inv_hbm), (adapted0, adapted_hbm), (act0, act_hbm))
+        )
+    ]
+    for copy in saves[:3]:
+        copy.start()
     place_weights(sec, 0, *weights, up0, down0, sems.at[0], False)
     forward_tiles(adapted0, up0, down0, small0, act0, slope0, acc)
-    save_act = pltpu.make_async_copy(act0, act_hbm, sems.at[2, 0])
-    save_act.start()
+    saves[3].start()
+    saves[0].wait()
+    saves[1].wait()
 
     def between(r):
         rows = pl.ds(pl.multiple_of(r * 256, 256), 256)
         branch = acc[rows] + small0[DOWNB : DOWNB + 1]
         branch0[rows] = branch
-        result = (tokens[r].astype(F32) + small0[GAIN : GAIN + 1] * branch).astype(BF16)
+        result = (v[r].astype(F32) + small0[GAIN : GAIN + 1] * branch).astype(BF16)
         out0[r] = result
-        a, n, i = normalize(result.astype(F32), small1, r)
-        adapted1[rows] = a
-        normed1[rows] = n
-        inv1[rows] = i
+        adapted1[rows], normed[rows], inv[rows] = normalize(result.astype(F32), small1, r)
 
     pl.loop(0, clips)(between)
     place_weights(sec, 1, *weights, up1, down1, sems.at[1], False)
     forward_tiles(adapted1, up1, down1, small1, act1, slope1, acc)
-    sums0[...] = jnp.zeros_like(sums0)
-    sums1[...] = jnp.zeros_like(sums1)
+    loads[1].wait()
 
     def top(r):
         rows = pl.ds(pl.multiple_of(r * 256, 256), 256)
         branch = acc[rows] + small1[DOWNB : DOWNB + 1]
         gain = small1[GAIN : GAIN + 1]
         out1[r] = (out0[r].astype(F32) + gain * branch).astype(BF16)
-        grad = cot[r].astype(F32) * valid[sec[0] * clips + r].astype(F32)
-        low = (grad * gain).astype(BF16)
-        gb1[rows] = low
-        sums1[GAIN : GAIN + 1] += rowsum(grad * branch)
+        above = grad[r].astype(F32) * valid[sec[0] * clips + r].astype(F32)
+        low = (above * gain).astype(BF16)
+        gb[rows] = low
+        sums1[GAIN : GAIN + 1] += rowsum(above * branch)
         sums1[DOWNB : DOWNB + 1] += rowsum(low.astype(F32))
 
     pl.loop(0, clips)(top)
-    half_own = out_own.at[pl.ds(sec[0] * clips, clips)]
+    half_own = out_own.at[mine]
     route(sec, out0, out1, half_own, out_send, sems.at[4], True)
     for j in range(3):
-        activation_tile(j, gb1, down1, slope1, sums1)
+        activation_tile(j, gb, down1, slope1, sums1)
         for r in range(clips):
             rows = slice(r * 256, (r + 1) * 256)
             part = dot(slope1[j, rows], up1[:, j * TILE : (j + 1) * TILE], NT)
             acc[rows] = part if j == 0 else acc[rows] + part
-        weight_tile(j, gb1, adapted1, act1[j], slope1[j], upd, dnd)
+        weight_tile(j, gb, adapted1, act1[j], slope1[j], upd, dnd)
     route(sec, upd, dnd, keep, send, sems.at[3], True)
+
+    def move(r):
+        rows = pl.ds(pl.multiple_of(r * 256, 256), 256)
+        return (
+            pltpu.make_async_copy(grad.at[r], gin1.at[r], pieces.at[0, r]),
+            pltpu.make_async_copy(gb.at[rows], gb0_hbm.at[rows], pieces.at[1, r]),
+        )
 
     def under(r):
         rows = pl.ds(pl.multiple_of(r * 256, 256), 256)
-        grad = cot[r].astype(F32) * valid[sec[0] * clips + r].astype(F32)
+        above = grad[r].astype(F32) * valid[sec[0] * clips + r].astype(F32)
         gin, smalls, g_scale, g_shift = norm_backward(
-            acc[rows], normed1[rows], inv1[rows], small1, r, grad, out0[r].astype(F32)
+            acc[rows], normed[rows], inv[rows], small1, r, above, out0[r].astype(F32)
         )
-        gin1[r] = gin
+        grad[r] = gin
         sums1[TAPS : TAPS + 8] += smalls
         sums1[pl.ds(SCALE + r, 1)] = g_scale
         sums1[pl.ds(SHIFT + r, 1)] = g_shift
         grad0 = gin.astype(F32)
         low = (grad0 * small0[GAIN : GAIN + 1]).astype(BF16)
-        gb0[rows] = low
+        gb[rows] = low
+        for copy in move(r):
+            copy.start()
         sums0[GAIN : GAIN + 1] += rowsum(grad0 * branch0[rows])
         sums0[DOWNB : DOWNB + 1] += rowsum(low.astype(F32))
 
     pl.loop(0, clips)(under)
-    saves = []
+    tiles = []
     for j in range(3):
-        activation_tile(j, gb0, down0, slope0, sums0)
-        saves.append(pltpu.make_async_copy(slope0.at[j], gpre_hbm.at[j], sems.at[5 + j // 2, j % 2]))
-        saves[-1].start()
-    save_act.wait()
+        activation_tile(j, gb, down0, slope0, sums0)
+        tiles.append(pltpu.make_async_copy(slope0.at[j], gpre_hbm.at[j], sems.at[5 + j // 2 * 4, j % 2]))
+        tiles[-1].start()
     route(sec, out0, out1, half_own, out_send, sems.at[4], False)
     route(sec, upd, dnd, keep, send, sems.at[3], False)
-    for copy in saves:
+    for copy in saves[2:] + tiles:
         copy.wait()
+    for r in range(clips):
+        for copy in move(r):
+            copy.wait()
 
 
 def weights_body(sec, gb, adapted, act, gpre, keep, send, upd, dnd, sems):
@@ -386,7 +416,8 @@
     return total
 
 
-def pack_body(step, blocks, bases, share, extras, spot, speaker, *refs):
+def pack_body(step, blocks, bases, share, extras, sec, place, speaker, *refs):
+    spot = (sec[0], place[0])
     levels = step + 2
     sources = [refs[b * levels : (b + 1) * levels] for b in range(blocks)]
     refs = refs[blocks * levels :]
@@ -456,8 +487,10 @@
 
 
 def finish_body(
-    spot, before, after, smalls_in, mine, got, scale, shift, up, down, smalls, rows_of, tail, sems
+    sec, place, before, after, smalls_in, mine, got, scale, shift, up, down, taps, conv, upb, downb, gain,
+    rows_of, tail, sems,
 ):
+    spot = (sec[0], place[0])
     size = rows_of.shape[0] // 2
     bit = bit_of(spot, GATHER[3])
     copies = []
@@ -475,7 +508,6 @@
     for copy in copies:
         copy.wait()
     total = smalls_in[...] + tail[...].astype(F32)
-    smalls[...] = total
     owned = scale.shape[0]
     count = 2 * size
     who = total[13:14, :count] * 64.0 + total[14:15, :count]
@@ -484,14 +516,29 @@
     kind = (lax.broadcasted_iota(jnp.int32, (owned, count), 1) >> 2) & 1
     for k, out in enumerate((scale, shift)):
         out[...] = dot(jnp.where(hit & (kind == k), 1.0, 0.0).astype(BF16), rows_of[...], NN)
+    width = total.shape[1]
+    lanes = width // BLOCKS
+    turn = lax.rem(BLOCKS - spot[1], BLOCKS)
+    cut = pltpu.roll(total, turn * lanes, 1)[:, :lanes]
+    for k in range(7):
+        taps[k] = cut[k : k + 1]
+    conv[...] = cut[CONV : CONV + 1]
+    downb[...] = cut[DOWNB : DOWNB + 1]
+    gain[...] = cut[GAIN : GAIN + 1]
+    line = jnp.concatenate([total[UPB + k : UPB + k + 1] for k in range(3)], axis=1)
+    upb[...] = pltpu.roll(line, turn * 3 * lanes, 1)[:, : 3 * lanes]
 
 
 def struct(shape, dtype):
     return jax.ShapeDtypeStruct(shape, dtype)
 
 
-def params(limit=60):
+def params(limit):
     return pltpu.CompilerParams(vmem_limit_bytes=limit * 1024 * 1024)
+
+
+def cost(flops, moved):
+    return pl.CostEstimate(flops=int(flops), bytes_accessed=int(moved), transcendentals=0)
 
 
 def local(
@@ -508,7 +555,6 @@
     half = clips // 2
     rows = half * frames
     sec = section[None]
-    spot = jnp.stack([section, place])
     swap = [(0, 1), (1, 0)]
 
     own_small, other_small = pl.pallas_call(
@@ -526,82 +572,66 @@
     up_own, down_own = up_weight[0], down_weight[0]
     up_got = lax.ppermute(up_own, "section", swap)
     down_got = lax.ppermute(down_own, "section", swap)
-    small0 = jnp.where(first_section, own_small, got_small)
-    small1 = jnp.where(first_section, got_small, own_small)
-
     clip_block = (1, frames, width)
-    mine = pl.BlockSpec(clip_block, lambda c, sec: (sec[0] * half + c, 0, 0))
     whole_small = pl.BlockSpec((SMALL, width), lambda c, sec: (0, 0))
-    flat = pl.BlockSpec((frames, width), lambda c, sec: (c, 0))
-    flat_inv = pl.BlockSpec((frames, 128), lambda c, sec: (c, 0))
-    adapted0, normed0, inv0 = pl.pallas_call(
-        first_norm_body,
-        grid_spec=pltpu.PrefetchScalarGridSpec(
-            num_scalar_prefetch=1,
-            grid=(half,),
-            in_specs=[mine, whole_small],
-            out_specs=[flat, flat, flat_inv],
-        ),
-        out_shape=[
-            struct((rows, width), BF16), struct((rows, width), BF16), struct((rows, 128), F32)
-        ],
-        name="first_norm",
-    )(sec, tokens, small0)
-
     half_struct = struct((half, frames, width), BF16)
     whole_struct = struct((clips, frames, width), BF16)
     small_struct = struct((SMALL, width), F32)
+    flat_struct = struct((rows, width), BF16)
     tiles = hidden // TILE
     tiled = (tiles, rows, TILE)
     share = hidden // BLOCKS
     gradient = (BLOCKS, share, width)
     gradient_struct = struct(gradient, BF16)
-    half_spec = pl.BlockSpec((half, frames, width), lambda i, sec, valid: (sec[0], 0, 0))
+    product = 2 * rows * width * hidden
 
     def full(*shape):
         return pl.BlockSpec(shape, lambda i, *_: (0,) * len(shape))
 
-    gin1, gb0, sums0, sums1, out_own, out_send, act0, gpre0, keep1, send1 = pl.pallas_call(
+    (
+        sums0, sums1, gin1, gb0, adapted0, normed0, inv0, out_own, out_send, act0, gpre0, keep1, send1,
+        small0,
+    ) = pl.pallas_call(
         main_body,
-        grid_spec=pltpu.PrefetchScalarGridSpec(
-            num_scalar_prefetch=2,
-            grid=(1,),
-            in_specs=[full(rows, width), half_spec, half_spec, full(SMALL, width), full(SMALL, width)]
-            + [ANY] * 4,
-            out_specs=[full(half, frames, width), full(rows, width)]
-            + [full(SMALL, width)] * 2
-            + [ANY] * 6,
-            scratch_shapes=[
-                pltpu.VMEM((width, hidden), BF16),
-                pltpu.VMEM((hidden, width), BF16),
-                pltpu.VMEM((width, hidden), BF16),
-                pltpu.VMEM((hidden, width), BF16),
-                pltpu.VMEM(tiled, BF16),
-                pltpu.VMEM(tiled, BF16),
-                pltpu.VMEM(tiled, BF16),
-                pltpu.VMEM(tiled, BF16),
-                pltpu.VMEM((rows, width), F32),
-                pltpu.VMEM((rows, width), BF16),
-                pltpu.VMEM((rows, width), BF16),
-                pltpu.VMEM((rows, 128), F32),
-                pltpu.VMEM((rows, width), F32),
-                pltpu.VMEM((rows, width), BF16),
-                pltpu.VMEM((half, frames, width), BF16),
-                pltpu.VMEM((half, frames, width), BF16),
-                pltpu.VMEM(gradient, BF16),
-                pltpu.VMEM(gradient, BF16),
-                pltpu.SemaphoreType.DMA((7, 2)),
-            ],
-        ),
         out_shape=[
-            half_struct, struct((rows, width), BF16), small_struct, small_struct,
-            whole_struct, half_struct, struct(tiled, BF16), struct(tiled, BF16),
-            gradient_struct, gradient_struct,
+            small_struct, small_struct, half_struct, flat_struct, flat_struct, flat_struct,
+            struct((rows, 128), F32), whole_struct, half_struct, struct(tiled, BF16),
+            struct(tiled, BF16), gradient_struct, gradient_struct, small_struct,
         ],
-        compiler_params=params(),
+        in_specs=[SMEM, SMEM, VMEM, VMEM] + [ANY] * 6,
+        out_specs=[VMEM, VMEM] + [ANY] * 11 + [VMEM],
+        scratch_shapes=[
+            pltpu.VMEM((width, hidden), BF16),
+            pltpu.VMEM((hidden, width), BF16),
+            pltpu.VMEM((width, hidden), BF16),
+            pltpu.VMEM((hidden, width), BF16),
+            pltpu.VMEM(tiled, BF16),
+            pltpu.VMEM(tiled, BF16),
+            pltpu.VMEM(tiled, BF16),
+            pltpu.VMEM(tiled, BF16),
+            pltpu.VMEM((rows, width), F32),
+            pltpu.VMEM((rows, width), BF16),
+            pltpu.VMEM((rows, width), BF16),
+            pltpu.VMEM((rows, 128), F32),
+            pltpu.VMEM((rows, width), BF16),
+            pltpu.VMEM((rows, width), F32),
+            pltpu.VMEM((rows, width), BF16),
+            pltpu.VMEM((half, frames, width), BF16),
+            pltpu.VMEM((half, frames, width), BF16),
+            pltpu.VMEM((half, frames, width), BF16),
+            pltpu.VMEM((half, frames, width), BF16),
+            pltpu.VMEM((SMALL, width), F32),
+            pltpu.VMEM((SMALL, width), F32),
+            pltpu.VMEM(gradient, BF16),
+            pltpu.VMEM(gradient, BF16),
+            pltpu.SemaphoreType.DMA((10, 2)),
+            pltpu.SemaphoreType.DMA((2, half)),
+        ],
+        compiler_params=params(42),
+        cost_estimate=cost(9 * product, 24 << 20),
         name="main",
     )(
-        sec, valid, adapted0, tokens, out_cotangent, small0, small1, up_own, up_got, down_own, down_got
+        sec, valid, own_small, got_small, tokens, out_cotangent, up_own, up_got, down_own, down_got
     )
     got1 = lax.ppermute(send1, "section", swap)
     got_out = lax.ppermute(out_send, "section", swap)
@@ -621,7 +651,8 @@
             ],
         ),
         out_shape=[gradient_struct, gradient_struct],
-        compiler_params=params(),
+        compiler_params=params(20),
+        cost_estimate=cost(2 * product, 12 << 20),
         name="weights",
     )(sec, gb0, adapted0, act0, gpre0)
     got0 = lax.ppermute(send0, "section", swap)
@@ -656,7 +687,8 @@
             ),
             out_shape=[whole_struct, half_struct, small_struct],
             input_output_aliases={10 + i: i for i in range(len(others))},
-            compiler_params=params(),
+            compiler_params=params(14),
+            cost_estimate=cost(8 * product, 12 << 20),
             name="last",
         )(sec, gpre0, up_own, up_got, normed0, inv0, small0, gin1, tokens, sums, *others)
 
@@ -671,28 +703,10 @@
     input_grads = joined(gin_own, got_gin)
     pairs = [[keep0, got0], [keep1, got1]]
     if devices == BLOCKS:
-        outs = halved(spot, speaker, pairs, sums0, sums1, got_sums, table_rows)
+        outs = halved(sec, place[None], speaker, pairs, sums0, sums1, got_sums, table_rows)
     else:
         outs = scattered(section, place, devices, speaker, pairs, sums0, sums1, got_sums, table_rows)
-    up_share, down_share, table_scale, table_shift, smalls = outs
-    lanes = width // devices
-    own_lanes = lax.dynamic_slice_in_dim(smalls, place * lanes, lanes, 1)
-    up_bias_share = lax.dynamic_slice_in_dim(
-        smalls[UPB : UPB + 3].reshape(-1), place * (hidden // devices), hidden // devices, 0
-    )
-    return (
-        block_outputs,
-        input_grads,
-        own_lanes[TAPS : TAPS + 7][None],
-        own_lanes[CONV : CONV + 1],
-        table_scale[None],
-        table_shift[None],
-        up_share[None],
-        up_bias_share[None],
-        down_share[None],
-        own_lanes[DOWNB : DOWNB + 1],
-        own_lanes[GAIN : GAIN + 1],
-    )
+    return (block_outputs, input_grads) + outs
 
 
 def exchanged(packet, step):
@@ -705,17 +719,17 @@
     return lax.ppermute(packet, PAIR, moves)
 
 
-def halved(spot, speaker, pairs, sums0, sums1, got_sums, table_rows):
+def halved(sec, place, speaker, pairs, sums0, sums1, got_sums, table_rows):
     _, share, width = pairs[0][0].shape
     pairs = [[piece.reshape(-1, width) for piece in pair] for pair in pairs]
 
-    def pack(step, block_sources, bases, extra_in, name):
+    def pack(step, block_sources, bases, extra_in):
         blocks = len(block_sources)
         levels = step + 2
         count = 1 if step == 4 else 8 >> step
         rows = count * share
         extras = len(extra_in) > 0
-        outs, specs = [], []
+        outs = []
         size = (8 << step) if extras else 0
         length = (blocks * rows if step < 4 else 0) + (size + 16 if extras else 0)
         outs.append(struct((length, width), BF16))
@@ -732,24 +746,24 @@
         return pl.pallas_call(
             functools.partial(pack_body, step, blocks, bases, share, int(extras)),
             out_shape=outs,
-            in_specs=[SMEM, SMEM] + [ANY] * (blocks * levels) + extra_specs,
+            in_specs=[SMEM, SMEM, SMEM] + [ANY] * (blocks * levels) + extra_specs,
             out_specs=[VMEM] * len(outs),
             scratch_shapes=[
                 pltpu.VMEM((blocks, levels, rows, width), BF16),
                 pltpu.VMEM((16, width), BF16),
                 pltpu.SemaphoreType.DMA((3, max(levels, 3))),
             ],
-            compiler_params=params(),
-            name=name,
-        )(spot, speaker, *[x for sources in block_sources for x in sources], *extra_in)
+            compiler_params=params(8),
+            cost_estimate=cost(0, 4 << 20),
+        )(sec, place, speaker, *[x for sources in block_sources for x in sources], *extra_in)
 
     for b in (1, 0):
-        (packet,) = pack(0, [pairs[b]], [[0]], [], f"pack0_{b}")
+        (packet,) = pack(0, [pairs[b]], [[0]], [])
         pairs[b].append(exchanged(packet, 0))
     bases = [[0, 0], [0, 0]]
     extra_in = [sums0, sums1, got_sums]
     for step in range(1, 4):
-        packet, smalls = pack(step, pairs, bases, extra_in, f"pack{step}")
+        packet, smalls = pack(step, pairs, bases, extra_in)
         got = exchanged(packet, step)
         rows = (8 >> step) * share
         for b in range(2):
@@ -757,30 +771,39 @@
             bases[b].append(b * rows)
         bases = [list(x) for x in bases]
         extra_in = [packet, got, smalls]
-    packet, smalls, mine, away = pack(4, pairs, bases, extra_in, "pack4")
+    packet, smalls, mine, away = pack(4, pairs, bases, extra_in)
     got = exchanged(packet, 0)
     got_share = lax.ppermute(away, "section", [(0, 1), (1, 0)])
     owned = table_rows // BLOCKS
     up_rows = width // BLOCKS
-    scale, shift, up, down, smalls = pl.pallas_call(
+    lanes = width // BLOCKS
+    one = struct((1, lanes), F32)
+    scale, shift, up, down, taps, conv, upb, downb, gain = pl.pallas_call(
         finish_body,
         out_shape=[
             struct((owned, width), F32),
             struct((owned, width), F32),
             struct((up_rows, 3 * TILE), F32),
             struct((share, width), F32),
-            struct((SCALE, width), F32),
+            struct((7, 1, lanes), F32),
+            one,
+            struct((1, 3 * lanes), F32),
+            one,
+            one,
         ],
-        in_specs=[SMEM, ANY, ANY, VMEM, VMEM, VMEM],
-        out_specs=[VMEM] * 5,
+        in_specs=[SMEM, SMEM, ANY, ANY, VMEM, VMEM, VMEM],
+        out_specs=[VMEM] * 9,
         scratch_shapes=[
             pltpu.VMEM((16 * BLOCKS, width), BF16),
             pltpu.VMEM((16, width), BF16),
             pltpu.SemaphoreType.DMA((3,)),
         ],
+        compiler_params=params(8),
         name="finish",
-    )(spot, packet, got, smalls, mine, got_share)
-    return up, down, scale, shift, smalls
+    )(sec, place, packet, got, smalls, mine, got_share)
+    return (
+        taps.transpose(1, 0, 2), conv, scale[None], shift[None], up[None], upb, down[None], downb, gain
+    )
 
 
 def scattered(section, place, devices, speaker, pairs, sums0, sums1, got_sums, table_rows):
@@ -821,7 +844,20 @@
     )
     up_share = pick(first_section, own_share, got_share).reshape(width // devices, -1)
     down_share = pick(first_section, got_share, own_share).reshape(-1, width)
-    return up_share, down_share, tables[0], tables[1], smalls
+    lanes = width // devices
+    own_lanes = lax.dynamic_slice_in_dim(smalls, place * lanes, lanes, 1)
+    upb = lax.dynamic_slice_in_dim(smalls[UPB : UPB + 3].reshape(-1), place * 3 * lanes, 3 * lanes, 0)
+    return (
+        own_lanes[TAPS : TAPS + 7][None],
+        own_lanes[CONV : CONV + 1],
+        tables[0][None],
+        tables[1][None],
+        up_share[None],
+        upb[None],
+        down_share[None],
+        own_lanes[DOWNB : DOWNB + 1],
+        own_lanes[GAIN : GAIN + 1],
+    )
 
 
 def solution(mesh):
@@ -840,6 +876,7 @@
         P("section", None),
         P("section", None),
     )
+
     return jax.shard_map(
         local,
         mesh=mesh,

time: 158 us -> 146 us (0.924)
  Pallas kernels: 88.3 us -> 72.1 us
  local copies, waits for them, and re-layouts: 12.9 us -> 19.9 us
  other arithmetic: 2.05 us -> 0.01 us
    unnamed x27 -> x54, local copies, waits for them, and re-layouts: 7.37 us -> 16.2 us
    pallas_call x2 -> x1, Pallas kernels: 44.8 us -> 39.4 us  [local(): pl.pallas_call(main_body, out_shape=[small_struct, small_struct, half_str...]
    pallas_call x6, Pallas kernels: 19.4 us -> 15.3 us  [pack(): pl.pallas_call(functools.partial(pack_body, step, blocks, bases, share, i...]
    pallas_call x1, Pallas kernels: 7.81 us -> 5.15 us  [local(): pl.pallas_call(weights_body, grid_spec=pltpu.PrefetchScalarGridSpec(num_s...]
    pallas_call x1, Pallas kernels: 10.7 us -> 8.32 us  [last(): pl.pallas_call(functools.partial(last_body, first), grid_spec=pltpu.Prefe...]
    slice x2 -> x0, local copies, waits for them, and re-layouts: 2.07 us -> none  [the longest x1 1.35 us: local(): own_lanes[GAIN:GAIN + 1]]
    dynamic_update_slice x2, local copies, waits for them, and re-layouts: 2.08 us -> 3.73 us  [joined(): lax.dynamic_update_slice(whole, got, ((1 - section) * half, 0, 0))[None]]
    pallas_call x1, Pallas kernels: 3.15 us -> 1.52 us  [halved(): pl.pallas_call(finish_body, out_shape=[struct((owned, width), F32), struc...]
  transfers between devices with their start and end apart: 15 -> 15, of which waited for: 8 -> 8; matrix products, arithmetic and copies ran while one was open for 3% -> 3% of each run, Pallas kernels for 22% -> 16%
where the time goes in v2:
time: 146 us
  Pallas kernels  72.1 us (49%)
  waiting for transfers between devices  37.9 us (26%)
  local copies, waits for them, and re-layouts  19.9 us (14%)
  starting transfers between devices  14.5 us (10%)
    pallas_call x1, Pallas kernels, local(): pl.pallas_call(main_body, out_shape=[small_struct, small_struct, half_str...  39.4 us
    ppermute x6, waiting for transfers between devices, exchanged(): return lax.ppermute(packet, PAIR, moves)  30.9 us
    unnamed x54, local copies, waits for them, and re-layouts  16.2 us
    pallas_call x6, Pallas kernels, pack(): pl.pallas_call(functools.partial(pack_body, step, blocks, bases, share, i...  15.3 us
    ppermute x6, starting transfers between devices, exchanged(): return lax.ppermute(packet, PAIR, moves)  12.3 us
    pallas_call x1, Pallas kernels, last(): pl.pallas_call(functools.partial(last_body, first), grid_spec=pltpu.Prefe...  8.32 us
    pallas_call x1, Pallas kernels, local(): pl.pallas_call(weights_body, grid_spec=pltpu.PrefetchScalarGridSpec(num_s...  5.15 us
    dynamic_update_slice x2, local copies, waits for them, and re-layouts, joined(): lax.dynamic_update_slice(whole, got, ((1 - section) * half, 0, 0))[None]  3.73 us
  transfers between devices with their start and end apart: 15, of which 8 were waited for; matrix products, arithmetic and copies ran while one was open for 3% of the time, Pallas kernels for 16%

profile of v2, /device:TPU:0, one launch (start us, length us, event | category | flops | bytes accessed | tf_op | source)
XLA Modules:
  0.0 145.5 jit_solution(15632967796476147950)
XLA Ops:
  0.6 0.6 collective-permute-start.1
  1.2 0.1 collective-permute-start.2
  1.3 2.4 %prep.1 = (f32[24,512]{1,0:T(8,128)}, f32[24,512]{1,0:T(8,128)}) custom-call(s32[1]{0:T(128)} %bitcast.sec, s32[8]{0:T(128)} %speaker.13, f32[7,1,512]{2,1,0:T(1,128)} %bitcast.33, f32[1,512]{1,0:T(1,128)} %conv.1, f32[1,1536]{1,0:T(1,128)} %upb.1, f32[1,512]{1,0:T(1,128)} %downb.1, f32[1,512]{1,0:T(1,128)} %gain.1, f32[1,2560,512]{2,1,0:T(8,128)} %scale_hbm.1, ...), custom_call_target="tpu_custom_call" | custom-call | tf_op jit(solution)/shard_map/prep/pallas_call | solution.py:560
  3.7 0.5 collective-permute-start
  4.2 2.5 %collective-permute-done.got_small = f32[24,512]{1,0:T(8,128)S(1)} collective-permute-done((f32[24,512]{1,0:T(8,128)}, f32[24,512]{1,0:T(8,128)S(1)}, u32[]{:S(2)}, u32[]{:S(2)}) %collective-permute-start) | collective-permute-done | bytes 49184 | tf_op jit(solution)/shard_map/ppermute | solution.py:571
  6.8 1.1 copy-done.12
  7.9 1.2 copy-done.26
  9.1 1.4 copy-done.10
  10.5 1.4 copy-done.13
  11.9 0.8 copy-done.15
  12.7 39.4 %main.1 = (f32[24,512]{1,0:T(8,128)S(1)}, f32[24,512]{1,0:T(8,128)S(1)}, bf16[4,256,512]{2,1,0:T(8,128)(2,1)S(1)}, bf16[1024,512]{1,0:T(8,128)(2,1)S(1)}, bf16[1...) custom-call(s32[1]{0:T(128)} %bitcast.sec, ...), custom_call_target="tpu_custom_call" | custom-call | flops 14495514624 | bytes 25165824 | tf_op jit(solution)/shard_map/main/pallas_call | solution.py:594
  52.2 2.6 %copy-done.17 = bf16[3,1024,512]{2,1,0:T(8,128)(2,1)S(1)} copy-done((bf16[3,1024,512]{2,1,0:T(8,128)(2,1)S(1)}, bf16[3,1024,512]{2,1,0:T(8,128)(2,1)}, u32[]{:S(2)}) %copy-start.17) | copy-done | bytes 3145752
  54.9 1.9 %copy-done.19 = bf16[3,1024,512]{2,1,0:T(8,128)(2,1)S(1)} copy-done((bf16[3,1024,512]{2,1,0:T(8,128)(2,1)S(1)}, bf16[3,1024,512]{2,1,0:T(8,128)(2,1)}, u32[]{:S(2)}) %copy-start.19) | copy-done | bytes 3145752
  56.7 5.1 %weights.1 = (bf16[16,96,512]{2,1,0:T(8,128)(2,1)S(1)}, bf16[16,96,512]{2,1,0:T(8,128)(2,1)}) custom-call(s32[1]{0:T(128)} %bitcast.sec, bf16[1024,512]{1,0:T(8,128)(2,1)S(1)} %get-tuple-element.63.gb, bf16[1024,512]{1,0:T(8,128)(2,1)S(1)} %get-tuple-element.64.adapted, bf16[3,1024,512]{2,1,0:T(8,128)(2,1)S(1)} %copy-done.19, ...), custom_call_target="tpu_custom_call" | custom-call | flops 3221225472 | bytes 12582912 | tf_op jit(solution)/shard_map/weights/pallas_call | solution.py:640
  61.9 1.2 copy-done
  63.1 0.4 collective-permute-start.5
  63.5 0.1 collective-permute-start.7
  63.6 3.2 %collective-permute-done.5 = bf16[16,96,512]{2,1,0:T(8,128)(2,1)} collective-permute-done((bf16[16,96,512]{2,1,0:T(8,128)(2,1)}, bf16[16,96,512]{2,1,0:T(8,128)(2,1)}, u32[]{:S(2)}, u32[]{:S(2)}) %collective-permute-start.5) | collective-permute-done | bytes 1572896 | tf_op jit(solution)/shard_map/ppermute | solution.py:658
  66.9 1.4 copy-done.1
  68.3 2.3 %shard_map.212 = bf16[768,512]{1,0:T(8,128)(2,1)S(1)} custom-call(s32[1]{0:T(128)} %bitcast.sec, s32[1]{0:T(128)} %bitcast.8.place, s32[8]{0:T(128)S(1)} %copy-done.8, bf16[1536,512]{1,0:T(8,128)(2,1)S(1)} %bitcast.25, bf16[1536,512]{1,0:T(8,128)(2,1)} %bitcast.10.refs_1_), custom_call_target="tpu_custom_call" | custom-call | bytes 4194304 | tf_op jit(solution)/shard_map/pallas_call | solution.py:746
  70.6 0.0 copy-start.9
  70.6 0.0 copy-start.11
  70.6 2.9 %collective-permute-start.6 = (bf16[768,512]{1,0:T(8,128)(2,1)S(1)}, bf16[768,512]{1,0:T(8,128)(2,1)S(1)}, u32[]{:S(2)}, u32[]{:S(2)}) collective-permute-start(bf16[768,512]{1,0:T(8,128)(2,1)S(1)} %shard_map.212), channel_id=1, source_target_pairs={{0,1},{1,0},{2,3},{3,2},{4,5},{5,4},{6,7},{7,6},{8,9},{9,8},{10,11... | collective-permute-start | bytes 2359304 | tf_op jit(solution)/shard_map/ppermute | solution.py:719
  73.5 2.0 %shard_map.213 = bf16[768,512]{1,0:T(8,128)(2,1)S(1)} custom-call(s32[1]{0:T(128)} %bitcast.sec, s32[1]{0:T(128)} %bitcast.8.place, s32[8]{0:T(128)S(1)} %copy-done.8, bf16[1536,512]{1,0:T(8,128)(2,1)S(1)} %bitcast.20, bf16[1536,512]{1,0:T(8,128)(2,1)} %bitcast.12.refs_1_.refs_4_.refs_5_.refs_6_.refs_7_), custom_call_target="tpu_custom_call" | custom-call | bytes 4194304 | tf_op jit(solution)/shard_map/pallas_call | solution.py:746
  75.5 0.4 collective-permute-start.8
  76.0 1.9 %copy-done.18 = bf16[3,1024,512]{2,1,0:T(8,128)(2,1)S(1)} copy-done((bf16[3,1024,512]{2,1,0:T(8,128)(2,1)S(1)}, bf16[3,1024,512]{2,1,0:T(8,128)(2,1)}, u32[]{:S(2)}) %copy-start.18) | copy-done | bytes 3145752
  77.9 8.3 %last.1 = (bf16[8,256,512]{2,1,0:T(8,128)(2,1)}, bf16[4,256,512]{2,1,0:T(8,128)(2,1)}, f32[24,512]{1,0:T(8,128)S(1)}) custom-call(s32[1]{0:T(128)} %bitcast.sec, bf16[3,1024,512]{2,1,0:T(8,128)(2,1)S(1)} %copy-done.18, bf16[512,1536]{1,0:T(8,128)(2,1)S(1)} %bitcast.32, bf16[512,1536]{1,0:T(8,128)(2,1)S(1)} %copy-done.14, bf16[1024,512]{1,0:T(8,128)(2,1)S(1)} %copy-done.23, ...), custom_call_target="tpu_custom_call" | custom-call | flops 12884901888 | bytes 12582912 | tf_op jit(solution)/shard_map/last/pallas_call | solution.py:664
  86.2 0.1 collective-permute-start.9
  86.3 1.2 collective-permute-done.9.refs_8_
  87.5 4.4 %collective-permute-done.8.refs_5_.refs_6_.refs_7_.refs_8_ = bf16[768,512]{1,0:T(8,128)(2,1)S(1)} collective-permute-done((bf16[768,512]{1,0:T(8,128)(2,1)S(1)}, bf16[768,512]{1,0:T(8,128)(2,1)S(1)}, u32[]{:S(2)}, u32[]{:S(2)}) %collective-permute-start.8) | collective-permute-done | bytes 786464 | tf_op jit(solution)/shard_map/ppermute | solution.py:719
  91.9 2.4 %shard_map.214 = (bf16[800,512]{1,0:T(8,128)(2,1)S(1)}, f32[16,512]{1,0:T(8,128)S(1)}) custom-call(s32[1]{0:T(128)} %bitcast.sec, s32[1]{0:T(128)} %bitcast.8.place, s32[8]{0:T(128)S(1)} %copy-done.8, bf16[1536,512]{1,0:T(8,128)(2,1)S(1)} %bitcast.26, bf16[1536,512]{1,0:T(8,128)(2,1)} %bitcast.10.refs_1_, ...), custom_call_target="tpu_custom_call" | custom-call | bytes 4194304 | tf_op jit(solution)/shard_map/pallas_call | solution.py:746
  94.3 2.1 %collective-permute-start.10 = (bf16[800,512]{1,0:T(8,128)(2,1)S(1)}, bf16[800,512]{1,0:T(8,128)(2,1)S(1)}, u32[]{:S(2)}, u32[]{:S(2)}) collective-permute-start(bf16[800,512]{1,0:T(8,128)(2,1)S(1)} %get-tuple-element.72.refs_8_), channel_id=1, source_target_pairs={{0,2},{1,3},{2,0},{3,1},{4,6},{5,7},{6,4},{7,5},{8,10},{9,11},{10,... | collective-permute-start | bytes 2457608 | tf_op jit(solution)/shard_map/ppermute | solution.py:719
  96.4 0.5 collective-permute-start.4
  96.9 9.8 %collective-permute-done.10.refs_3_.refs_7_.refs_9_.refs_8_ = bf16[800,512]{1,0:T(8,128)(2,1)S(1)} collective-permute-done((bf16[800,512]{1,0:T(8,128)(2,1)S(1)}, bf16[800,512]{1,0:T(8,128)(2,1)S(1)}, u32[]{:S(2)}, u32[]{:S(2)}) %collective-permute-start.10) | collective-permute-done | bytes 819232 | tf_op jit(solution)/shard_map/ppermute | solution.py:719
  106.7 2.7 %shard_map.215 = (bf16[432,512]{1,0:T(8,128)(2,1)S(1)}, f32[16,512]{1,0:T(8,128)S(1)}) custom-call(s32[1]{0:T(128)} %bitcast.sec, s32[1]{0:T(128)} %bitcast.8.place, s32[8]{0:T(128)S(1)} %copy-done.8, bf16[1536,512]{1,0:T(8,128)(2,1)S(1)} %bitcast.27, bf16[1536,512]{1,0:T(8,128)(2,1)} %bitcast.10.refs_1_, ...), custom_call_target="tpu_custom_call" | custom-call | bytes 4194304 | tf_op jit(solution)/shard_map/pallas_call | solution.py:746
  109.5 2.1 %collective-permute-start.11 = (bf16[432,512]{1,0:T(8,128)(2,1)S(1)}, bf16[432,512]{1,0:T(8,128)(2,1)S(1)}, u32[]{:S(2)}, u32[]{:S(2)}) collective-permute-start(bf16[432,512]{1,0:T(8,128)(2,1)S(1)} %get-tuple-element.74.refs_10_), channel_id=1, source_target_pairs={{0,4},{1,5},{2,6},{3,7},{4,0},{5,1},{6,2},{7,3},{8,12},{9,13},{10,... | collective-permute-start | bytes 1327112 | tf_op jit(solution)/shard_map/ppermute | solution.py:719
  111.6 6.3 %collective-permute-done.11.refs_4_.refs_9_.refs_11_.refs_10_ = bf16[432,512]{1,0:T(8,128)(2,1)S(1)} collective-permute-done((bf16[432,512]{1,0:T(8,128)(2,1)S(1)}, bf16[432,512]{1,0:T(8,128)(2,1)S(1)}, u32[]{:S(2)}, u32[]{:S(2)}) %collective-permute-start.11) | collective-permute-done | bytes 442400 | tf_op jit(solution)/shard_map/ppermute | solution.py:719
  117.9 3.0 %shard_map.216 = (bf16[272,512]{1,0:T(8,128)(2,1)}, f32[16,512]{1,0:T(8,128)S(1)}) custom-call(s32[1]{0:T(128)} %bitcast.sec, s32[1]{0:T(128)} %bitcast.8.place, s32[8]{0:T(128)S(1)} %copy-done.8, bf16[1536,512]{1,0:T(8,128)(2,1)S(1)} %bitcast.28, bf16[1536,512]{1,0:T(8,128)(2,1)} %bitcast.10.refs_1_, bf16[768,512]{1,0:T(8,128)(2,1)S(1)} %collective-permute-done.6.refs_2_, ...), custom_call_target="tpu_custom_call" | custom-call | bytes 4194304 | tf_op jit(solution)/shard_map/pallas_call | solution.py:746
  120.9 3.1 %collective-permute-start.12 = (bf16[272,512]{1,0:T(8,128)(2,1)}, bf16[272,512]{1,0:T(8,128)(2,1)S(1)}, u32[]{:S(2)}, u32[]{:S(2)}) collective-permute-start(bf16[272,512]{1,0:T(8,128)(2,1)} %get-tuple-element.76.refs_12_), channel_id=1, source_target_pairs={{0,8},{1,9},{2,10},{3,11},{4,12},{5,13},{6,14},{7,15},{8,0},{9,1},... | collective-permute-start | bytes 835592 | tf_op jit(solution)/shard_map/ppermute | solution.py:719
  124.0 2.4 %bitcast_dynamic-update-slice_fusion.1 = bf16[1,8,256,512]{3,2,1,0:T(8,128)(2,1)} fusion(bf16[1,8,256,512]{3,2,1,0:T(8,128)(2,1)} %bitcast.34, s32[]{:T(128)S(6)} %select_n.12, bf16[4,256,512]{2,1,0:T(8,128)(2,1)} %collective-permute-done.3), kind=kLoop, calls=%fused_computation.1 | loop fusion | bytes 2097156 | tf_op jit(solution)/shard_map/dynamic_update_slice | solution.py:700
  126.5 8.2 %collective-permute-done.12.refs_5_.refs_11_.refs_13_ = bf16[272,512]{1,0:T(8,128)(2,1)S(1)} collective-permute-done((bf16[272,512]{1,0:T(8,128)(2,1)}, bf16[272,512]{1,0:T(8,128)(2,1)S(1)}, u32[]{:S(2)}, u32[]{:S(2)}) %collective-permute-start.12) | collective-permute-done | bytes 278560 | tf_op jit(solution)/shard_map/ppermute | solution.py:719
  134.6 1.1 copy-done.5
  135.8 2.9 %shard_map.217 = (bf16[144,512]{1,0:T(8,128)(2,1)S(1)}, f32[16,512]{1,0:T(8,128)S(1)}, f32[96,512]{1,0:T(8,128)S(1)}, f32[96,512]{1,0:T(8,128)S(1)}) custom-call(s32[1]{0:T(128)} %bitcast.sec, s32[1]{0:T(128)} %bitcast.8.place, s32[8]{0:T(128)S(1)} %copy-done.8, bf16[1536,512]{1,0:T(8,128)(2,1)S(1)} %bitcast.29, bf16[1536,512]{1,0:T(8,128)(2,1)} %bitcast.10.refs_1_, ...), custom_call_target="tpu_custom_call" | custom-call | bytes 4194304 | tf_op jit(solution)/shard_map/pallas_call | solution.py:746
  138.6 1.6 %collective-permute-start.13 = (bf16[144,512]{1,0:T(8,128)(2,1)S(1)}, bf16[144,512]{1,0:T(8,128)(2,1)S(1)}, u32[]{:S(2)}, u32[]{:S(2)}) collective-permute-start(bf16[144,512]{1,0:T(8,128)(2,1)S(1)} %get-tuple-element.78.before), channel_id=1, source_target_pairs={{0,1},{1,0},{2,3},{3,2},{4,5},{5,4},{6,7},{7,6},{8,9},{9,8},{10,11... | collective-permute-start | bytes 442376 | tf_op jit(solution)/shard_map/ppermute | solution.py:719
  140.3 1.3 bitcast_dynamic-update-slice_fusion
  141.6 0.0 copy-start.25
  141.6 2.2 %collective-permute-done.13.after = bf16[144,512]{1,0:T(8,128)(2,1)S(1)} collective-permute-done((bf16[144,512]{1,0:T(8,128)(2,1)S(1)}, bf16[144,512]{1,0:T(8,128)(2,1)S(1)}, u32[]{:S(2)}, u32[]{:S(2)}) %collective-permute-start.13) | collective-permute-done | bytes 147488 | tf_op jit(solution)/shard_map/ppermute | solution.py:719
  143.9 1.5 %finish.1 = (f32[160,512]{1,0:T(8,128)}, f32[160,512]{1,0:T(8,128)}, f32[32,1536]{1,0:T(8,128)}, f32[96,512]{1,0:T(8,128)}, f32[7,1,32]{2,1,0:T(1,128)}, /*index...) custom-call(s32[1]{0:T(128)} %bitcast.sec, s32[1]{0:T(128)} %bitcast.8.place, ...), custom_call_target="tpu_custom_call" | custom-call | tf_op jit(solution)/shard_map/finish/pallas_call | solution.py:781
  (50 shorter events, 0.1 us)
Async XLA Ops:
  0.6 6.1 %collective-permute-start.1 = (bf16[512,1536]{1,0:T(8,128)(2,1)}, bf16[512,1536]{1,0:T(8,128)(2,1)S(1)}, u32[]{:S(2)}, u32[]{:S(2)}) collective-permute-start(bf16[512,1536]{1,0:T(8,128)(2,1)} %bitcast.30), channel_id=1, source_target_pairs={{0,16},{16,0},{1,17},{17,1},{2,18},{18,2},{3,19},{19,3},{4,20},{20... | collective-permute-start | bytes 4718600 | tf_op jit(solution)/shard_map/ppermute | solution.py:573
  1.2 6.7 %collective-permute-start.2 = (bf16[1536,512]{1,0:T(8,128)(2,1)}, bf16[1536,512]{1,0:T(8,128)(2,1)S(1)}, u32[]{:S(2)}, u32[]{:S(2)}) collective-permute-start(bf16[1536,512]{1,0:T(8,128)(2,1)} %bitcast.36), channel_id=1, source_target_pairs={{0,16},{16,0},{1,17},{17,1},{2,18},{18,2},{3,19},{19,3},{4,20},{20... | collective-permute-start | bytes 4718600 | tf_op jit(solution)/shard_map/ppermute | solution.py:574
  1.3 7.8 %copy-start.16 = (s32[8]{0:T(128)S(1)}, s32[8]{0:T(128)}, u32[]{:S(2)}) copy-start(s32[8]{0:T(128)} %valid.1) | copy-start | bytes 100
  3.7 3.0 %collective-permute-start = (f32[24,512]{1,0:T(8,128)}, f32[24,512]{1,0:T(8,128)S(1)}, u32[]{:S(2)}, u32[]{:S(2)}) collective-permute-start(f32[24,512]{1,0:T(8,128)} %get-tuple-element.52), channel_id=1, source_target_pairs={{0,16},{16,0},{1,17},{17,1},{2,18},{18,2},{3,19},{19,3},{4,20},{20... | collective-permute-start | bytes 147464 | tf_op jit(solution)/shard_map/ppermute | solution.py:571
  6.8 1.1 copy-start.12
  7.9 1.2 copy-start.26
  9.1 1.4 copy-start.10
  10.5 1.4 copy-start.13
  11.9 0.8 copy-start.15
  52.2 9.7 %copy-start.20 = (bf16[4,256,512]{2,1,0:T(8,128)(2,1)}, bf16[4,256,512]{2,1,0:T(8,128)(2,1)S(1)}, u32[]{:S(2)}) copy-start(bf16[4,256,512]{2,1,0:T(8,128)(2,1)S(1)} %get-tuple-element.59.grad_out) | copy-start | bytes 3145732
  52.2 9.7 %copy-start.22 = (bf16[1024,512]{1,0:T(8,128)(2,1)}, bf16[1024,512]{1,0:T(8,128)(2,1)S(1)}, u32[]{:S(2)}) copy-start(bf16[1024,512]{1,0:T(8,128)(2,1)S(1)} %get-tuple-element.56.normed) | copy-start | bytes 3145732
  52.2 2.6 %copy-start.17 = (bf16[3,1024,512]{2,1,0:T(8,128)(2,1)S(1)}, bf16[3,1024,512]{2,1,0:T(8,128)(2,1)}, u32[]{:S(2)}) copy-start(bf16[3,1024,512]{2,1,0:T(8,128)(2,1)} %get-tuple-element.55.gpre) | copy-start | bytes 9437188
  54.9 1.9 %copy-start.19 = (bf16[3,1024,512]{2,1,0:T(8,128)(2,1)S(1)}, bf16[3,1024,512]{2,1,0:T(8,128)(2,1)}, u32[]{:S(2)}) copy-start(bf16[3,1024,512]{2,1,0:T(8,128)(2,1)} %get-tuple-element.65.act) | copy-start | bytes 9437188
  56.7 10.1 %copy-start.8 = (s32[8]{0:T(128)S(1)}, s32[8]{0:T(128)}, u32[]{:S(2)}) copy-start(s32[8]{0:T(128)} %speaker.13) | copy-start | bytes 100
  61.9 1.2 copy-start
  63.1 3.8 %collective-permute-start.5 = (bf16[16,96,512]{2,1,0:T(8,128)(2,1)}, bf16[16,96,512]{2,1,0:T(8,128)(2,1)}, u32[]{:S(2)}, u32[]{:S(2)}) collective-permute-start(bf16[16,96,512]{2,1,0:T(8,128)(2,1)} %get-tuple-element.67), channel_id=1, source_target_pairs={{0,16},{16,0},{1,17},{17,1},{2,18},{18,2},{3,19},{19,3},{4,20},{20... | collective-permute-start | bytes 4718600 | tf_op jit(solution)/shard_map/ppermute | solution.py:658
  63.5 10.0 %collective-permute-start.7 = (bf16[16,96,512]{2,1,0:T(8,128)(2,1)}, bf16[16,96,512]{2,1,0:T(8,128)(2,1)}, u32[]{:S(2)}, u32[]{:S(2)}) collective-permute-start(bf16[16,96,512]{2,1,0:T(8,128)(2,1)} %get-tuple-element.69), channel_id=1, source_target_pairs={{0,16},{16,0},{1,17},{17,1},{2,18},{18,2},{3,19},{19,3},{4,20},{20... | collective-permute-start | bytes 4718600 | tf_op jit(solution)/shard_map/ppermute | solution.py:636
  66.9 1.4 copy-start.1
  68.3 7.7 %copy-start.14 = (bf16[512,1536]{1,0:T(8,128)(2,1)S(1)}, bf16[512,1536]{1,0:T(8,128)(2,1)}, u32[]{:S(2)}) copy-start(bf16[512,1536]{1,0:T(8,128)(2,1)} %copy-done.12) | copy-start | bytes 4718596
  68.3 7.7 %copy-start.21 = (bf16[4,256,512]{2,1,0:T(8,128)(2,1)S(1)}, bf16[4,256,512]{2,1,0:T(8,128)(2,1)}, u32[]{:S(2)}) copy-start(bf16[4,256,512]{2,1,0:T(8,128)(2,1)} %copy-done.20) | copy-start | bytes 3145732
  68.3 7.7 %copy-start.23 = (bf16[1024,512]{1,0:T(8,128)(2,1)S(1)}, bf16[1024,512]{1,0:T(8,128)(2,1)}, u32[]{:S(2)}) copy-start(bf16[1024,512]{1,0:T(8,128)(2,1)} %copy-done.22) | copy-start | bytes 3145732
  70.6 5.4 %copy-start.9 = (bf16[8,256,512]{2,1,0:T(8,128)(2,1)S(1)}, bf16[8,256,512]{2,1,0:T(8,128)(2,1)}, u32[]{:S(2)}) copy-start(bf16[8,256,512]{2,1,0:T(8,128)(2,1)} %tokens.3) | copy-start | bytes 6291460
  70.6 5.4 %copy-start.11 = (bf16[1,512,1536]{2,1,0:T(8,128)(2,1)S(1)}, bf16[1,512,1536]{2,1,0:T(8,128)(2,1)}, u32[]{:S(2)}) copy-start(bf16[1,512,1536]{2,1,0:T(8,128)(2,1)} %param.21) | copy-start | bytes 4718596
  70.6 16.9 %collective-permute-start.6 = (bf16[768,512]{1,0:T(8,128)(2,1)S(1)}, bf16[768,512]{1,0:T(8,128)(2,1)S(1)}, u32[]{:S(2)}, u32[]{:S(2)}) collective-permute-start(bf16[768,512]{1,0:T(8,128)(2,1)S(1)} %shard_map.212), channel_id=1, source_target_pairs={{0,1},{1,0},{2,3},{3,2},{4,5},{5,4},{6,7},{7,6},{8,9},{9,8},{10,11... | collective-permute-start | bytes 2359304 | tf_op jit(solution)/shard_map/ppermute | solution.py:719
  75.5 16.4 %collective-permute-start.8 = (bf16[768,512]{1,0:T(8,128)(2,1)S(1)}, bf16[768,512]{1,0:T(8,128)(2,1)S(1)}, u32[]{:S(2)}, u32[]{:S(2)}) collective-permute-start(bf16[768,512]{1,0:T(8,128)(2,1)S(1)} %shard_map.213), channel_id=1, source_target_pairs={{0,1},{1,0},{2,3},{3,2},{4,5},{5,4},{6,7},{7,6},{8,9},{9,8},{10,11... | collective-permute-start | bytes 2359304 | tf_op jit(solution)/shard_map/ppermute | solution.py:719
  76.0 1.9 %copy-start.18 = (bf16[3,1024,512]{2,1,0:T(8,128)(2,1)S(1)}, bf16[3,1024,512]{2,1,0:T(8,128)(2,1)}, u32[]{:S(2)}) copy-start(bf16[3,1024,512]{2,1,0:T(8,128)(2,1)} %get-tuple-element.55.gpre) | copy-start | bytes 9437188
  77.9 14.0 %copy-start.2 = (bf16[16,96,512]{2,1,0:T(8,128)(2,1)S(1)}, bf16[16,96,512]{2,1,0:T(8,128)(2,1)}, u32[]{:S(2)}) copy-start(bf16[16,96,512]{2,1,0:T(8,128)(2,1)} %copy-done) | copy-start | bytes 4718596
  86.2 1.3 collective-permute-start.9
  91.9 26.0 %copy-start.4 = (bf16[768,512]{1,0:T(8,128)(2,1)}, bf16[768,512]{1,0:T(8,128)(2,1)S(1)}, u32[]{:S(2)}) copy-start(bf16[768,512]{1,0:T(8,128)(2,1)S(1)} %collective-permute-done.8.refs_5_.refs_6_.refs_7_.refs_8_) | copy-start | bytes 2359300
  94.3 12.4 %collective-permute-start.10 = (bf16[800,512]{1,0:T(8,128)(2,1)S(1)}, bf16[800,512]{1,0:T(8,128)(2,1)S(1)}, u32[]{:S(2)}, u32[]{:S(2)}) collective-permute-start(bf16[800,512]{1,0:T(8,128)(2,1)S(1)} %get-tuple-element.72.refs_8_), channel_id=1, source_target_pairs={{0,2},{1,3},{2,0},{3,1},{4,6},{5,7},{6,4},{7,5},{8,10},{9,11},{10,... | collective-permute-start | bytes 2457608 | tf_op jit(solution)/shard_map/ppermute | solution.py:719
  96.4 27.6 %collective-permute-start.3 = (bf16[4,256,512]{2,1,0:T(8,128)(2,1)}, bf16[4,256,512]{2,1,0:T(8,128)(2,1)}, u32[]{:S(2)}, u32[]{:S(2)}) collective-permute-start(bf16[4,256,512]{2,1,0:T(8,128)(2,1)} %get-tuple-element.54), channel_id=1, source_target_pairs={{0,16},{16,0},{1,17},{17,1},{2,18},{18,2},{3,19},{19,3},{4,20},{20... | collective-permute-start | bytes 3145736 | tf_op jit(solution)/shard_map/ppermute | solution.py:637
  96.4 43.9 %collective-permute-start.4 = (bf16[4,256,512]{2,1,0:T(8,128)(2,1)}, bf16[4,256,512]{2,1,0:T(8,128)(2,1)}, u32[]{:S(2)}, u32[]{:S(2)}) collective-permute-start(bf16[4,256,512]{2,1,0:T(8,128)(2,1)} %get-tuple-element.62), channel_id=1, source_target_pairs={{0,16},{16,0},{1,17},{17,1},{2,18},{18,2},{3,19},{19,3},{4,20},{20... | collective-permute-start | bytes 3145736 | tf_op jit(solution)/shard_map/ppermute | solution.py:696
  109.5 8.4 %collective-permute-start.11 = (bf16[432,512]{1,0:T(8,128)(2,1)S(1)}, bf16[432,512]{1,0:T(8,128)(2,1)S(1)}, u32[]{:S(2)}, u32[]{:S(2)}) collective-permute-start(bf16[432,512]{1,0:T(8,128)(2,1)S(1)} %get-tuple-element.74.refs_10_), channel_id=1, source_target_pairs={{0,4},{1,5},{2,6},{3,7},{4,0},{5,1},{6,2},{7,3},{8,12},{9,13},{10,... | collective-permute-start | bytes 1327112 | tf_op jit(solution)/shard_map/ppermute | solution.py:719
  117.9 3.0 %copy-start.6 = (bf16[432,512]{1,0:T(8,128)(2,1)}, bf16[432,512]{1,0:T(8,128)(2,1)S(1)}, u32[]{:S(2)}) copy-start(bf16[432,512]{1,0:T(8,128)(2,1)S(1)} %collective-permute-done.11.refs_4_.refs_9_.refs_11_.refs_10_) | copy-start | bytes 1327108
  120.9 13.7 %collective-permute-start.12 = (bf16[272,512]{1,0:T(8,128)(2,1)}, bf16[272,512]{1,0:T(8,128)(2,1)S(1)}, u32[]{:S(2)}, u32[]{:S(2)}) collective-permute-start(bf16[272,512]{1,0:T(8,128)(2,1)} %get-tuple-element.76.refs_12_), channel_id=1, source_target_pairs={{0,8},{1,9},{2,10},{3,11},{4,12},{5,13},{6,14},{7,15},{8,0},{9,1},... | collective-permute-start | bytes 835592 | tf_op jit(solution)/shard_map/ppermute | solution.py:719
  124.0 10.6 %copy-start.3 = (bf16[16,96,512]{2,1,0:T(8,128)(2,1)S(1)}, bf16[16,96,512]{2,1,0:T(8,128)(2,1)}, u32[]{:S(2)}) copy-start(bf16[16,96,512]{2,1,0:T(8,128)(2,1)} %copy-done) | copy-start | bytes 4718596
  124.0 10.6 %copy-start.7 = (bf16[432,512]{1,0:T(8,128)(2,1)S(1)}, bf16[432,512]{1,0:T(8,128)(2,1)}, u32[]{:S(2)}) copy-start(bf16[432,512]{1,0:T(8,128)(2,1)} %copy-done.6) | copy-start | bytes 1327108
  134.6 1.1 copy-start.5
  135.8 4.5 %copy-start.24 = (bf16[8,256,512]{2,1,0:T(8,128)(2,1)S(1)}, bf16[8,256,512]{2,1,0:T(8,128)(2,1)}, u32[]{:S(2)}) copy-start(bf16[8,256,512]{2,1,0:T(8,128)(2,1)} %get-tuple-element.61) | copy-start | bytes 6291460
  138.6 5.2 %collective-permute-start.13 = (bf16[144,512]{1,0:T(8,128)(2,1)S(1)}, bf16[144,512]{1,0:T(8,128)(2,1)S(1)}, u32[]{:S(2)}, u32[]{:S(2)}) collective-permute-start(bf16[144,512]{1,0:T(8,128)(2,1)S(1)} %get-tuple-element.78.before), channel_id=1, source_target_pairs={{0,1},{1,0},{2,3},{3,2},{4,5},{5,4},{6,7},{7,6},{8,9},{9,8},{10,11... | collective-permute-start | bytes 442376 | tf_op jit(solution)/shard_map/ppermute | solution.py:719
  140.3 3.6 %collective-permute-start.14 = (f32[96,512]{1,0:T(8,128)S(1)}, f32[96,512]{1,0:T(8,128)S(1)}, u32[]{:S(2)}, u32[]{:S(2)}) collective-permute-start(f32[96,512]{1,0:T(8,128)S(1)} %get-tuple-element.81), channel_id=1, source_target_pairs={{0,16},{16,0},{1,17},{17,1},{2,18},{18,2},{3,19},{19,3},{4,20},{20... | collective-permute-start | bytes 589832 | tf_op jit(solution)/shard_map/ppermute | solution.py:776
  141.6 3.8 %copy-start.25 = (bf16[1,8,256,512]{3,2,1,0:T(8,128)(2,1)}, bf16[1,8,256,512]{3,2,1,0:T(8,128)(2,1)S(1)}, u32[]{:S(2)}) copy-start(bf16[1,8,256,512]{3,2,1,0:T(8,128)(2,1)S(1)} %bitcast_dynamic-update-slice_fusion) | copy-start | bytes 6291460

commit v3 on v2

--- a/solution.py
+++ b/solution.py
@@ -12,11 +12,13 @@
 BF16 = jnp.bfloat16
 PAIR = ("section", "dp")
 TILE = 512
+LAST_MIB = 48
 HALF_ROOT = 0.7071067811865476
 DENSITY = 0.3989422804014327
 BLOCKS = 16
 ORDERS = ((0, 1, 2, 3), (2, 0, 1, 3))
 ANY = pl.BlockSpec(memory_space=pl.ANY)
+HBM = pl.BlockSpec(memory_space=pltpu.HBM)
 VMEM = pl.BlockSpec(memory_space=pltpu.VMEM)
 SMEM = pl.BlockSpec(memory_space=pltpu.SMEM)
 
@@ -39,14 +41,21 @@
 TN = ((0,), (0,))
 
 
-def shifted(x, offset):
-    if offset == 0:
-        return x
+OFFSETS = (-3, -2, -1, 1, 2, 3)
+
+
+def set_shifts(shifts):
+    frames = shifts.shape[1]
+    row = lax.broadcasted_iota(jnp.int32, (frames, frames), 0)
+    col = lax.broadcasted_iota(jnp.int32, (frames, frames), 1)
+    for n, offset in enumerate(OFFSETS):
+        shifts[n * frames : (n + 1) * frames] = jnp.where(col == row + offset, 1.0, 0.0).astype(BF16)
+
+
+def shifted(shifts, x, offset):
     frames = x.shape[0]
-    rows = lax.broadcasted_iota(jnp.int32, (frames, 1), 0)
-    rolled = pltpu.roll(x, (-offset) % frames, 0)
-    kept = rows < frames - offset if offset > 0 else rows >= -offset
-    return jnp.where(kept, rolled, 0.0)
+    n = OFFSETS.index(offset)
+    return dot(shifts[n * frames : (n + 1) * frames], x, NN)
 
 
 def wide(x, width):
@@ -57,11 +66,10 @@
     return jnp.sum(x, axis=0, keepdims=True)
 
 
-def normalize(x, small, clip):
-    conv = small[CONV : CONV + 1] + x * small[3:4]
-    for k in range(7):
-        if k != 3:
-            conv = conv + shifted(x, k - 3) * small[k : k + 1]
+def normalize(x, small, clip, shifts):
+    conv = small[CONV : CONV + 1] + x.astype(F32) * small[3:4]
+    for offset in OFFSETS:
+        conv = conv + shifted(shifts, x, offset) * small[offset + 3 : offset + 4]
     centred = conv - jnp.mean(conv, axis=-1, keepdims=True)
     inv = lax.rsqrt(jnp.mean(centred * centred, axis=-1, keepdims=True) + 1e-06)
     normed = centred * inv
@@ -103,21 +111,24 @@
 
 
 def forward_tiles(adapted, up, down, small, act, slope, acc):
-    clips = acc.shape[0] // 256
-    for j in range(3):
-        bias = small[UPB + j : UPB + j + 1]
-        for r in range(clips):
-            rows = slice(r * 256, (r + 1) * 256)
-            pre = dot(adapted[rows], up[:, j * TILE : (j + 1) * TILE], NN) + bias
-            phi = 0.5 * lax.erf(pre * HALF_ROOT) + 0.5
-            low = (pre * phi).astype(BF16)
-            act[j, rows] = low
-            slope[j, rows] = (phi + pre * (DENSITY * jnp.exp(-0.5 * pre * pre))).astype(BF16)
-            part = dot(low, down[j * TILE : (j + 1) * TILE], NN)
-            if j == 0:
-                acc[rows] = part
-            else:
-                acc[rows] = acc[rows] + part
+    steps = [(j, r) for j in range(3) for r in range(acc.shape[0] // 256)]
+
+    def hidden(j, r):
+        part = dot(adapted[r * 256 : (r + 1) * 256], up[:, j * TILE : (j + 1) * TILE], NN)
+        return part + small[UPB + j : UPB + j + 1]
+
+    ahead = hidden(*steps[0])
+    for n, (j, r) in enumerate(steps):
+        rows = slice(r * 256, (r + 1) * 256)
+        pre = ahead
+        if n + 1 < len(steps):
+            ahead = hidden(*steps[n + 1])
+        phi = 0.5 * lax.erf(pre * HALF_ROOT) + 0.5
+        low = (pre * phi).astype(BF16)
+        act[j, rows] = low
+        slope[j, rows] = (phi + pre * (DENSITY * jnp.exp(-0.5 * pre * pre))).astype(BF16)
+        part = dot(low, down[j * TILE : (j + 1) * TILE], NN)
+        acc[rows] = part if j == 0 else acc[rows] + part
 
 
 def activation_tile(j, gb, down, slope, sums):
@@ -131,24 +142,27 @@
     sums[UPB + j : UPB + j + 1] = total
 
 
+def down_pieces(j):
+    share = 3 * TILE // BLOCKS
+    at, pieces = j * TILE, []
+    while at < (j + 1) * TILE:
+        stop = min((at // share + 1) * share, (j + 1) * TILE)
+        pieces.append((position(at // share, ORDERS[1]), at % share, stop - at, at - j * TILE))
+        at = stop
+    return pieces
+
+
 def weight_tile(j, gb, adapted, act, gpre, upd, dnd):
     gup = dot(adapted[...], gpre, TN).astype(BF16)
     share = TILE // BLOCKS
     for i in range(BLOCKS):
         upd[position(i, ORDERS[0]), j * share : (j + 1) * share] = gup[i * share : (i + 1) * share]
     gdn = dot(act, gb[...], TN).astype(BF16)
-    share = 3 * TILE // BLOCKS
-    at = j * TILE
-    while at < (j + 1) * TILE:
-        stop = min((at // share + 1) * share, (j + 1) * TILE)
-        first = at % share
-        dnd[position(at // share, ORDERS[1]), first : first + stop - at] = gdn[
-            at - j * TILE : stop - j * TILE
-        ]
-        at = stop
-
-
-def norm_backward(gad, normed, inv, small, clip, grad_out, v):
+    for block, first, rows, at in down_pieces(j):
+        dnd[block, first : first + rows] = gdn[at : at + rows]
+
+
+def norm_backward(gad, normed, inv, small, clip, grad_out, v, shifts):
     n = normed.astype(F32)
     width = n.shape[1]
     scale = small[pl.ds(SCALE + clip, 1)]
@@ -158,14 +172,18 @@
     m1 = jnp.mean(gn, axis=-1, keepdims=True)
     m2 = jnp.mean(gn * n, axis=-1, keepdims=True)
     gc = (gn - m1 - n * m2) * wide(inv, width)
-    g_conv = rowsum(gc)
-    total = grad_out
+    low = gc.astype(BF16)
+    total = grad_out + gc * small[3:4]
+    v = v.astype(F32)
     g_taps = []
     for k in range(7):
-        moved = shifted(gc, 3 - k)
+        if k == 3:
+            g_taps.append(rowsum(gc * v))
+            continue
+        moved = shifted(shifts, low, 3 - k)
         total = total + moved * small[k : k + 1]
         g_taps.append(rowsum(moved * v))
-    return total.astype(BF16), jnp.concatenate(g_taps + [g_conv], axis=0), g_scale, g_shift
+    return total.astype(BF16), jnp.concatenate(g_taps + [rowsum(gc)], axis=0), g_scale, g_shift
 
 
 def place_weights(sec, block, up_own, up_got, down_own, down_got, up, down, sems, start):
@@ -211,7 +229,7 @@
     sums0, sums1, gin1, gb0_hbm, adapted_hbm, normed_hbm, inv_hbm, out_own, out_send, act_hbm,
     gpre_hbm, keep, send, small0_out,
     up0, down0, up1, down1, act0, slope0, act1, slope1, acc, adapted0, normed, inv, adapted1, branch0,
-    gb, v, grad, out0, out1, small0, small1, upd, dnd, sems, pieces,
+    gb, v, grad, out0, out1, small0, small1, shifts, upd, dnd, sems, pieces,
 ):
     clips = acc.shape[0] // 256
     mine = pl.ds(sec[0] * clips, clips)
@@ -230,13 +248,14 @@
     small0_out[...] = small0[...]
     sums0[...] = jnp.zeros_like(sums0)
     sums1[...] = jnp.zeros_like(sums1)
+    set_shifts(shifts)
     loads[0].wait()
 
     def begin(r):
         rows = pl.ds(pl.multiple_of(r * 256, 256), 256)
-        adapted0[rows], normed[rows], inv[rows] = normalize(v[r].astype(F32), small0, r)
-
-    pl.loop(0, clips)(begin)
+        adapted0[rows], normed[rows], inv[rows] = normalize(v[r], small0, r, shifts)
+
+    pl.loop(0, clips, unroll=True)(begin)
     saves = [
         pltpu.make_async_copy(source, target, sems.at[7 + n // 2, n % 2])
         for n, (source, target) in enumerate(
@@ -257,9 +276,9 @@
         branch0[rows] = branch
         result = (v[r].astype(F32) + small0[GAIN : GAIN + 1] * branch).astype(BF16)
         out0[r] = result
-        adapted1[rows], normed[rows], inv[rows] = normalize(result.astype(F32), small1, r)
-
-    pl.loop(0, clips)(between)
+        adapted1[rows], normed[rows], inv[rows] = normalize(result, small1, r, shifts)
+
+    pl.loop(0, clips, unroll=True)(between)
     place_weights(sec, 1, *weights, up1, down1, sems.at[1], False)
     forward_tiles(adapted1, up1, down1, small1, act1, slope1, acc)
     loads[1].wait()
@@ -298,7 +317,7 @@
         rows = pl.ds(pl.multiple_of(r * 256, 256), 256)
         above = grad[r].astype(F32) * valid[sec[0] * clips + r].astype(F32)
         gin, smalls, g_scale, g_shift = norm_backward(
-            acc[rows], normed[rows], inv[rows], small1, r, above, out0[r].astype(F32)
+            acc[rows], normed[rows], inv[rows], small1, r, above, out0[r], shifts
         )
         grad[r] = gin
         sums1[TAPS : TAPS + 8] += smalls
@@ -329,22 +348,45 @@
 
 def weights_body(sec, gb, adapted, act, gpre, keep, send, upd, dnd, sems):
     step = pl.program_id(0)
+    share = TILE // BLOCKS
+
+    def copies(j, up_to, down_to):
+        part = pl.ds(j * share, share)
+        moves = [pltpu.make_async_copy(upd.at[:, part], up_to.at[:, part], sems.at[j, 0])]
+        for n, (block, first, rows, _) in enumerate(down_pieces(j)):
+            part = pl.ds(first, rows)
+            moves.append(
+                pltpu.make_async_copy(dnd.at[block, part], down_to.at[block, part], sems.at[j, 1 + n])
+            )
+        return moves
+
     for j in range(3):
 
         @pl.when(step == j)
         def _():
             weight_tile(j, gb, adapted, act[0], gpre[0], upd, dnd)
 
+            @pl.when(sec[0] == 0)
+            def _():
+                for copy in copies(j, keep, send):
+                    copy.start()
+
+            @pl.when(sec[0] != 0)
+            def _():
+                for copy in copies(j, send, keep):
+                    copy.start()
+
     @pl.when(step == 2)
     def _():
-        route(sec, upd, dnd, keep, send, sems, True)
-        route(sec, upd, dnd, keep, send, sems, False)
+        for j in range(3):
+            for copy in copies(j, keep, send):
+                copy.wait()
 
 
 def last_body(
     first, sec, gpre, up_own, up_got, normed, inv, small, grad_out, tokens, sums_in, *rest
 ):
-    gin, away, sums, up, sem = rest[-5:]
+    gin, away, sums, up, shifts, sem = rest[-6:]
     step = pl.program_id(0)
     clip = first + step
 
@@ -360,6 +402,7 @@
         def _():
             pltpu.make_async_copy(up_got, up, sem).start()
 
+        set_shifts(shifts)
         pltpu.make_async_copy(up_own, up, sem).wait()
 
     gad = dot(gpre[0], up[:, :TILE], NT)
@@ -367,7 +410,7 @@
         gad = gad + dot(gpre[j], up[:, j * TILE : (j + 1) * TILE], NT)
     above = grad_out[0]
     out, smalls, g_scale, g_shift = norm_backward(
-        gad, normed[...], inv[...], small, clip, above.astype(F32), tokens[0].astype(F32)
+        gad, normed[...], inv[...], small, clip, above.astype(F32), tokens[0], shifts
     )
     gin[0] = jnp.where(sec[0] == 0, out, above)
     away[0] = jnp.where(sec[0] == 0, above, out)
@@ -385,15 +428,6 @@
     return (spot[1] >> (low if low == high else pick(spot[0] == 0, low, high))) & 1
 
 
-def region(spot, level, step):
-    start = 0
-    for i in range(level, min(step, 4)):
-        start = start + bit_of(spot, i) * (8 >> i)
-    if step < 4:
-        start = start + (1 - bit_of(spot, step)) * (8 >> step)
-    return start
-
-
 GATHER = (1, 2, 3, 0)
 
 
@@ -409,36 +443,52 @@
     copies[-1].start()
 
 
-def add_up(buffers, rows):
-    total = buffers[0][:rows].astype(F32)
-    for buffer in buffers[1:]:
-        total = total + buffer[:rows].astype(F32)
-    return total
-
-
-def pack_body(step, blocks, bases, share, extras, sec, place, speaker, *refs):
+def split_body(share, sec, place, keep, got, packet, kept, came, sems):
+    rows = 8 * share
+    first = pl.multiple_of((1 - bit_of((sec[0], place[0]), 0)) * rows, rows)
+    pieces = 4
+    size = rows // pieces
+    copies = []
+    for n in range(pieces):
+        for m, (source, target) in enumerate(((keep, kept), (got, came))):
+            fetch(
+                copies, source, first + n * size, size, target.at[pl.ds(n * size, size)], sems.at[n, m]
+            )
+    for n in range(pieces):
+        copies[2 * n].wait()
+        copies[2 * n + 1].wait()
+        part = slice(n * size, (n + 1) * size)
+        packet[part] = (kept[part].astype(F32) + came[part].astype(F32)).astype(BF16)
+
+
+def pack_body(step, share, sec, place, speaker, total0, total1, *refs):
     spot = (sec[0], place[0])
-    levels = step + 2
-    sources = [refs[b * levels : (b + 1) * levels] for b in range(blocks)]
-    refs = refs[blocks * levels :]
-    count = 1 if step == 4 else 8 >> step
-    rows = count * share
-    extra_in, refs = refs[: 3 * extras], refs[3 * extras :]
-    packet, refs = (refs[0], refs[1:]) if step < 4 or extras else (None, refs)
-    if extras:
-        smalls_out, refs = refs[0], refs[1:]
-    if step == 4:
-        mine, away, refs = refs[0], refs[1], refs[2:]
-    buffers, tail, sems = refs
-    copies = []
-    for b in range(blocks):
-        for n in range(levels):
-            level = max(n - 1, 0)
-            base = bases[b][level]
-            first = pl.multiple_of((region(spot, level, step)) * share + base, 32)
-            fetch(copies, sources[b][n], first, rows, buffers.at[b, n], sems.at[b, n])
-    head = blocks * rows if step < 4 else 0
-    if extras and step == 1:
+    count = 8 >> step
+    rows = max(count, 1) * share
+    head = 2 * count * share
+    totals = (total0, total1)
+    if step == 1:
+        latest = [(refs[0], 0), (refs[1], 0)]
+        refs = refs[2:]
+    else:
+        latest = [(refs[0], 0), (refs[0], (16 >> step) * share)]
+    extra_in, refs = refs[:3], refs[3:]
+    packet, smalls_out = refs[:2]
+    for b in range(2):
+        source, base = latest[b]
+        if step < 4:
+            first = pl.multiple_of((1 - bit_of(spot, step)) * rows, 32)
+            away = totals[b][pl.ds(first, rows)] + source[pl.ds(base + first, rows)].astype(F32)
+            packet[b * rows : (b + 1) * rows] = away.astype(BF16)
+        else:
+            whole = totals[b][...] + source[base : base + rows].astype(F32)
+            for target, mine in ((refs[2], True), (refs[3], False)):
+
+                @pl.when((spot[0] == b) == mine)
+                def _():
+                    target[...] = whole
+
+    if step == 1:
         sums0, sums1, got = extra_in
         own = pick(spot[0] == 0, sums0[...], sums1[...])
         other = got[...]
@@ -455,49 +505,30 @@
         smalls_out[...] = own[:SCALE] + other[:SCALE]
         smalls_out[13:14] = (code >> 6).astype(F32)
         smalls_out[14:15] = (code & 63).astype(F32)
-        packet[head + 16 : head + 32] = smalls_out[...].astype(BF16)
-    elif extras:
-        before, after, smalls_in = extra_in
+        tail = head + 16
+    else:
+        after, before, smalls_in = extra_in
         size = 16 << (step - 2)
-        old_head = blocks * (8 >> (step - 1)) * share
+        old_head = (16 >> step) * 2 * share
         bit = bit_of(spot, GATHER[step - 2])
-        for n, (source, spot_bit) in enumerate(((before, bit), (after, 1 - bit))):
-            target = packet.at[pl.ds(pl.multiple_of(head + spot_bit * size, 16), size)]
-            fetch(copies, source, old_head, size, target, sems.at[2, n])
-        fetch(copies, after, old_head + size, 16, tail, sems.at[2, 2])
-    for b in range(blocks):
-        for n in range(levels):
-            copies[b * levels + n].wait()
-        total = add_up([buffers.at[b, n] for n in range(levels)], rows)
-        if step < 4:
-            packet[b * rows : (b + 1) * rows] = total.astype(BF16)
-        else:
-            @pl.when(spot[0] == b)
-            def _():
-                mine[...] = total
-
-            @pl.when(spot[0] != b)
-            def _():
-                away[...] = total
-    if extras and step > 1:
-        for copy in copies[blocks * levels :]:
-            copy.wait()
-        smalls_out[...] = smalls_in[...] + tail[...].astype(F32)
-        packet[head + 2 * size : head + 2 * size + 16] = smalls_out[...].astype(BF16)
+        for source, side in ((before, bit), (after, 1 - bit)):
+            packet[pl.ds(pl.multiple_of(head + side * size, 16), size)] = source[
+                old_head : old_head + size
+            ]
+        smalls_out[...] = smalls_in[...] + after[old_head + size : old_head + size + 16].astype(F32)
+        tail = head + 2 * size
+    packet[tail : tail + 16] = smalls_out[...].astype(BF16)
 
 
 def finish_body(
     sec, place, before, after, smalls_in, mine, got, scale, shift, up, down, taps, conv, upb, downb, gain,
-    rows_of, tail, sems,
+    rows_of,
 ):
     spot = (sec[0], place[0])
     size = rows_of.shape[0] // 2
     bit = bit_of(spot, GATHER[3])
-    copies = []
-    for n, (source, spot_bit) in enumerate(((before, bit), (after, 1 - bit))):
-        target = rows_of.at[pl.ds(pl.multiple_of(spot_bit * size, 16), size)]
-        fetch(copies, source, 0, size, target, sems.at[n])
-    fetch(copies, after, size, 16, tail, sems.at[2])
+    for source, side in ((before, bit), (after, 1 - bit)):
+        rows_of[pl.ds(pl.multiple_of(side * size, 16), size)] = source[:size]
     first = spot[0] == 0
     one, two = mine[...], got[...]
     up_rows = up.shape[0]
@@ -505,9 +536,7 @@
     for j in range(3):
         up[:, j * TILE : (j + 1) * TILE] = ups[j * up_rows : (j + 1) * up_rows]
     down[...] = pick(first, two, one)
-    for copy in copies:
-        copy.wait()
-    total = smalls_in[...] + tail[...].astype(F32)
+    total = smalls_in[...] + after[size:].astype(F32)
     owned = scale.shape[0]
     count = 2 * size
     who = total[13:14, :count] * 64.0 + total[14:15, :count]
@@ -598,8 +627,8 @@
             struct((rows, 128), F32), whole_struct, half_struct, struct(tiled, BF16),
             struct(tiled, BF16), gradient_struct, gradient_struct, small_struct,
         ],
-        in_specs=[SMEM, SMEM, VMEM, VMEM] + [ANY] * 6,
-        out_specs=[VMEM, VMEM] + [ANY] * 11 + [VMEM],
+        in_specs=[SMEM, SMEM, VMEM, VMEM, HBM, HBM, HBM, ANY, HBM, ANY],
+        out_specs=[VMEM, VMEM] + [HBM] * 11 + [VMEM],
         scratch_shapes=[
             pltpu.VMEM((width, hidden), BF16),
             pltpu.VMEM((hidden, width), BF16),
@@ -622,12 +651,13 @@
             pltpu.VMEM((half, frames, width), BF16),
             pltpu.VMEM((SMALL, width), F32),
             pltpu.VMEM((SMALL, width), F32),
+            pltpu.VMEM((len(OFFSETS) * frames, frames), BF16),
             pltpu.VMEM(gradient, BF16),
             pltpu.VMEM(gradient, BF16),
             pltpu.SemaphoreType.DMA((10, 2)),
             pltpu.SemaphoreType.DMA((2, half)),
         ],
-        compiler_params=params(42),
+        compiler_params=params(46),
         cost_estimate=cost(9 * product, 24 << 20),
         name="main",
     )(
@@ -643,15 +673,15 @@
             num_scalar_prefetch=1,
             grid=(tiles,),
             in_specs=[full(rows, width), full(rows, width), tile_spec, tile_spec],
-            out_specs=[ANY, ANY],
+            out_specs=[HBM, HBM],
             scratch_shapes=[
                 pltpu.VMEM(gradient, BF16),
                 pltpu.VMEM(gradient, BF16),
-                pltpu.SemaphoreType.DMA((2,)),
+                pltpu.SemaphoreType.DMA((3, 8)),
             ],
         ),
         out_shape=[gradient_struct, gradient_struct],
-        compiler_params=params(20),
+        compiler_params=params(60),
         cost_estimate=cost(2 * product, 12 << 20),
         name="weights",
     )(sec, gb0, adapted0, act0, gpre0)
@@ -668,7 +698,7 @@
                 grid=(count,),
                 in_specs=[
                     pl.BlockSpec((tiles, frames, TILE), lambda c, sec: (0, at(c), 0)),
-                    ANY,
+                    HBM,
                     ANY,
                     pl.BlockSpec((frames, width), lambda c, sec: (at(c), 0)),
                     pl.BlockSpec((frames, 128), lambda c, sec: (at(c), 0)),
@@ -683,11 +713,15 @@
                     pl.BlockSpec(clip_block, lambda c, sec: (at(c), 0, 0)),
                     whole_small,
                 ],
-                scratch_shapes=[pltpu.VMEM((width, hidden), BF16), pltpu.SemaphoreType.DMA],
+                scratch_shapes=[
+                    pltpu.VMEM((width, hidden), BF16),
+                    pltpu.VMEM((len(OFFSETS) * frames, frames), BF16),
+                    pltpu.SemaphoreType.DMA,
+                ],
             ),
             out_shape=[whole_struct, half_struct, small_struct],
             input_output_aliases={10 + i: i for i in range(len(others))},
-            compiler_params=params(14),
+            compiler_params=params(LAST_MIB),
             cost_estimate=cost(8 * product, 12 << 20),
             name="last",
         )(sec, gpre0, up_own, up_got, normed0, inv0, small0, gin1, tokens, sums, *others)
@@ -722,56 +756,62 @@
 def halved(sec, place, speaker, pairs, sums0, sums1, got_sums, table_rows):
     _, share, width = pairs[0][0].shape
     pairs = [[piece.reshape(-1, width) for piece in pair] for pair in pairs]
-
-    def pack(step, block_sources, bases, extra_in):
-        blocks = len(block_sources)
-        levels = step + 2
-        count = 1 if step == 4 else 8 >> step
-        rows = count * share
-        extras = len(extra_in) > 0
-        outs = []
-        size = (8 << step) if extras else 0
-        length = (blocks * rows if step < 4 else 0) + (size + 16 if extras else 0)
-        outs.append(struct((length, width), BF16))
-        if extras:
-            outs.append(struct((SCALE, width), F32))
+    spot = (sec[0], place[0])
+    rows = 8 * share
+
+    def split(b):
+        return pl.pallas_call(
+            functools.partial(split_body, share),
+            out_shape=struct((rows, width), BF16),
+            in_specs=[SMEM, SMEM, HBM, ANY],
+            out_specs=VMEM,
+            scratch_shapes=[
+                pltpu.VMEM((rows, width), BF16),
+                pltpu.VMEM((rows, width), BF16),
+                pltpu.SemaphoreType.DMA((4, 2)),
+            ],
+            compiler_params=params(6),
+            cost_estimate=cost(0, 4 << 20),
+        )(sec, place, *pairs[b])
+
+    def part(array, first, count):
+        return lax.dynamic_slice_in_dim(array, first, count, 0).astype(F32)
+
+    latest, totals = [None, None], [None, None]
+    for b in (1, 0):
+        packet = split(b)
+        latest[b] = exchanged(packet, 0)
+    for b in (1, 0):
+        totals[b] = sum(part(piece, bit_of(spot, 0) * rows, rows) for piece in pairs[b])
+
+    def pack(step, extra_in):
+        count = 8 >> step
+        length = 2 * count * share + (8 << step) + 16
+        outs = [struct((length, width), BF16), struct((SCALE, width), F32)]
         if step == 4:
             outs += [struct((share, width), F32)] * 2
-        if extras and step == 1:
-            extra_specs = [VMEM] * 3
-        elif extras:
-            extra_specs = [ANY, ANY, VMEM]
-        else:
-            extra_specs = []
+        operands = list(totals) + (latest if step == 1 else []) + extra_in
         return pl.pallas_call(
-            functools.partial(pack_body, step, blocks, bases, share, int(extras)),
+            functools.partial(pack_body, step, share),
             out_shape=outs,
-            in_specs=[SMEM, SMEM, SMEM] + [ANY] * (blocks * levels) + extra_specs,
+            in_specs=[SMEM, SMEM, SMEM] + [VMEM] * len(operands),
             out_specs=[VMEM] * len(outs),
-            scratch_shapes=[
-                pltpu.VMEM((blocks, levels, rows, width), BF16),
-                pltpu.VMEM((16, width), BF16),
-                pltpu.SemaphoreType.DMA((3, max(levels, 3))),
-            ],
             compiler_params=params(8),
-            cost_estimate=cost(0, 4 << 20),
-        )(sec, place, speaker, *[x for sources in block_sources for x in sources], *extra_in)
-
-    for b in (1, 0):
-        (packet,) = pack(0, [pairs[b]], [[0]], [])
-        pairs[b].append(exchanged(packet, 0))
-    bases = [[0, 0], [0, 0]]
-    extra_in = [sums0, sums1, got_sums]
+            cost_estimate=cost(0, 2 << 20),
+        )(sec, place, speaker, *operands)
+
+    packet, smalls = pack(1, [sums0, sums1, got_sums])
     for step in range(1, 4):
-        packet, smalls = pack(step, pairs, bases, extra_in)
         got = exchanged(packet, step)
         rows = (8 >> step) * share
-        for b in range(2):
-            pairs[b].append(got)
-            bases[b].append(b * rows)
-        bases = [list(x) for x in bases]
-        extra_in = [packet, got, smalls]
-    packet, smalls, mine, away = pack(4, pairs, bases, extra_in)
+        first = bit_of(spot, step) * rows
+        bases = (0, 0) if step == 1 else (0, 2 * rows)
+        totals = [
+            part(totals[b], first, rows) + part(latest[b], bases[b] + first, rows) for b in range(2)
+        ]
+        latest = [got, got]
+        packet, smalls, *shares = pack(step + 1, [got, packet, smalls])
+    mine, away = shares
     got = exchanged(packet, 0)
     got_share = lax.ppermute(away, "section", [(0, 1), (1, 0)])
     owned = table_rows // BLOCKS
@@ -791,13 +831,9 @@
             one,
             one,
         ],
-        in_specs=[SMEM, SMEM, ANY, ANY, VMEM, VMEM, VMEM],
+        in_specs=[SMEM, SMEM] + [VMEM] * 5,
         out_specs=[VMEM] * 9,
-        scratch_shapes=[
-            pltpu.VMEM((16 * BLOCKS, width), BF16),
-            pltpu.VMEM((16, width), BF16),
-            pltpu.SemaphoreType.DMA((3,)),
-        ],
+        scratch_shapes=[pltpu.VMEM((16 * BLOCKS, width), BF16)],
         compiler_params=params(8),
         name="finish",
     )(sec, place, packet, got, smalls, mine, got_share)

time: 146 us -> 125 us (0.86)
  Pallas kernels: 72.1 us -> 61.1 us
  local copies, waits for them, and re-layouts: 19.9 us -> 10.7 us
  waiting for transfers between devices: 37.9 us -> 30.6 us
  other arithmetic: 0.01 us -> 4.3 us
  starting transfers between devices: 14.5 us -> 16.9 us
    unnamed x54 -> x52, local copies, waits for them, and re-layouts: 16.2 us -> 7.94 us
    pallas_call x1, Pallas kernels: 39.4 us -> 32.4 us  [local(): pl.pallas_call(main_body, out_shape=[small_struct, small_struct, half_str...]
    pallas_call x6, Pallas kernels: 15.3 us -> 9.23 us  [the longest x2 4.77 us: split(): pl.pallas_call(functools.partial(split_body, share), out_shape=struct((ro...]
    add x0 -> x6, other arithmetic: none -> 4.29 us  [the longest x4 2.69 us: halved(): part(totals[b], first, rows) + part(latest[b], bases[b] + first, rows)]
    ppermute x1, waiting for transfers between devices: 3.24 us -> 0.01 us  [local(): got0 = lax.ppermute(send0, 'section', swap)]
    ppermute x6, waiting for transfers between devices: 30.9 us -> 28 us  [exchanged(): return lax.ppermute(packet, PAIR, moves)]
    pallas_call x1, Pallas kernels: 5.15 us -> 7.6 us  [local(): pl.pallas_call(weights_body, grid_spec=pltpu.PrefetchScalarGridSpec(num_s...]
  transfers between devices with their start and end apart: 15 -> 15, of which waited for: 8 -> 6; matrix products, arithmetic and copies ran while one was open for 3% -> 6% of each run, Pallas kernels for 16% -> 21%
where the time goes in v3:
time: 125 us
  Pallas kernels  61.1 us (49%)
  waiting for transfers between devices  30.6 us (24%)
  starting transfers between devices  16.9 us (14%)
  local copies, waits for them, and re-layouts  10.7 us (9%)
  other arithmetic  4.3 us (3%)
    pallas_call x1, Pallas kernels, local(): pl.pallas_call(main_body, out_shape=[small_struct, small_struct, half_str...  32.4 us
    ppermute x6, waiting for transfers between devices, exchanged(): return lax.ppermute(packet, PAIR, moves)  28 us
    ppermute x6, starting transfers between devices, exchanged(): return lax.ppermute(packet, PAIR, moves)  12.9 us
    pallas_call x1, Pallas kernels, last(): pl.pallas_call(functools.partial(last_body, first), grid_spec=pltpu.Prefe...  8.32 us
    unnamed x52, local copies, waits for them, and re-layouts  7.94 us
    pallas_call x1, Pallas kernels, local(): pl.pallas_call(weights_body, grid_spec=pltpu.PrefetchScalarGridSpec(num_s...  7.6 us
    pallas_call x2, Pallas kernels, split(): pl.pallas_call(functools.partial(split_body, share), out_shape=struct((ro...  4.77 us
    pallas_call x4, Pallas kernels, pack(): pl.pallas_call(functools.partial(pack_body, step, share), out_shape=outs,...  4.46 us
  transfers between devices with their start and end apart: 15, of which 6 were waited for; matrix products, arithmetic and copies ran while one was open for 6% of the time, Pallas kernels for 21%

profile of v3, /device:TPU:0, one launch (start us, length us, event | category | flops | bytes accessed | tf_op | source)
XLA Modules:
  0.0 124.7 jit_solution(9921740750002281034)
XLA Ops:
  0.6 0.6 collective-permute-start.1
  1.2 0.1 collective-permute-start.2
  1.3 2.4 %prep.1 = (f32[24,512]{1,0:T(8,128)}, f32[24,512]{1,0:T(8,128)}) custom-call(s32[1]{0:T(128)} %bitcast.sec, s32[8]{0:T(128)} %speaker.9, f32[7,1,512]{2,1,0:T(1,128)} %bitcast.29, f32[1,512]{1,0:T(1,128)} %conv.1, f32[1,1536]{1,0:T(1,128)} %upb.1, f32[1,512]{1,0:T(1,128)} %downb.1, f32[1,512]{1,0:T(1,128)} %gain.1, f32[1,2560,512]{2,1,0:T(8,128)} %scale_hbm.1, ...), custom_call_target="tpu_custom_call" | custom-call | tf_op jit(solution)/shard_map/prep/pallas_call | solution.py:589
  3.7 0.5 collective-permute-start
  4.2 2.5 %collective-permute-done.got_small = f32[24,512]{1,0:T(8,128)S(1)} collective-permute-done((f32[24,512]{1,0:T(8,128)}, f32[24,512]{1,0:T(8,128)S(1)}, u32[]{:S(2)}, u32[]{:S(2)}) %collective-permute-start) | collective-permute-done | bytes 49184 | tf_op jit(solution)/shard_map/ppermute | solution.py:600
  6.8 1.1 copy-done.24
  7.9 1.1 copy-done.25
  9.1 0.8 copy-done.10
  9.9 32.4 %main.1 = (f32[24,512]{1,0:T(8,128)S(1)}, f32[24,512]{1,0:T(8,128)S(1)}, bf16[4,256,512]{2,1,0:T(8,128)(2,1)S(1)}, bf16[1024,512]{1,0:T(8,128)(2,1)S(1)}, bf16[1...) custom-call(s32[1]{0:T(128)} %bitcast.sec, ...), custom_call_target="tpu_custom_call" | custom-call | flops 14495514624 | bytes 25165824 | tf_op jit(solution)/shard_map/main/pallas_call | solution.py:623
  42.2 1.0 copy-done.12
  43.2 1.0 copy-done.13
  44.2 1.1 copy-done.14
  45.3 1.0 copy-done.16
  46.2 0.8 copy-done.18
  47.0 0.4 collective-permute-start.7
  47.4 7.6 %weights.1 = (bf16[16,96,512]{2,1,0:T(8,128)(2,1)}, bf16[16,96,512]{2,1,0:T(8,128)(2,1)}) custom-call(s32[1]{0:T(128)} %bitcast.sec, bf16[1024,512]{1,0:T(8,128)(2,1)} %copy-done.12, bf16[1024,512]{1,0:T(8,128)(2,1)} %copy-done.13, bf16[3,1024,512]{2,1,0:T(8,128)(2,1)} %get-tuple-element.65.act, bf16[3,1024,512]{2,1,0:T(8,128)(2,1)} %get-tuple-element.55.gpre), custom_call_target="tpu_custom_call" | custom-call | flops 3221225472 | bytes 12582912 | tf_op jit(solution)/shard_map/weights/pallas_call | solution.py:670
  55.0 0.5 collective-permute-start.5
  55.5 2.3 %shard_map.213 = bf16[768,512]{1,0:T(8,128)(2,1)S(1)} custom-call(s32[1]{0:T(128)} %bitcast.sec, s32[1]{0:T(128)} %bitcast.8.place, bf16[1536,512]{1,0:T(8,128)(2,1)S(1)} %bitcast.20, bf16[1536,512]{1,0:T(8,128)(2,1)S(1)} %bitcast.22), custom_call_target="tpu_custom_call" | custom-call | bytes 4194304 | tf_op jit(solution)/shard_map/pallas_call | solution.py:763
  57.8 2.9 %collective-permute-start.8 = (bf16[768,512]{1,0:T(8,128)(2,1)S(1)}, bf16[768,512]{1,0:T(8,128)(2,1)S(1)}, u32[]{:S(2)}, u32[]{:S(2)}) collective-permute-start(bf16[768,512]{1,0:T(8,128)(2,1)S(1)} %shard_map.213), channel_id=1, source_target_pairs={{0,1},{1,0},{2,3},{3,2},{4,5},{5,4},{6,7},{7,6},{8,9},{9,8},{10,11... | collective-permute-start | bytes 2359304 | tf_op jit(solution)/shard_map/ppermute | solution.py:753
  60.8 2.5 %shard_map.212 = bf16[768,512]{1,0:T(8,128)(2,1)S(1)} custom-call(s32[1]{0:T(128)} %bitcast.sec, s32[1]{0:T(128)} %bitcast.8.place, bf16[1536,512]{1,0:T(8,128)(2,1)S(1)} %bitcast.24, bf16[1536,512]{1,0:T(8,128)(2,1)} %bitcast.10.got), custom_call_target="tpu_custom_call" | custom-call | bytes 4194304 | tf_op jit(solution)/shard_map/pallas_call | solution.py:763
  63.3 1.0 collective-permute-start.6
  64.3 8.3 %last.1 = (bf16[8,256,512]{2,1,0:T(8,128)(2,1)}, bf16[4,256,512]{2,1,0:T(8,128)(2,1)S(1)}, f32[24,512]{1,0:T(8,128)S(1)}) custom-call(s32[1]{0:T(128)} %bitcast.sec, bf16[3,1024,512]{2,1,0:T(8,128)(2,1)} %get-tuple-element.55.gpre, bf16[512,1536]{1,0:T(8,128)(2,1)S(1)} %bitcast.28, bf16[512,1536]{1,0:T(8,128)(2,1)} %copy-done.24, ...), custom_call_target="tpu_custom_call" | custom-call | flops 12884901888 | bytes 12582912 | tf_op jit(solution)/shard_map/last/pallas_call | solution.py:694
  72.7 1.5 %collective-permute-start.9 = (f32[24,512]{1,0:T(8,128)S(1)}, f32[24,512]{1,0:T(8,128)S(1)}, u32[]{:S(2)}, u32[]{:S(2)}) collective-permute-start(f32[24,512]{1,0:T(8,128)S(1)} %broadcast_select_fusion), channel_id=1, source_target_pairs={{0,16},{16,0},{1,17},{17,1},{2,18},{18,2},{3,19},{19,3},{4,20},{20... | collective-permute-start | bytes 147464 | tf_op jit(solution)/shard_map/ppermute | solution.py:731
  74.2 0.2 convert_add_fusion.total1
  74.4 0.0 copy-start.7
  74.4 1.4 %convert_add_fusion.1.total0 = f32[768,512]{1,0:T(8,128)S(1)} fusion(bf16[1536,512]{1,0:T(8,128)(2,1)} %bitcast.10.got, s32[]{:T(128)S(6)} %select_n.59, bf16[1536,512]{1,0:T(8,128)(2,1)S(1)} %bitcast.25), kind=kLoop, calls=%fused_computation.1 | loop fusion | flops 1179648 | bytes 3145732 | tf_op jit(solution)/shard_map/add | solution.py:785
  75.8 3.3 %collective-permute-done.6.refs_0_ = bf16[768,512]{1,0:T(8,128)(2,1)S(1)} collective-permute-done((bf16[768,512]{1,0:T(8,128)(2,1)S(1)}, bf16[768,512]{1,0:T(8,128)(2,1)S(1)}, u32[]{:S(2)}, u32[]{:S(2)}) %collective-permute-start.6) | collective-permute-done | bytes 786464 | tf_op jit(solution)/shard_map/ppermute | solution.py:753
  79.2 1.7 %shard_map.214 = (bf16[800,512]{1,0:T(8,128)(2,1)}, f32[16,512]{1,0:T(8,128)S(1)}) custom-call(s32[1]{0:T(128)} %bitcast.sec, s32[1]{0:T(128)} %bitcast.8.place, s32[8]{0:T(128)S(1)} %copy-done.7, f32[768,512]{1,0:T(8,128)S(1)} %convert_add_fusion.1.total0, f32[768,512]{1,0:T(8,128)S(1)} %convert_add_fusion.total1, ...), custom_call_target="tpu_custom_call" | custom-call | bytes 2097152 | tf_op jit(solution)/shard_map/pallas_call | solution.py:794
  80.9 2.0 %collective-permute-start.10 = (bf16[800,512]{1,0:T(8,128)(2,1)}, bf16[800,512]{1,0:T(8,128)(2,1)}, u32[]{:S(2)}, u32[]{:S(2)}) collective-permute-start(bf16[800,512]{1,0:T(8,128)(2,1)} %get-tuple-element.72.refs_1_), channel_id=1, source_target_pairs={{0,2},{1,3},{2,0},{3,1},{4,6},{5,7},{6,4},{7,5},{8,10},{9,11},{10,... | collective-permute-start | bytes 2457608 | tf_op jit(solution)/shard_map/ppermute | solution.py:753
  82.9 0.5 collective-permute-start.4
  83.5 1.1 convert_add_fusion.2.total1
  84.6 0.1 convert_add_fusion.3.total0
  84.7 8.9 %collective-permute-done.10.refs_0_ = bf16[800,512]{1,0:T(8,128)(2,1)} collective-permute-done((bf16[800,512]{1,0:T(8,128)(2,1)}, bf16[800,512]{1,0:T(8,128)(2,1)}, u32[]{:S(2)}, u32[]{:S(2)}) %collective-permute-start.10) | collective-permute-done | bytes 819232 | tf_op jit(solution)/shard_map/ppermute | solution.py:753
  93.6 1.5 %shard_map.215 = (bf16[432,512]{1,0:T(8,128)(2,1)S(1)}, f32[16,512]{1,0:T(8,128)S(1)}) custom-call(s32[1]{0:T(128)} %bitcast.sec, s32[1]{0:T(128)} %bitcast.8.place, s32[8]{0:T(128)S(1)} %copy-done.7, f32[384,512]{1,0:T(8,128)S(1)} %convert_add_fusion.3.total0, f32[384,512]{1,0:T(8,128)S(1)} %convert_add_fusion.2.total1, ...), custom_call_target="tpu_custom_call" | custom-call | bytes 2097152 | tf_op jit(solution)/shard_map/pallas_call | solution.py:794
  95.1 2.1 %collective-permute-start.11 = (bf16[432,512]{1,0:T(8,128)(2,1)S(1)}, bf16[432,512]{1,0:T(8,128)(2,1)S(1)}, u32[]{:S(2)}, u32[]{:S(2)}) collective-permute-start(bf16[432,512]{1,0:T(8,128)(2,1)S(1)} %get-tuple-element.74.refs_1_), channel_id=1, source_target_pairs={{0,4},{1,5},{2,6},{3,7},{4,0},{5,1},{6,2},{7,3},{8,12},{9,13},{10,... | collective-permute-start | bytes 1327112 | tf_op jit(solution)/shard_map/ppermute | solution.py:753
  97.2 1.4 %convert_add_fusion.4 = (f32[192,512]{1,0:T(8,128)S(1)}, f32[192,512]{1,0:T(8,128)S(1)}) fusion(f32[384,512]{1,0:T(8,128)} %copy-done, s32[]{:T(128)S(6)} %select_n.63, bf16[800,512]{1,0:T(8,128)(2,1)} %collective-permute-done.10.refs_0_, s32[]{:T(128)S(6)} %select_n.69, s32[]{:T(128)S(6)} %select_n.66, f32[384,512]{1,0:T(8,128)S(1)} %convert_add_fusion.3.total0), kind=kLoop, calls=%fused_computation.6 | loop fusion | flops 393216 | bytes 1966092 | tf_op jit(solution)/shard_map/add | solution.py:810
  98.7 4.9 %collective-permute-done.11.refs_0_ = bf16[432,512]{1,0:T(8,128)(2,1)S(1)} collective-permute-done((bf16[432,512]{1,0:T(8,128)(2,1)S(1)}, bf16[432,512]{1,0:T(8,128)(2,1)S(1)}, u32[]{:S(2)}, u32[]{:S(2)}) %collective-permute-start.11) | collective-permute-done | bytes 442400 | tf_op jit(solution)/shard_map/ppermute | solution.py:753
  103.5 0.6 shard_map.216
  104.1 3.1 %collective-permute-start.12 = (bf16[272,512]{1,0:T(8,128)(2,1)S(1)}, bf16[272,512]{1,0:T(8,128)(2,1)S(1)}, u32[]{:S(2)}, u32[]{:S(2)}) collective-permute-start(bf16[272,512]{1,0:T(8,128)(2,1)S(1)} %get-tuple-element.76.refs_1_), channel_id=1, source_target_pairs={{0,8},{1,9},{2,10},{3,11},{4,12},{5,13},{6,14},{7,15},{8,0},{9,1},... | collective-permute-start | bytes 835592 | tf_op jit(solution)/shard_map/ppermute | solution.py:753
  107.2 1.5 %bitcast_dynamic-update-slice_fusion.1 = bf16[1,8,256,512]{3,2,1,0:T(8,128)(2,1)S(1)} fusion(bf16[1,8,256,512]{3,2,1,0:T(8,128)(2,1)S(1)} %bitcast.30, s32[]{:T(128)S(6)} %select_n.57, bf16[4,256,512]{2,1,0:T(8,128)(2,1)} %collective-permute-done.3), kind=kLoop, calls=%fused_computation.3 | loop fusion | bytes 2097156 | tf_op jit(solution)/shard_map/dynamic_update_slice | solution.py:734
  108.7 0.0 copy-start.21
  108.7 0.1 convert_add_fusion.6
  108.8 8.7 %collective-permute-done.12.refs_0_ = bf16[272,512]{1,0:T(8,128)(2,1)S(1)} collective-permute-done((bf16[272,512]{1,0:T(8,128)(2,1)S(1)}, bf16[272,512]{1,0:T(8,128)(2,1)S(1)}, u32[]{:S(2)}, u32[]{:S(2)}) %collective-permute-start.12) | collective-permute-done | bytes 278560 | tf_op jit(solution)/shard_map/ppermute | solution.py:753
  117.5 0.6 shard_map.217
  118.1 1.6 %collective-permute-start.13 = (bf16[144,512]{1,0:T(8,128)(2,1)S(1)}, bf16[144,512]{1,0:T(8,128)(2,1)S(1)}, u32[]{:S(2)}, u32[]{:S(2)}) collective-permute-start(bf16[144,512]{1,0:T(8,128)(2,1)S(1)} %get-tuple-element.78.before), channel_id=1, source_target_pairs={{0,1},{1,0},{2,3},{3,2},{4,5},{5,4},{6,7},{7,6},{8,9},{9,8},{10,11... | collective-permute-start | bytes 442376 | tf_op jit(solution)/shard_map/ppermute | solution.py:753
  119.8 1.3 %bitcast_dynamic-update-slice_fusion = bf16[1,8,256,512]{3,2,1,0:T(8,128)(2,1)S(1)} fusion(bf16[1,8,256,512]{3,2,1,0:T(8,128)(2,1)S(1)} %bitcast.31, s32[]{:T(128)S(6)} %select_n.57, bf16[4,256,512]{2,1,0:T(8,128)(2,1)} %collective-permute-done.4), kind=kLoop, calls=%fused_computation.2 | loop fusion | bytes 2097156 | tf_op jit(solution)/shard_map/dynamic_update_slice | solution.py:734
  121.1 2.2 %collective-permute-done.13.after = bf16[144,512]{1,0:T(8,128)(2,1)S(1)} collective-permute-done((bf16[144,512]{1,0:T(8,128)(2,1)S(1)}, bf16[144,512]{1,0:T(8,128)(2,1)S(1)}, u32[]{:S(2)}, u32[]{:S(2)}) %collective-permute-start.13) | collective-permute-done | bytes 147488 | tf_op jit(solution)/shard_map/ppermute | solution.py:753
  123.3 1.2 finish.1
  (54 shorter events, 0.1 us)
Async XLA Ops:
  0.6 6.1 %collective-permute-start.1 = (bf16[512,1536]{1,0:T(8,128)(2,1)}, bf16[512,1536]{1,0:T(8,128)(2,1)S(1)}, u32[]{:S(2)}, u32[]{:S(2)}) collective-permute-start(bf16[512,1536]{1,0:T(8,128)(2,1)} %bitcast.26), channel_id=1, source_target_pairs={{0,16},{16,0},{1,17},{17,1},{2,18},{18,2},{3,19},{19,3},{4,20},{20... | collective-permute-start | bytes 4718600 | tf_op jit(solution)/shard_map/ppermute | solution.py:602
  1.2 5.6 %collective-permute-start.2 = (bf16[1536,512]{1,0:T(8,128)(2,1)}, bf16[1536,512]{1,0:T(8,128)(2,1)S(1)}, u32[]{:S(2)}, u32[]{:S(2)}) collective-permute-start(bf16[1536,512]{1,0:T(8,128)(2,1)} %bitcast.32), channel_id=1, source_target_pairs={{0,16},{16,0},{1,17},{17,1},{2,18},{18,2},{3,19},{19,3},{4,20},{20... | collective-permute-start | bytes 4718600 | tf_op jit(solution)/shard_map/ppermute | solution.py:603
  1.3 7.8 %copy-start.11 = (s32[8]{0:T(128)S(1)}, s32[8]{0:T(128)}, u32[]{:S(2)}) copy-start(s32[8]{0:T(128)} %valid.1) | copy-start | bytes 100
  3.7 3.0 %collective-permute-start = (f32[24,512]{1,0:T(8,128)}, f32[24,512]{1,0:T(8,128)S(1)}, u32[]{:S(2)}, u32[]{:S(2)}) collective-permute-start(f32[24,512]{1,0:T(8,128)} %get-tuple-element.52), channel_id=1, source_target_pairs={{0,16},{16,0},{1,17},{17,1},{2,18},{18,2},{3,19},{19,3},{4,20},{20... | collective-permute-start | bytes 147464 | tf_op jit(solution)/shard_map/ppermute | solution.py:600
  6.8 1.1 copy-start.24
  7.9 1.1 copy-start.25
  9.1 0.8 copy-start.10
  42.2 1.0 copy-start.12
  43.2 1.0 copy-start.13
  44.2 1.1 copy-start.14
  45.3 1.0 copy-start.16
  46.2 0.8 copy-start.18
  47.0 8.5 %collective-permute-start.7 = (bf16[16,96,512]{2,1,0:T(8,128)(2,1)}, bf16[16,96,512]{2,1,0:T(8,128)(2,1)S(1)}, u32[]{:S(2)}, u32[]{:S(2)}) collective-permute-start(bf16[16,96,512]{2,1,0:T(8,128)(2,1)} %get-tuple-element.69), channel_id=1, source_target_pairs={{0,16},{16,0},{1,17},{17,1},{2,18},{18,2},{3,19},{19,3},{4,20},{20... | collective-permute-start | bytes 4718600 | tf_op jit(solution)/shard_map/ppermute | solution.py:666
  55.0 5.8 %collective-permute-start.5 = (bf16[16,96,512]{2,1,0:T(8,128)(2,1)}, bf16[16,96,512]{2,1,0:T(8,128)(2,1)}, u32[]{:S(2)}, u32[]{:S(2)}) collective-permute-start(bf16[16,96,512]{2,1,0:T(8,128)(2,1)} %get-tuple-element.67), channel_id=1, source_target_pairs={{0,16},{16,0},{1,17},{17,1},{2,18},{18,2},{3,19},{19,3},{4,20},{20... | collective-permute-start | bytes 4718600 | tf_op jit(solution)/shard_map/ppermute | solution.py:688
  55.5 2.3 %copy-start.1 = (bf16[16,96,512]{2,1,0:T(8,128)(2,1)}, bf16[16,96,512]{2,1,0:T(8,128)(2,1)S(1)}, u32[]{:S(2)}) copy-start(bf16[16,96,512]{2,1,0:T(8,128)(2,1)S(1)} %collective-permute-done.7) | copy-start | bytes 4718596
  55.5 5.3 %copy-start.3 = (bf16[16,96,512]{2,1,0:T(8,128)(2,1)S(1)}, bf16[16,96,512]{2,1,0:T(8,128)(2,1)}, u32[]{:S(2)}) copy-start(bf16[16,96,512]{2,1,0:T(8,128)(2,1)} %get-tuple-element.66) | copy-start | bytes 4718596
  55.5 8.8 %copy-start.19 = (f32[1024,128]{1,0:T(8,128)S(1)}, f32[1024,128]{1,0:T(8,128)}, u32[]{:S(2)}) copy-start(f32[1024,128]{1,0:T(8,128)} %copy-done.18) | copy-start | bytes 1572868
  57.8 18.0 %collective-permute-start.8 = (bf16[768,512]{1,0:T(8,128)(2,1)S(1)}, bf16[768,512]{1,0:T(8,128)(2,1)S(1)}, u32[]{:S(2)}, u32[]{:S(2)}) collective-permute-start(bf16[768,512]{1,0:T(8,128)(2,1)S(1)} %shard_map.213), channel_id=1, source_target_pairs={{0,1},{1,0},{2,3},{3,2},{4,5},{5,4},{6,7},{7,6},{8,9},{9,8},{10,11... | collective-permute-start | bytes 2359304 | tf_op jit(solution)/shard_map/ppermute | solution.py:753
  60.8 3.5 %copy-start.8 = (bf16[1,512,1536]{2,1,0:T(8,128)(2,1)S(1)}, bf16[1,512,1536]{2,1,0:T(8,128)(2,1)}, u32[]{:S(2)}) copy-start(bf16[1,512,1536]{2,1,0:T(8,128)(2,1)} %param.21) | copy-start | bytes 4718596
  60.8 3.5 %copy-start.15 = (bf16[4,256,512]{2,1,0:T(8,128)(2,1)S(1)}, bf16[4,256,512]{2,1,0:T(8,128)(2,1)}, u32[]{:S(2)}) copy-start(bf16[4,256,512]{2,1,0:T(8,128)(2,1)} %copy-done.14) | copy-start | bytes 3145732
  60.8 3.5 %copy-start.17 = (bf16[1024,512]{1,0:T(8,128)(2,1)S(1)}, bf16[1024,512]{1,0:T(8,128)(2,1)}, u32[]{:S(2)}) copy-start(bf16[1024,512]{1,0:T(8,128)(2,1)} %copy-done.16) | copy-start | bytes 3145732
  63.3 15.9 %collective-permute-start.6 = (bf16[768,512]{1,0:T(8,128)(2,1)S(1)}, bf16[768,512]{1,0:T(8,128)(2,1)S(1)}, u32[]{:S(2)}, u32[]{:S(2)}) collective-permute-start(bf16[768,512]{1,0:T(8,128)(2,1)S(1)} %shard_map.212), channel_id=1, source_target_pairs={{0,1},{1,0},{2,3},{3,2},{4,5},{5,4},{6,7},{7,6},{8,9},{9,8},{10,11... | collective-permute-start | bytes 2359304 | tf_op jit(solution)/shard_map/ppermute | solution.py:753
  64.3 9.9 %copy-start.2 = (bf16[16,96,512]{2,1,0:T(8,128)(2,1)S(1)}, bf16[16,96,512]{2,1,0:T(8,128)(2,1)}, u32[]{:S(2)}) copy-start(bf16[16,96,512]{2,1,0:T(8,128)(2,1)} %copy-done.1) | copy-start | bytes 4718596
  72.6 8.3 %copy-start.9 = (bf16[4,256,512]{2,1,0:T(8,128)(2,1)}, bf16[4,256,512]{2,1,0:T(8,128)(2,1)S(1)}, u32[]{:S(2)}) copy-start(bf16[4,256,512]{2,1,0:T(8,128)(2,1)S(1)} %get-tuple-element.62) | copy-start | bytes 3145732
  72.7 3.1 %collective-permute-start.9 = (f32[24,512]{1,0:T(8,128)S(1)}, f32[24,512]{1,0:T(8,128)S(1)}, u32[]{:S(2)}, u32[]{:S(2)}) collective-permute-start(f32[24,512]{1,0:T(8,128)S(1)} %broadcast_select_fusion), channel_id=1, source_target_pairs={{0,16},{16,0},{1,17},{17,1},{2,18},{18,2},{3,19},{19,3},{4,20},{20... | collective-permute-start | bytes 147464 | tf_op jit(solution)/shard_map/ppermute | solution.py:731
  74.4 4.8 %copy-start.7 = (s32[8]{0:T(128)S(1)}, s32[8]{0:T(128)}, u32[]{:S(2)}) copy-start(s32[8]{0:T(128)} %speaker.9) | copy-start | bytes 100
  75.8 3.3 %copy-start.4 = (bf16[768,512]{1,0:T(8,128)(2,1)}, bf16[768,512]{1,0:T(8,128)(2,1)S(1)}, u32[]{:S(2)}) copy-start(bf16[768,512]{1,0:T(8,128)(2,1)S(1)} %collective-permute-done.8.refs_1_) | copy-start | bytes 2359300
  79.2 1.7 %copy-start.5 = (bf16[768,512]{1,0:T(8,128)(2,1)}, bf16[768,512]{1,0:T(8,128)(2,1)S(1)}, u32[]{:S(2)}) copy-start(bf16[768,512]{1,0:T(8,128)(2,1)S(1)} %collective-permute-done.6.refs_0_) | copy-start | bytes 2359300
  80.9 12.7 %collective-permute-start.10 = (bf16[800,512]{1,0:T(8,128)(2,1)}, bf16[800,512]{1,0:T(8,128)(2,1)}, u32[]{:S(2)}, u32[]{:S(2)}) collective-permute-start(bf16[800,512]{1,0:T(8,128)(2,1)} %get-tuple-element.72.refs_1_), channel_id=1, source_target_pairs={{0,2},{1,3},{2,0},{3,1},{4,6},{5,7},{6,4},{7,5},{8,10},{9,11},{10,... | collective-permute-start | bytes 2457608 | tf_op jit(solution)/shard_map/ppermute | solution.py:753
  82.9 24.3 %collective-permute-start.3 = (bf16[4,256,512]{2,1,0:T(8,128)(2,1)}, bf16[4,256,512]{2,1,0:T(8,128)(2,1)}, u32[]{:S(2)}, u32[]{:S(2)}) collective-permute-start(bf16[4,256,512]{2,1,0:T(8,128)(2,1)} %get-tuple-element.54), channel_id=1, source_target_pairs={{0,16},{16,0},{1,17},{17,1},{2,18},{18,2},{3,19},{19,3},{4,20},{20... | collective-permute-start | bytes 3145736 | tf_op jit(solution)/shard_map/ppermute | solution.py:667
  82.9 1.6 %copy-start.6 = (bf16[768,512]{1,0:T(8,128)(2,1)S(1)}, bf16[768,512]{1,0:T(8,128)(2,1)}, u32[]{:S(2)}) copy-start(bf16[768,512]{1,0:T(8,128)(2,1)} %copy-done.5) | copy-start | bytes 2359300
  82.9 36.8 %collective-permute-start.4 = (bf16[4,256,512]{2,1,0:T(8,128)(2,1)}, bf16[4,256,512]{2,1,0:T(8,128)(2,1)}, u32[]{:S(2)}, u32[]{:S(2)}) collective-permute-start(bf16[4,256,512]{2,1,0:T(8,128)(2,1)} %copy-done.9), channel_id=1, source_target_pairs={{0,16},{16,0},{1,17},{17,1},{2,18},{18,2},{3,19},{19,3},{4,20},{20... | collective-permute-start | bytes 3145736 | tf_op jit(solution)/shard_map/ppermute | solution.py:730
  84.6 10.5 %copy-start = (f32[384,512]{1,0:T(8,128)}, f32[384,512]{1,0:T(8,128)S(1)}, u32[]{:S(2)}) copy-start(f32[384,512]{1,0:T(8,128)S(1)} %convert_add_fusion.2.total1) | copy-start | bytes 2359300
  95.1 8.4 %collective-permute-start.11 = (bf16[432,512]{1,0:T(8,128)(2,1)S(1)}, bf16[432,512]{1,0:T(8,128)(2,1)S(1)}, u32[]{:S(2)}, u32[]{:S(2)}) collective-permute-start(bf16[432,512]{1,0:T(8,128)(2,1)S(1)} %get-tuple-element.74.refs_1_), channel_id=1, source_target_pairs={{0,4},{1,5},{2,6},{3,7},{4,0},{5,1},{6,2},{7,3},{8,12},{9,13},{10,... | collective-permute-start | bytes 1327112 | tf_op jit(solution)/shard_map/ppermute | solution.py:753
  97.2 10.0 %copy-start.20 = (bf16[8,256,512]{2,1,0:T(8,128)(2,1)S(1)}, bf16[8,256,512]{2,1,0:T(8,128)(2,1)}, u32[]{:S(2)}) copy-start(bf16[8,256,512]{2,1,0:T(8,128)(2,1)} %get-tuple-element.53) | copy-start | bytes 6291460
  104.1 13.4 %collective-permute-start.12 = (bf16[272,512]{1,0:T(8,128)(2,1)S(1)}, bf16[272,512]{1,0:T(8,128)(2,1)S(1)}, u32[]{:S(2)}, u32[]{:S(2)}) collective-permute-start(bf16[272,512]{1,0:T(8,128)(2,1)S(1)} %get-tuple-element.76.refs_1_), channel_id=1, source_target_pairs={{0,8},{1,9},{2,10},{3,11},{4,12},{5,13},{6,14},{7,15},{8,0},{9,1},... | collective-permute-start | bytes 835592 | tf_op jit(solution)/shard_map/ppermute | solution.py:753
  107.2 12.5 %copy-start.22 = (bf16[8,256,512]{2,1,0:T(8,128)(2,1)S(1)}, bf16[8,256,512]{2,1,0:T(8,128)(2,1)}, u32[]{:S(2)}) copy-start(bf16[8,256,512]{2,1,0:T(8,128)(2,1)} %get-tuple-element.61) | copy-start | bytes 6291460
  108.7 12.4 %copy-start.21 = (bf16[1,8,256,512]{3,2,1,0:T(8,128)(2,1)}, bf16[1,8,256,512]{3,2,1,0:T(8,128)(2,1)S(1)}, u32[]{:S(2)}) copy-start(bf16[1,8,256,512]{3,2,1,0:T(8,128)(2,1)S(1)} %bitcast_dynamic-update-slice_fusion.1) | copy-start | bytes 6291460
  118.1 5.2 %collective-permute-start.13 = (bf16[144,512]{1,0:T(8,128)(2,1)S(1)}, bf16[144,512]{1,0:T(8,128)(2,1)S(1)}, u32[]{:S(2)}, u32[]{:S(2)}) collective-permute-start(bf16[144,512]{1,0:T(8,128)(2,1)S(1)} %get-tuple-element.78.before), channel_id=1, source_target_pairs={{0,1},{1,0},{2,3},{3,2},{4,5},{5,4},{6,7},{7,6},{8,9},{9,8},{10,11... | collective-permute-start | bytes 442376 | tf_op jit(solution)/shard_map/ppermute | solution.py:753
  119.8 3.6 %collective-permute-start.14 = (f32[96,512]{1,0:T(8,128)S(1)}, f32[96,512]{1,0:T(8,128)S(1)}, u32[]{:S(2)}, u32[]{:S(2)}) collective-permute-start(f32[96,512]{1,0:T(8,128)S(1)} %get-tuple-element.81), channel_id=1, source_target_pairs={{0,16},{16,0},{1,17},{17,1},{2,18},{18,2},{3,19},{19,3},{4,20},{20... | collective-permute-start | bytes 589832 | tf_op jit(solution)/shard_map/ppermute | solution.py:816
  121.1 3.4 %copy-start.23 = (bf16[1,8,256,512]{3,2,1,0:T(8,128)(2,1)}, bf16[1,8,256,512]{3,2,1,0:T(8,128)(2,1)S(1)}, u32[]{:S(2)}) copy-start(bf16[1,8,256,512]{3,2,1,0:T(8,128)(2,1)S(1)} %bitcast_dynamic-update-slice_fusion) | copy-start | bytes 6291460

commit v4 on v3

--- a/solution.py
+++ b/solution.py
@@ -12,7 +12,7 @@
 BF16 = jnp.bfloat16
 PAIR = ("section", "dp")
 TILE = 512
-LAST_MIB = 48
+ALL_VMEM = 67043328
 HALF_ROOT = 0.7071067811865476
 DENSITY = 0.3989422804014327
 BLOCKS = 16
@@ -205,6 +205,33 @@
         go(up_got, down_got)
 
 
+def route_tile(sec, j, upd, dnd, keep, send, sems, start):
+    share = TILE // BLOCKS
+
+    def go(up_to, down_to):
+        part = pl.ds(j * share, share)
+        copies = [pltpu.make_async_copy(upd.at[:, part], up_to.at[:, part], sems.at[j, 0])]
+        for n, (block, first, rows, _) in enumerate(down_pieces(j)):
+            part = pl.ds(first, rows)
+            copies.append(
+                pltpu.make_async_copy(dnd.at[block, part], down_to.at[block, part], sems.at[j, 1 + n])
+            )
+        for copy in copies:
+            copy.start() if start else copy.wait()
+
+    if not start:
+        go(keep, send)
+        return
+
+    @pl.when(sec[0] == 0)
+    def _():
+        go(keep, send)
+
+    @pl.when(sec[0] != 0)
+    def _():
+        go(send, keep)
+
+
 def route(sec, upd, dnd, keep, send, sems, start):
     def go(kept, sent):
         for source, target, sem in ((kept, keep, sems.at[0]), (sent, send, sems.at[1])):
@@ -226,10 +253,10 @@
 
 def main_body(
     sec, valid, own_small, got_small, tokens, cot, up_own, up_got, down_own, down_got,
-    sums0, sums1, gin1, gb0_hbm, adapted_hbm, normed_hbm, inv_hbm, out_own, out_send, act_hbm,
-    gpre_hbm, keep, send, small0_out,
+    sums0, sums1, gin1, normed_hbm, inv_hbm, out_own, out_send, gpre_hbm, keep1, send1, keep0, send0,
+    small0_out,
     up0, down0, up1, down1, act0, slope0, act1, slope1, acc, adapted0, normed, inv, adapted1, branch0,
-    gb, v, grad, out0, out1, small0, small1, shifts, upd, dnd, sems, pieces,
+    gb, v, grad, out0, out1, small0, small1, shifts, upd, dnd, upd0, dnd0, sems, pieces, parts,
 ):
     clips = acc.shape[0] // 256
     mine = pl.ds(sec[0] * clips, clips)
@@ -259,16 +286,15 @@
     saves = [
         pltpu.make_async_copy(source, target, sems.at[7 + n // 2, n % 2])
         for n, (source, target) in enumerate(
-            ((normed, normed_hbm), (inv, inv_hbm), (adapted0, adapted_hbm), (act0, act_hbm))
+            ((normed, normed_hbm), (inv, inv_hbm))
         )
     ]
-    for copy in saves[:3]:
+    for copy in saves:
         copy.start()
     place_weights(sec, 0, *weights, up0, down0, sems.at[0], False)
     forward_tiles(adapted0, up0, down0, small0, act0, slope0, acc)
-    saves[3].start()
-    saves[0].wait()
-    saves[1].wait()
+    for copy in saves:
+        copy.wait()
 
     def between(r):
         rows = pl.ds(pl.multiple_of(r * 256, 256), 256)
@@ -304,14 +330,10 @@
             part = dot(slope1[j, rows], up1[:, j * TILE : (j + 1) * TILE], NT)
             acc[rows] = part if j == 0 else acc[rows] + part
         weight_tile(j, gb, adapted1, act1[j], slope1[j], upd, dnd)
-    route(sec, upd, dnd, keep, send, sems.at[3], True)
+    route(sec, upd, dnd, keep1, send1, sems.at[3], True)
 
     def move(r):
-        rows = pl.ds(pl.multiple_of(r * 256, 256), 256)
-        return (
-            pltpu.make_async_copy(grad.at[r], gin1.at[r], pieces.at[0, r]),
-            pltpu.make_async_copy(gb.at[rows], gb0_hbm.at[rows], pieces.at[1, r]),
-        )
+        return pltpu.make_async_copy(grad.at[r], gin1.at[r], pieces.at[r])
 
     def under(r):
         rows = pl.ds(pl.multiple_of(r * 256, 256), 256)
@@ -326,8 +348,7 @@
         grad0 = gin.astype(F32)
         low = (grad0 * small0[GAIN : GAIN + 1]).astype(BF16)
         gb[rows] = low
-        for copy in move(r):
-            copy.start()
+        move(r).start()
         sums0[GAIN : GAIN + 1] += rowsum(grad0 * branch0[rows])
         sums0[DOWNB : DOWNB + 1] += rowsum(low.astype(F32))
 
@@ -335,52 +356,16 @@
     tiles = []
     for j in range(3):
         activation_tile(j, gb, down0, slope0, sums0)
-        tiles.append(pltpu.make_async_copy(slope0.at[j], gpre_hbm.at[j], sems.at[5 + j // 2 * 4, j % 2]))
+        tiles.append(pltpu.make_async_copy(slope0.at[j], gpre_hbm.at[j], sems.at[5 + j // 2 * 3, j % 2]))
         tiles[-1].start()
+        weight_tile(j, gb, adapted0, act0[j], slope0[j], upd0, dnd0)
+        route_tile(sec, j, upd0, dnd0, keep0, send0, parts, True)
     route(sec, out0, out1, half_own, out_send, sems.at[4], False)
-    route(sec, upd, dnd, keep, send, sems.at[3], False)
-    for copy in saves[2:] + tiles:
+    route(sec, upd, dnd, keep1, send1, sems.at[3], False)
+    for copy in tiles + [move(r) for r in range(clips)]:
         copy.wait()
-    for r in range(clips):
-        for copy in move(r):
-            copy.wait()
-
-
-def weights_body(sec, gb, adapted, act, gpre, keep, send, upd, dnd, sems):
-    step = pl.program_id(0)
-    share = TILE // BLOCKS
-
-    def copies(j, up_to, down_to):
-        part = pl.ds(j * share, share)
-        moves = [pltpu.make_async_copy(upd.at[:, part], up_to.at[:, part], sems.at[j, 0])]
-        for n, (block, first, rows, _) in enumerate(down_pieces(j)):
-            part = pl.ds(first, rows)
-            moves.append(
-                pltpu.make_async_copy(dnd.at[block, part], down_to.at[block, part], sems.at[j, 1 + n])
-            )
-        return moves
-
     for j in range(3):
-
-        @pl.when(step == j)
-        def _():
-            weight_tile(j, gb, adapted, act[0], gpre[0], upd, dnd)
-
-            @pl.when(sec[0] == 0)
-            def _():
-                for copy in copies(j, keep, send):
-                    copy.start()
-
-            @pl.when(sec[0] != 0)
-            def _():
-                for copy in copies(j, send, keep):
-                    copy.start()
-
-    @pl.when(step == 2)
-    def _():
-        for j in range(3):
-            for copy in copies(j, keep, send):
-                copy.wait()
+        route_tile(sec, j, upd0, dnd0, keep0, send0, parts, False)
 
 
 def last_body(
@@ -562,8 +547,8 @@
     return jax.ShapeDtypeStruct(shape, dtype)
 
 
-def params(limit):
-    return pltpu.CompilerParams(vmem_limit_bytes=limit * 1024 * 1024)
+def params(limit=None):
+    return pltpu.CompilerParams(vmem_limit_bytes=limit * 1024 * 1024 if limit else ALL_VMEM)
 
 
 def cost(flops, moved):
@@ -592,6 +577,7 @@
         in_specs=[SMEM, SMEM] + [VMEM] * 5 + [ANY] * 2,
         out_specs=[VMEM] * 2,
         scratch_shapes=[pltpu.SemaphoreType.DMA((2, 2, half))],
+        compiler_params=params(),
         name="prep",
     )(
         sec, speaker, conv_weight.transpose(1, 0, 2), conv_bias, up_bias, down_bias, layer_scale,
@@ -614,21 +600,17 @@
     gradient_struct = struct(gradient, BF16)
     product = 2 * rows * width * hidden
 
-    def full(*shape):
-        return pl.BlockSpec(shape, lambda i, *_: (0,) * len(shape))
-
     (
-        sums0, sums1, gin1, gb0, adapted0, normed0, inv0, out_own, out_send, act0, gpre0, keep1, send1,
-        small0,
+        sums0, sums1, gin1, normed0, inv0, out_own, out_send, gpre0, keep1, send1, keep0, send0, small0,
     ) = pl.pallas_call(
         main_body,
         out_shape=[
-            small_struct, small_struct, half_struct, flat_struct, flat_struct, flat_struct,
-            struct((rows, 128), F32), whole_struct, half_struct, struct(tiled, BF16),
-            struct(tiled, BF16), gradient_struct, gradient_struct, small_struct,
+            small_struct, small_struct, half_struct, flat_struct, struct((rows, 128), F32),
+            whole_struct, half_struct, struct(tiled, BF16), gradient_struct, gradient_struct,
+            gradient_struct, gradient_struct, small_struct,
         ],
         in_specs=[SMEM, SMEM, VMEM, VMEM, HBM, HBM, HBM, ANY, HBM, ANY],
-        out_specs=[VMEM, VMEM] + [HBM] * 11 + [VMEM],
+        out_specs=[VMEM, VMEM] + [HBM] * 10 + [VMEM],
         scratch_shapes=[
             pltpu.VMEM((width, hidden), BF16),
             pltpu.VMEM((hidden, width), BF16),
@@ -654,38 +636,21 @@
             pltpu.VMEM((len(OFFSETS) * frames, frames), BF16),
             pltpu.VMEM(gradient, BF16),
             pltpu.VMEM(gradient, BF16),
-            pltpu.SemaphoreType.DMA((10, 2)),
-            pltpu.SemaphoreType.DMA((2, half)),
+            pltpu.VMEM(gradient, BF16),
+            pltpu.VMEM(gradient, BF16),
+            pltpu.SemaphoreType.DMA((9, 2)),
+            pltpu.SemaphoreType.DMA((half,)),
+            pltpu.SemaphoreType.DMA((3, 8)),
         ],
-        compiler_params=params(46),
-        cost_estimate=cost(9 * product, 24 << 20),
+        compiler_params=params(),
+        cost_estimate=cost(11 * product, 24 << 20),
         name="main",
     )(
         sec, valid, own_small, got_small, tokens, out_cotangent, up_own, up_got, down_own, down_got
     )
     got1 = lax.ppermute(send1, "section", swap)
+    got0 = lax.ppermute(send0, "section", swap)
     got_out = lax.ppermute(out_send, "section", swap)
-
-    tile_spec = pl.BlockSpec((1, rows, TILE), lambda j, *_: (j, 0, 0))
-    keep0, send0 = pl.pallas_call(
-        weights_body,
-        grid_spec=pltpu.PrefetchScalarGridSpec(
-            num_scalar_prefetch=1,
-            grid=(tiles,),
-            in_specs=[full(rows, width), full(rows, width), tile_spec, tile_spec],
-            out_specs=[HBM, HBM],
-            scratch_shapes=[
-                pltpu.VMEM(gradient, BF16),
-                pltpu.VMEM(gradient, BF16),
-                pltpu.SemaphoreType.DMA((3, 8)),
-            ],
-        ),
-        out_shape=[gradient_struct, gradient_struct],
-        compiler_params=params(60),
-        cost_estimate=cost(2 * product, 12 << 20),
-        name="weights",
-    )(sec, gb0, adapted0, act0, gpre0)
-    got0 = lax.ppermute(send0, "section", swap)
 
     def last(first, count, sums, *others):
         def at(c):
@@ -721,12 +686,12 @@
             ),
             out_shape=[whole_struct, half_struct, small_struct],
             input_output_aliases={10 + i: i for i in range(len(others))},
-            compiler_params=params(LAST_MIB),
-            cost_estimate=cost(8 * product, 12 << 20),
-            name="last",
+            compiler_params=params(),
+            cost_estimate=cost(2 * count * product, 12 << 20),
         )(sec, gpre0, up_own, up_got, normed0, inv0, small0, gin1, tokens, sums, *others)
 
-    gin_own, gin_send, sums0 = last(0, half, sums0)
+    gin_own, gin_send, sums0 = last(0, 1, sums0)
+    gin_own, gin_send, sums0 = last(1, half - 1, sums0, gin_own, gin_send)
     got_gin = lax.ppermute(gin_send, "section", swap)
     got_sums = lax.ppermute(pick(first_section, sums1, sums0), "section", swap)
 

time: 125 us -> 122 us (0.976)
  local copies, waits for them, and re-layouts: 10.7 us -> 4.26 us
  other arithmetic: 4.3 us -> 7.87 us
  Pallas kernels: 61.1 us -> 64.3 us
  starting transfers between devices: 16.9 us -> 14.4 us
    pallas_call x1 -> x0, Pallas kernels: 7.6 us -> none  [local(): pl.pallas_call(weights_body, grid_spec=pltpu.PrefetchScalarGridSpec(num_s...]
    unnamed x52 -> x22, local copies, waits for them, and re-layouts: 7.94 us -> 1.45 us
    pallas_call x1 -> x2, Pallas kernels: 8.32 us -> 13.5 us  [last(): pl.pallas_call(functools.partial(last_body, first), grid_spec=pltpu.Prefe...]
    pallas_call x1, Pallas kernels: 32.4 us -> 35.9 us  [local(): pl.pallas_call(main_body, out_shape=[small_struct, small_struct, half_str...]
    add x2, other arithmetic: 1.6 us -> 3.08 us  [halved(): sum((part(piece, bit_of(spot, 0) * rows, rows) for piece in pairs[b]))]
    ppermute x1, starting transfers between devices: 1.49 us -> 0.2 us  [local(): got_sums = lax.ppermute(pick(first_section, sums1, sums0), 'section', swap)]
    ppermute x6, waiting for transfers between devices: 28 us -> 26.7 us  [exchanged(): return lax.ppermute(packet, PAIR, moves)]
    add x4, other arithmetic: 2.69 us -> 3.97 us  [halved(): part(totals[b], first, rows) + part(latest[b], bases[b] + first, rows)]
  transfers between devices with their start and end apart: 15 -> 15, of which waited for: 6 -> 6; matrix products, arithmetic and copies ran while one was open for 6% -> 9% of each run, Pallas kernels for 21% -> 20%
where the time goes in v4:
time: 122 us; the launch traced here: 121 us
  Pallas kernels  64.3 us (53%)
  waiting for transfers between devices  29.4 us (24%)
  starting transfers between devices  14.4 us (12%)
  other arithmetic  7.87 us (6%)
  local copies, waits for them, and re-layouts  4.26 us (3%)
    pallas_call x1, Pallas kernels, local(): pl.pallas_call(main_body, out_shape=[small_struct, small_struct, half_str...  35.9 us
    ppermute x6, waiting for transfers between devices, exchanged(): return lax.ppermute(packet, PAIR, moves)  26.7 us
    pallas_call x2, Pallas kernels, last(): pl.pallas_call(functools.partial(last_body, first), grid_spec=pltpu.Prefe...  13.5 us
    ppermute x6, starting transfers between devices, exchanged(): return lax.ppermute(packet, PAIR, moves)  11.8 us
    pallas_call x2, Pallas kernels, split(): pl.pallas_call(functools.partial(split_body, share), out_shape=struct((ro...  6.02 us
    pallas_call x4, Pallas kernels, pack(): pl.pallas_call(functools.partial(pack_body, step, share), out_shape=outs,...  5.3 us
    add x4, other arithmetic, halved(): part(totals[b], first, rows) + part(latest[b], bases[b] + first, rows)  3.97 us
    add x2, other arithmetic, halved(): sum((part(piece, bit_of(spot, 0) * rows, rows) for piece in pairs[b]))  3.08 us
  transfers between devices with their start and end apart: 15, of which 6 were waited for; matrix products, arithmetic and copies ran while one was open for 9% of the time, Pallas kernels for 20%

profile of v4, /device:TPU:0, one launch (start us, length us, event | category | flops | bytes accessed | tf_op | source)
XLA Modules:
  0.0 121.2 jit_solution(9522359583317005448)
XLA Ops:
  0.6 0.6 collective-permute-start.1
  1.2 0.1 collective-permute-start.2
  1.3 2.4 %prep.1 = (f32[24,512]{1,0:T(8,128)}, f32[24,512]{1,0:T(8,128)}) custom-call(s32[1]{0:T(128)} %bitcast.sec, s32[8]{0:T(128)} %speaker.9, f32[7,1,512]{2,1,0:T(1,128)} %bitcast.24, f32[1,512]{1,0:T(1,128)} %conv.1, f32[1,1536]{1,0:T(1,128)} %upb.1, f32[1,512]{1,0:T(1,128)} %downb.1, f32[1,512]{1,0:T(1,128)} %gain.1, f32[1,2560,512]{2,1,0:T(8,128)} %scale_hbm.1, ...), custom_call_target="tpu_custom_call" | custom-call | tf_op jit(solution)/shard_map/prep/pallas_call | solution.py:574
  3.7 0.5 collective-permute-start
  4.2 2.7 %collective-permute-done.got_small = f32[24,512]{1,0:T(8,128)} collective-permute-done((f32[24,512]{1,0:T(8,128)}, f32[24,512]{1,0:T(8,128)}, u32[]{:S(2)}, u32[]{:S(2)}) %collective-permute-start) | collective-permute-done | bytes 49184 | tf_op jit(solution)/shard_map/ppermute | solution.py:586
  6.9 35.9 %main.1 = (f32[24,512]{1,0:T(8,128)}, f32[24,512]{1,0:T(8,128)}, bf16[4,256,512]{2,1,0:T(8,128)(2,1)}, bf16[1024,512]{1,0:T(8,128)(2,1)}, f32[1024,128]{1,0:T(8,...) custom-call(s32[1]{0:T(128)} %bitcast.sec, ...), custom_call_target="tpu_custom_call" | custom-call | flops 17716740096 | bytes 25165824 | tf_op jit(solution)/shard_map/main/pallas_call | solution.py:605
  42.8 0.7 collective-permute-start.7
  43.5 0.1 collective-permute-start.5
  43.5 5.1 %shard_map.212 = (bf16[8,256,512]{2,1,0:T(8,128)(2,1)}, bf16[4,256,512]{2,1,0:T(8,128)(2,1)}, f32[24,512]{1,0:T(8,128)}) custom-call(s32[1]{0:T(128)} %bitcast.sec, bf16[3,1024,512]{2,1,0:T(8,128)(2,1)} %get-tuple-element.55.gpre, bf16[512,1536]{1,0:T(8,128)(2,1)} %bitcast.31, bf16[512,1536]{1,0:T(8,128)(2,1)} %collective-permute-done.1.up_got, ...), custom_call_target="tpu_custom_call" | custom-call | flops 3221225472 | bytes 12582912 | tf_op jit(solution)/shard_map/pallas_call | solution.py:659
  48.7 0.0 copy-start.3
  48.7 1.4 %copy-done.3 = bf16[16,96,512]{2,1,0:T(8,128)(2,1)S(1)} copy-done((bf16[16,96,512]{2,1,0:T(8,128)(2,1)S(1)}, bf16[16,96,512]{2,1,0:T(8,128)(2,1)}, u32[]{:S(2)}) %copy-start.3) | copy-done | bytes 1572888
  50.1 3.0 %shard_map.215 = bf16[768,512]{1,0:T(8,128)(2,1)} custom-call(s32[1]{0:T(128)} %bitcast.sec, s32[1]{0:T(128)} %bitcast.8.place, bf16[1536,512]{1,0:T(8,128)(2,1)S(1)} %bitcast.23, bf16[1536,512]{1,0:T(8,128)(2,1)} %bitcast.12.got), custom_call_target="tpu_custom_call" | custom-call | bytes 4194304 | tf_op jit(solution)/shard_map/pallas_call | solution.py:728
  53.1 2.7 %collective-permute-start.8 = (bf16[768,512]{1,0:T(8,128)(2,1)}, bf16[768,512]{1,0:T(8,128)(2,1)}, u32[]{:S(2)}, u32[]{:S(2)}) collective-permute-start(bf16[768,512]{1,0:T(8,128)(2,1)} %shard_map.215), channel_id=1, source_target_pairs={{0,1},{1,0},{2,3},{3,2},{4,5},{5,4},{6,7},{7,6},{8,9},{9,8},{10,11... | collective-permute-start | bytes 2359304 | tf_op jit(solution)/shard_map/ppermute | solution.py:718
  55.9 3.0 %shard_map.214 = bf16[768,512]{1,0:T(8,128)(2,1)} custom-call(s32[1]{0:T(128)} %bitcast.sec, s32[1]{0:T(128)} %bitcast.8.place, bf16[1536,512]{1,0:T(8,128)(2,1)S(1)} %bitcast.20, bf16[1536,512]{1,0:T(8,128)(2,1)} %bitcast.10.got), custom_call_target="tpu_custom_call" | custom-call | bytes 4194304 | tf_op jit(solution)/shard_map/pallas_call | solution.py:728
  58.9 0.1 collective-permute-start.6
  59.0 8.3 %shard_map.213 = (bf16[8,256,512]{2,1,0:T(8,128)(2,1)}, bf16[4,256,512]{2,1,0:T(8,128)(2,1)}, f32[24,512]{1,0:T(8,128)}) custom-call(s32[1]{0:T(128)} %bitcast.sec, bf16[3,1024,512]{2,1,0:T(8,128)(2,1)} %get-tuple-element.55.gpre, bf16[512,1536]{1,0:T(8,128)(2,1)} %bitcast.32, ...), custom_call_target="tpu_custom_call", output_to_operand_aliasing={{0}: (10, {}), {1}: (11, {})} | custom-call | flops 9663676416 | bytes 12582912 | tf_op jit(solution)/shard_map/pallas_call | solution.py:659
  67.4 0.8 broadcast_select_fusion
  68.2 0.2 collective-permute-start.9
  68.4 1.7 %convert_add_fusion.total1 = f32[768,512]{1,0:T(8,128)S(1)} fusion(bf16[1536,512]{1,0:T(8,128)(2,1)} %bitcast.12.got, s32[]{:T(128)S(6)} %select_n.59, bf16[1536,512]{1,0:T(8,128)(2,1)} %bitcast.22), kind=kLoop, calls=%fused_computation | loop fusion | flops 1179648 | bytes 3145732 | tf_op jit(solution)/shard_map/add | solution.py:750
  70.1 0.0 copy-start.4
  70.1 0.0 copy-start.5
  70.1 0.0 copy-start.6
  70.1 1.4 %convert_add_fusion.1.total0 = f32[768,512]{1,0:T(8,128)S(1)} fusion(bf16[1536,512]{1,0:T(8,128)(2,1)} %bitcast.10.got, s32[]{:T(128)S(6)} %select_n.59, bf16[1536,512]{1,0:T(8,128)(2,1)S(1)} %bitcast.21), kind=kLoop, calls=%fused_computation.1 | loop fusion | flops 1179648 | bytes 3145732 | tf_op jit(solution)/shard_map/add | solution.py:750
  71.5 0.0 collective-permute-done.8.refs_1_
  71.6 3.0 %collective-permute-done.6.refs_0_ = bf16[768,512]{1,0:T(8,128)(2,1)} collective-permute-done((bf16[768,512]{1,0:T(8,128)(2,1)}, bf16[768,512]{1,0:T(8,128)(2,1)}, u32[]{:S(2)}, u32[]{:S(2)}) %collective-permute-start.6) | collective-permute-done | bytes 786464 | tf_op jit(solution)/shard_map/ppermute | solution.py:718
  74.6 2.6 %shard_map.216 = (bf16[800,512]{1,0:T(8,128)(2,1)}, f32[16,512]{1,0:T(8,128)S(1)}) custom-call(s32[1]{0:T(128)} %bitcast.sec, s32[1]{0:T(128)} %bitcast.8.place, s32[8]{0:T(128)S(1)} %copy-done.6, f32[768,512]{1,0:T(8,128)S(1)} %convert_add_fusion.1.total0, f32[768,512]{1,0:T(8,128)S(1)} %convert_add_fusion.total1, ...), custom_call_target="tpu_custom_call" | custom-call | bytes 2097152 | tf_op jit(solution)/shard_map/pallas_call | solution.py:759
  77.2 2.0 %collective-permute-start.10 = (bf16[800,512]{1,0:T(8,128)(2,1)}, bf16[800,512]{1,0:T(8,128)(2,1)}, u32[]{:S(2)}, u32[]{:S(2)}) collective-permute-start(bf16[800,512]{1,0:T(8,128)(2,1)} %get-tuple-element.72.refs_1_), channel_id=1, source_target_pairs={{0,2},{1,3},{2,0},{3,1},{4,6},{5,7},{6,4},{7,5},{8,10},{9,11},{10,... | collective-permute-start | bytes 2457608 | tf_op jit(solution)/shard_map/ppermute | solution.py:718
  79.2 0.0 collective-permute-start.3
  79.2 0.5 collective-permute-start.4
  79.7 1.1 convert_add_fusion.2.total1
  80.8 1.4 %convert_add_fusion.3.total0 = f32[384,512]{1,0:T(8,128)S(1)} fusion(f32[768,512]{1,0:T(8,128)S(1)} %convert_add_fusion.1.total0, s32[]{:T(128)S(6)} %select_n.61, bf16[768,512]{1,0:T(8,128)(2,1)} %collective-permute-done.6.refs_0_), kind=kLoop, calls=%fused_computation.5 | loop fusion | flops 393216 | bytes 1966084 | tf_op jit(solution)/shard_map/add | solution.py:775
  82.2 7.6 %collective-permute-done.10.refs_0_ = bf16[800,512]{1,0:T(8,128)(2,1)} collective-permute-done((bf16[800,512]{1,0:T(8,128)(2,1)}, bf16[800,512]{1,0:T(8,128)(2,1)}, u32[]{:S(2)}, u32[]{:S(2)}) %collective-permute-start.10) | collective-permute-done | bytes 819232 | tf_op jit(solution)/shard_map/ppermute | solution.py:718
  89.8 1.5 %shard_map.217 = (bf16[432,512]{1,0:T(8,128)(2,1)S(1)}, f32[16,512]{1,0:T(8,128)S(1)}) custom-call(s32[1]{0:T(128)} %bitcast.sec, s32[1]{0:T(128)} %bitcast.8.place, s32[8]{0:T(128)S(1)} %copy-done.6, f32[384,512]{1,0:T(8,128)S(1)} %convert_add_fusion.3.total0, f32[384,512]{1,0:T(8,128)S(1)} %convert_add_fusion.2.total1, ...), custom_call_target="tpu_custom_call" | custom-call | bytes 2097152 | tf_op jit(solution)/shard_map/pallas_call | solution.py:759
  91.4 2.1 %collective-permute-start.11 = (bf16[432,512]{1,0:T(8,128)(2,1)S(1)}, bf16[432,512]{1,0:T(8,128)(2,1)S(1)}, u32[]{:S(2)}, u32[]{:S(2)}) collective-permute-start(bf16[432,512]{1,0:T(8,128)(2,1)S(1)} %get-tuple-element.74.refs_1_), channel_id=1, source_target_pairs={{0,4},{1,5},{2,6},{3,7},{4,0},{5,1},{6,2},{7,3},{8,12},{9,13},{10,... | collective-permute-start | bytes 1327112 | tf_op jit(solution)/shard_map/ppermute | solution.py:718
  93.5 1.4 %convert_add_fusion.4 = (f32[192,512]{1,0:T(8,128)S(1)}, f32[192,512]{1,0:T(8,128)S(1)}) fusion(f32[384,512]{1,0:T(8,128)} %copy-done, s32[]{:T(128)S(6)} %select_n.63, bf16[800,512]{1,0:T(8,128)(2,1)} %collective-permute-done.10.refs_0_, s32[]{:T(128)S(6)} %select_n.69, s32[]{:T(128)S(6)} %select_n.66, f32[384,512]{1,0:T(8,128)S(1)} %convert_add_fusion.3.total0), kind=kLoop, calls=%fused_computation.6 | loop fusion | flops 393216 | bytes 1966092 | tf_op jit(solution)/shard_map/add | solution.py:775
  95.0 4.9 %collective-permute-done.11.refs_0_ = bf16[432,512]{1,0:T(8,128)(2,1)S(1)} collective-permute-done((bf16[432,512]{1,0:T(8,128)(2,1)S(1)}, bf16[432,512]{1,0:T(8,128)(2,1)S(1)}, u32[]{:S(2)}, u32[]{:S(2)}) %collective-permute-start.11) | collective-permute-done | bytes 442400 | tf_op jit(solution)/shard_map/ppermute | solution.py:718
  99.8 0.6 shard_map.218
  100.4 3.1 %collective-permute-start.12 = (bf16[272,512]{1,0:T(8,128)(2,1)S(1)}, bf16[272,512]{1,0:T(8,128)(2,1)S(1)}, u32[]{:S(2)}, u32[]{:S(2)}) collective-permute-start(bf16[272,512]{1,0:T(8,128)(2,1)S(1)} %get-tuple-element.76.refs_1_), channel_id=1, source_target_pairs={{0,8},{1,9},{2,10},{3,11},{4,12},{5,13},{6,14},{7,15},{8,0},{9,1},... | collective-permute-start | bytes 835592 | tf_op jit(solution)/shard_map/ppermute | solution.py:718
  103.5 1.5 %bitcast_dynamic-update-slice_fusion.1 = bf16[1,8,256,512]{3,2,1,0:T(8,128)(2,1)S(1)} fusion(bf16[1,8,256,512]{3,2,1,0:T(8,128)(2,1)S(1)} %bitcast.25, s32[]{:T(128)S(6)} %select_n.57, bf16[4,256,512]{2,1,0:T(8,128)(2,1)} %collective-permute-done.3), kind=kLoop, calls=%fused_computation.3 | loop fusion | bytes 2097156 | tf_op jit(solution)/shard_map/dynamic_update_slice | solution.py:699
  105.0 0.0 copy-start.8
  105.0 0.1 convert_add_fusion.6
  105.1 9.0 %collective-permute-done.12.refs_0_ = bf16[272,512]{1,0:T(8,128)(2,1)S(1)} collective-permute-done((bf16[272,512]{1,0:T(8,128)(2,1)S(1)}, bf16[272,512]{1,0:T(8,128)(2,1)S(1)}, u32[]{:S(2)}, u32[]{:S(2)}) %collective-permute-start.12) | collective-permute-done | bytes 278560 | tf_op jit(solution)/shard_map/ppermute | solution.py:718
  114.1 0.6 shard_map.219
  114.7 1.6 %collective-permute-start.13 = (bf16[144,512]{1,0:T(8,128)(2,1)S(1)}, bf16[144,512]{1,0:T(8,128)(2,1)S(1)}, u32[]{:S(2)}, u32[]{:S(2)}) collective-permute-start(bf16[144,512]{1,0:T(8,128)(2,1)S(1)} %get-tuple-element.78.before), channel_id=1, source_target_pairs={{0,1},{1,0},{2,3},{3,2},{4,5},{5,4},{6,7},{7,6},{8,9},{9,8},{10,11... | collective-permute-start | bytes 442376 | tf_op jit(solution)/shard_map/ppermute | solution.py:718
  116.3 1.3 %bitcast_dynamic-update-slice_fusion = bf16[1,8,256,512]{3,2,1,0:T(8,128)(2,1)S(1)} fusion(bf16[1,8,256,512]{3,2,1,0:T(8,128)(2,1)S(1)} %bitcast.26, s32[]{:T(128)S(6)} %select_n.57, bf16[4,256,512]{2,1,0:T(8,128)(2,1)} %collective-permute-done.4), kind=kLoop, calls=%fused_computation.2 | loop fusion | bytes 2097156 | tf_op jit(solution)/shard_map/dynamic_update_slice | solution.py:699
  117.7 0.0 copy-start.10
  117.7 2.2 %collective-permute-done.13.after = bf16[144,512]{1,0:T(8,128)(2,1)S(1)} collective-permute-done((bf16[144,512]{1,0:T(8,128)(2,1)S(1)}, bf16[144,512]{1,0:T(8,128)(2,1)S(1)}, u32[]{:S(2)}, u32[]{:S(2)}) %collective-permute-start.13) | collective-permute-done | bytes 147488 | tf_op jit(solution)/shard_map/ppermute | solution.py:718
  119.9 1.2 finish.1
  (24 shorter events, 0.1 us)
Async XLA Ops:
  0.6 6.3 %collective-permute-start.1 = (bf16[512,1536]{1,0:T(8,128)(2,1)}, bf16[512,1536]{1,0:T(8,128)(2,1)}, u32[]{:S(2)}, u32[]{:S(2)}) collective-permute-start(bf16[512,1536]{1,0:T(8,128)(2,1)} %bitcast.29), channel_id=1, source_target_pairs={{0,16},{16,0},{1,17},{17,1},{2,18},{18,2},{3,19},{19,3},{4,20},{20... | collective-permute-start | bytes 4718600 | tf_op jit(solution)/shard_map/ppermute | solution.py:588
  1.2 5.7 %collective-permute-start.2 = (bf16[1536,512]{1,0:T(8,128)(2,1)}, bf16[1536,512]{1,0:T(8,128)(2,1)}, u32[]{:S(2)}, u32[]{:S(2)}) collective-permute-start(bf16[1536,512]{1,0:T(8,128)(2,1)} %bitcast.27), channel_id=1, source_target_pairs={{0,16},{16,0},{1,17},{17,1},{2,18},{18,2},{3,19},{19,3},{4,20},{20... | collective-permute-start | bytes 4718600 | tf_op jit(solution)/shard_map/ppermute | solution.py:589
  3.7 3.2 %collective-permute-start = (f32[24,512]{1,0:T(8,128)}, f32[24,512]{1,0:T(8,128)}, u32[]{:S(2)}, u32[]{:S(2)}) collective-permute-start(f32[24,512]{1,0:T(8,128)} %get-tuple-element.52), channel_id=1, source_target_pairs={{0,16},{16,0},{1,17},{17,1},{2,18},{18,2},{3,19},{19,3},{4,20},{20... | collective-permute-start | bytes 147464 | tf_op jit(solution)/shard_map/ppermute | solution.py:586
  42.8 5.9 %collective-permute-start.7 = (bf16[16,96,512]{2,1,0:T(8,128)(2,1)}, bf16[16,96,512]{2,1,0:T(8,128)(2,1)}, u32[]{:S(2)}, u32[]{:S(2)}) collective-permute-start(bf16[16,96,512]{2,1,0:T(8,128)(2,1)} %get-tuple-element.69), channel_id=1, source_target_pairs={{0,16},{16,0},{1,17},{17,1},{2,18},{18,2},{3,19},{19,3},{4,20},{20... | collective-permute-start | bytes 4718600 | tf_op jit(solution)/shard_map/ppermute | solution.py:651
  43.5 12.4 %collective-permute-start.5 = (bf16[16,96,512]{2,1,0:T(8,128)(2,1)}, bf16[16,96,512]{2,1,0:T(8,128)(2,1)}, u32[]{:S(2)}, u32[]{:S(2)}) collective-permute-start(bf16[16,96,512]{2,1,0:T(8,128)(2,1)} %get-tuple-element.67), channel_id=1, source_target_pairs={{0,16},{16,0},{1,17},{17,1},{2,18},{18,2},{3,19},{19,3},{4,20},{20... | collective-permute-start | bytes 4718600 | tf_op jit(solution)/shard_map/ppermute | solution.py:652
  48.7 1.4 %copy-start.3 = (bf16[16,96,512]{2,1,0:T(8,128)(2,1)S(1)}, bf16[16,96,512]{2,1,0:T(8,128)(2,1)}, u32[]{:S(2)}) copy-start(bf16[16,96,512]{2,1,0:T(8,128)(2,1)} %get-tuple-element.68) | copy-start | bytes 4718596
  50.1 5.8 %copy-start.1 = (bf16[16,96,512]{2,1,0:T(8,128)(2,1)S(1)}, bf16[16,96,512]{2,1,0:T(8,128)(2,1)}, u32[]{:S(2)}) copy-start(bf16[16,96,512]{2,1,0:T(8,128)(2,1)} %get-tuple-element.66) | copy-start | bytes 4718596
  53.1 18.4 %collective-permute-start.8 = (bf16[768,512]{1,0:T(8,128)(2,1)}, bf16[768,512]{1,0:T(8,128)(2,1)}, u32[]{:S(2)}, u32[]{:S(2)}) collective-permute-start(bf16[768,512]{1,0:T(8,128)(2,1)} %shard_map.215), channel_id=1, source_target_pairs={{0,1},{1,0},{2,3},{3,2},{4,5},{5,4},{6,7},{7,6},{8,9},{9,8},{10,11... | collective-permute-start | bytes 2359304 | tf_op jit(solution)/shard_map/ppermute | solution.py:718
  58.9 15.7 %collective-permute-start.6 = (bf16[768,512]{1,0:T(8,128)(2,1)}, bf16[768,512]{1,0:T(8,128)(2,1)}, u32[]{:S(2)}, u32[]{:S(2)}) collective-permute-start(bf16[768,512]{1,0:T(8,128)(2,1)} %shard_map.214), channel_id=1, source_target_pairs={{0,1},{1,0},{2,3},{3,2},{4,5},{5,4},{6,7},{7,6},{8,9},{9,8},{10,11... | collective-permute-start | bytes 2359304 | tf_op jit(solution)/shard_map/ppermute | solution.py:718
  68.2 1.9 %copy-start.2 = (bf16[16,96,512]{2,1,0:T(8,128)(2,1)S(1)}, bf16[16,96,512]{2,1,0:T(8,128)(2,1)}, u32[]{:S(2)}) copy-start(bf16[16,96,512]{2,1,0:T(8,128)(2,1)} %get-tuple-element.66) | copy-start | bytes 4718596
  68.2 3.3 %collective-permute-start.9 = (f32[24,512]{1,0:T(8,128)S(1)}, f32[24,512]{1,0:T(8,128)S(1)}, u32[]{:S(2)}, u32[]{:S(2)}) collective-permute-start(f32[24,512]{1,0:T(8,128)S(1)} %broadcast_select_fusion), channel_id=1, source_target_pairs={{0,16},{16,0},{1,17},{17,1},{2,18},{18,2},{3,19},{19,3},{4,20},{20... | collective-permute-start | bytes 147464 | tf_op jit(solution)/shard_map/ppermute | solution.py:696
  70.1 4.5 %copy-start.4 = (f32[24,512]{1,0:T(8,128)S(1)}, f32[24,512]{1,0:T(8,128)}, u32[]{:S(2)}) copy-start(f32[24,512]{1,0:T(8,128)} %get-tuple-element.71.refs_3_) | copy-start | bytes 147460
  70.1 4.5 %copy-start.5 = (f32[24,512]{1,0:T(8,128)S(1)}, f32[24,512]{1,0:T(8,128)}, u32[]{:S(2)}) copy-start(f32[24,512]{1,0:T(8,128)} %get-tuple-element.70.refs_2_) | copy-start | bytes 147460
  70.1 4.5 %copy-start.6 = (s32[8]{0:T(128)S(1)}, s32[8]{0:T(128)}, u32[]{:S(2)}) copy-start(s32[8]{0:T(128)} %speaker.9) | copy-start | bytes 100
  77.2 12.7 %collective-permute-start.10 = (bf16[800,512]{1,0:T(8,128)(2,1)}, bf16[800,512]{1,0:T(8,128)(2,1)}, u32[]{:S(2)}, u32[]{:S(2)}) collective-permute-start(bf16[800,512]{1,0:T(8,128)(2,1)} %get-tuple-element.72.refs_1_), channel_id=1, source_target_pairs={{0,2},{1,3},{2,0},{3,1},{4,6},{5,7},{6,4},{7,5},{8,10},{9,11},{10,... | collective-permute-start | bytes 2457608 | tf_op jit(solution)/shard_map/ppermute | solution.py:718
  79.2 24.3 %collective-permute-start.3 = (bf16[4,256,512]{2,1,0:T(8,128)(2,1)}, bf16[4,256,512]{2,1,0:T(8,128)(2,1)}, u32[]{:S(2)}, u32[]{:S(2)}) collective-permute-start(bf16[4,256,512]{2,1,0:T(8,128)(2,1)} %get-tuple-element.54), channel_id=1, source_target_pairs={{0,16},{16,0},{1,17},{17,1},{2,18},{18,2},{3,19},{19,3},{4,20},{20... | collective-permute-start | bytes 3145736 | tf_op jit(solution)/shard_map/ppermute | solution.py:653
  79.2 37.1 %collective-permute-start.4 = (bf16[4,256,512]{2,1,0:T(8,128)(2,1)}, bf16[4,256,512]{2,1,0:T(8,128)(2,1)}, u32[]{:S(2)}, u32[]{:S(2)}) collective-permute-start(bf16[4,256,512]{2,1,0:T(8,128)(2,1)} %get-tuple-element.65), channel_id=1, source_target_pairs={{0,16},{16,0},{1,17},{17,1},{2,18},{18,2},{3,19},{19,3},{4,20},{20... | collective-permute-start | bytes 3145736 | tf_op jit(solution)/shard_map/ppermute | solution.py:695
  80.8 10.5 %copy-start = (f32[384,512]{1,0:T(8,128)}, f32[384,512]{1,0:T(8,128)S(1)}, u32[]{:S(2)}) copy-start(f32[384,512]{1,0:T(8,128)S(1)} %convert_add_fusion.2.total1) | copy-start | bytes 2359300
  91.4 8.4 %collective-permute-start.11 = (bf16[432,512]{1,0:T(8,128)(2,1)S(1)}, bf16[432,512]{1,0:T(8,128)(2,1)S(1)}, u32[]{:S(2)}, u32[]{:S(2)}) collective-permute-start(bf16[432,512]{1,0:T(8,128)(2,1)S(1)} %get-tuple-element.74.refs_1_), channel_id=1, source_target_pairs={{0,4},{1,5},{2,6},{3,7},{4,0},{5,1},{6,2},{7,3},{8,12},{9,13},{10,... | collective-permute-start | bytes 1327112 | tf_op jit(solution)/shard_map/ppermute | solution.py:718
  93.5 10.0 %copy-start.7 = (bf16[8,256,512]{2,1,0:T(8,128)(2,1)S(1)}, bf16[8,256,512]{2,1,0:T(8,128)(2,1)}, u32[]{:S(2)}) copy-start(bf16[8,256,512]{2,1,0:T(8,128)(2,1)} %get-tuple-element.53) | copy-start | bytes 6291460
  100.4 13.7 %collective-permute-start.12 = (bf16[272,512]{1,0:T(8,128)(2,1)S(1)}, bf16[272,512]{1,0:T(8,128)(2,1)S(1)}, u32[]{:S(2)}, u32[]{:S(2)}) collective-permute-start(bf16[272,512]{1,0:T(8,128)(2,1)S(1)} %get-tuple-element.76.refs_1_), channel_id=1, source_target_pairs={{0,8},{1,9},{2,10},{3,11},{4,12},{5,13},{6,14},{7,15},{8,0},{9,1},... | collective-permute-start | bytes 835592 | tf_op jit(solution)/shard_map/ppermute | solution.py:718
  103.5 12.8 %copy-start.9 = (bf16[8,256,512]{2,1,0:T(8,128)(2,1)S(1)}, bf16[8,256,512]{2,1,0:T(8,128)(2,1)}, u32[]{:S(2)}) copy-start(bf16[8,256,512]{2,1,0:T(8,128)(2,1)} %get-tuple-element.64) | copy-start | bytes 6291460
  105.0 12.6 %copy-start.8 = (bf16[1,8,256,512]{3,2,1,0:T(8,128)(2,1)}, bf16[1,8,256,512]{3,2,1,0:T(8,128)(2,1)S(1)}, u32[]{:S(2)}) copy-start(bf16[1,8,256,512]{3,2,1,0:T(8,128)(2,1)S(1)} %bitcast_dynamic-update-slice_fusion.1) | copy-start | bytes 6291460
  114.7 5.2 %collective-permute-start.13 = (bf16[144,512]{1,0:T(8,128)(2,1)S(1)}, bf16[144,512]{1,0:T(8,128)(2,1)S(1)}, u32[]{:S(2)}, u32[]{:S(2)}) collective-permute-start(bf16[144,512]{1,0:T(8,128)(2,1)S(1)} %get-tuple-element.78.before), channel_id=1, source_target_pairs={{0,1},{1,0},{2,3},{3,2},{4,5},{5,4},{6,7},{7,6},{8,9},{9,8},{10,11... | collective-permute-start | bytes 442376 | tf_op jit(solution)/shard_map/ppermute | solution.py:718
  116.3 3.6 %collective-permute-start.14 = (f32[96,512]{1,0:T(8,128)S(1)}, f32[96,512]{1,0:T(8,128)S(1)}, u32[]{:S(2)}, u32[]{:S(2)}) collective-permute-start(f32[96,512]{1,0:T(8,128)S(1)} %get-tuple-element.81), channel_id=1, source_target_pairs={{0,16},{16,0},{1,17},{17,1},{2,18},{18,2},{3,19},{19,3},{4,20},{20... | collective-permute-start | bytes 589832 | tf_op jit(solution)/shard_map/ppermute | solution.py:781
  117.7 3.5 %copy-start.10 = (bf16[1,8,256,512]{3,2,1,0:T(8,128)(2,1)}, bf16[1,8,256,512]{3,2,1,0:T(8,128)(2,1)S(1)}, u32[]{:S(2)}) copy-start(bf16[1,8,256,512]{3,2,1,0:T(8,128)(2,1)S(1)} %bitcast_dynamic-update-slice_fusion) | copy-start | bytes 6291460

commit v5 on v4

--- a/solution.py
+++ b/solution.py
@@ -413,13 +413,17 @@
     return (spot[1] >> (low if low == high else pick(spot[0] == 0, low, high))) & 1
 
 
-GATHER = (1, 2, 3, 0)
+GATHER = (3, 2, 0, 1)
+
+
+def gather_bit(spot, hop):
+    return (spot[1] >> GATHER[hop]) & 1
 
 
 def gather_slot(spot):
     slot = 0
-    for i, step in enumerate(GATHER):
-        slot = slot + bit_of(spot, step) * (1 << i)
+    for hop in range(len(GATHER)):
+        slot = slot + gather_bit(spot, hop) * (1 << hop)
     return slot
 
 
@@ -446,93 +450,86 @@
         packet[part] = (kept[part].astype(F32) + came[part].astype(F32)).astype(BF16)
 
 
-def pack_body(step, share, sec, place, speaker, total0, total1, *refs):
+def second_body(share, sec, place, *refs):
     spot = (sec[0], place[0])
-    count = 8 >> step
-    rows = max(count, 1) * share
-    head = 2 * count * share
-    totals = (total0, total1)
-    if step == 1:
-        latest = [(refs[0], 0), (refs[1], 0)]
-        refs = refs[2:]
-    else:
-        latest = [(refs[0], 0), (refs[0], (16 >> step) * share)]
-    extra_in, refs = refs[:3], refs[3:]
-    packet, smalls_out = refs[:2]
+    sources, (packet, buffer, sems) = refs[:6], refs[6:]
+    rows = 4 * share
+    away = (1 - bit_of(spot, 1)) * rows
+    copies = []
+    for n, source in enumerate(sources):
+        first = away if n % 3 == 2 else away + bit_of(spot, 0) * 2 * rows
+        fetch(copies, source, pl.multiple_of(first, 32), rows, buffer.at[n], sems.at[n])
     for b in range(2):
-        source, base = latest[b]
-        if step < 4:
-            first = pl.multiple_of((1 - bit_of(spot, step)) * rows, 32)
-            away = totals[b][pl.ds(first, rows)] + source[pl.ds(base + first, rows)].astype(F32)
-            packet[b * rows : (b + 1) * rows] = away.astype(BF16)
-        else:
-            whole = totals[b][...] + source[base : base + rows].astype(F32)
-            for target, mine in ((refs[2], True), (refs[3], False)):
-
-                @pl.when((spot[0] == b) == mine)
-                def _():
-                    target[...] = whole
-
-    if step == 1:
-        sums0, sums1, got = extra_in
-        own = pick(spot[0] == 0, sums0[...], sums1[...])
-        other = got[...]
-        low = pick(spot[0] == 0, own[SCALE:], other[SCALE:])
-        high = pick(spot[0] == 0, other[SCALE:], own[SCALE:])
-        packet[head : head + 16] = jnp.concatenate([low, high], axis=0).astype(BF16)
-        width = own.shape[1]
-        lane = lax.broadcasted_iota(jnp.int32, (1, width), 1)
-        mine_lane = (lane >> 4) == gather_slot(spot)
-        which = ((lane >> 3) & 1) * 4 + (lane & 3)
-        code = jnp.zeros((1, width), jnp.int32)
-        for c in range(8):
-            code = jnp.where(mine_lane & (which == c), speaker[c], code)
-        smalls_out[...] = own[:SCALE] + other[:SCALE]
-        smalls_out[13:14] = (code >> 6).astype(F32)
-        smalls_out[14:15] = (code & 63).astype(F32)
-        tail = head + 16
-    else:
-        after, before, smalls_in = extra_in
-        size = 16 << (step - 2)
-        old_head = (16 >> step) * 2 * share
-        bit = bit_of(spot, GATHER[step - 2])
-        for source, side in ((before, bit), (after, 1 - bit)):
-            packet[pl.ds(pl.multiple_of(head + side * size, 16), size)] = source[
-                old_head : old_head + size
-            ]
-        smalls_out[...] = smalls_in[...] + after[old_head + size : old_head + size + 16].astype(F32)
-        tail = head + 2 * size
-    packet[tail : tail + 16] = smalls_out[...].astype(BF16)
-
-
-def finish_body(
-    sec, place, before, after, smalls_in, mine, got, scale, shift, up, down, taps, conv, upb, downb, gain,
-    rows_of,
-):
+        total = 0.0
+        for n in range(3 * b, 3 * b + 3):
+            copies[n].wait()
+            total = total + buffer[n].astype(F32)
+        packet[b * rows : (b + 1) * rows] = total.astype(BF16)
+
+
+def pack_body(step, share, sec, place, total0, total1, came, packet):
+    rows = (8 >> step) * share
+    first = pl.multiple_of((1 - bit_of((sec[0], place[0]), step)) * rows, 32)
+    for b, total in enumerate((total0, total1)):
+        latest = came[pl.ds(b * 2 * rows + first, rows)]
+        packet[b * rows : (b + 1) * rows] = (total[pl.ds(first, rows)] + latest.astype(F32)).astype(BF16)
+
+
+def share_body(share, sec, total0, total1, came, mine, away):
+    for b, total in enumerate((total0, total1)):
+        whole = total[...] + came[b * share : (b + 1) * share].astype(F32)
+        for target, stays in ((mine, True), (away, False)):
+
+            @pl.when((sec[0] == b) == stays)
+            def _():
+                target[...] = whole
+
+
+def begin_rows_body(sec, place, speaker, sums0, sums1, got, packet, smalls):
     spot = (sec[0], place[0])
+    first = spot[0] == 0
+    own = pick(first, sums0[...], sums1[...])
+    other = got[...]
+    low = pick(first, own[SCALE:], other[SCALE:])
+    high = pick(first, other[SCALE:], own[SCALE:])
+    packet[:16] = jnp.concatenate([low, high], axis=0).astype(BF16)
+    lane = lax.broadcasted_iota(jnp.int32, (1, own.shape[1]), 1)
+    here = (lane >> 4) == gather_slot(spot)
+    which = ((lane >> 3) & 1) * 4 + (lane & 3)
+    code = jnp.zeros(lane.shape, jnp.int32)
+    for c in range(8):
+        code = jnp.where(here & (which == c), speaker[c], code)
+    smalls[...] = own[:SCALE] + other[:SCALE]
+    smalls[13:14] = (code >> 6).astype(F32)
+    smalls[14:15] = (code & 63).astype(F32)
+    packet[16:32] = smalls[...].astype(BF16)
+
+
+def more_rows_body(hop, place, before, after, smalls_in, packet, smalls):
+    size = 16 << (hop - 1)
+    bit = gather_bit((0, place[0]), hop - 1)
+    for source, side in ((before, bit), (after, 1 - bit)):
+        packet[pl.ds(pl.multiple_of(side * size, 16), size)] = source[:size]
+    smalls[...] = smalls_in[...] + after[size:].astype(F32)
+    packet[2 * size :] = smalls[...].astype(BF16)
+
+
+def tables_body(place, before, after, smalls_in, scale, shift, taps, conv, upb, downb, gain, rows_of):
     size = rows_of.shape[0] // 2
-    bit = bit_of(spot, GATHER[3])
+    bit = gather_bit((0, place[0]), len(GATHER) - 1)
     for source, side in ((before, bit), (after, 1 - bit)):
         rows_of[pl.ds(pl.multiple_of(side * size, 16), size)] = source[:size]
-    first = spot[0] == 0
-    one, two = mine[...], got[...]
-    up_rows = up.shape[0]
-    ups = pick(first, one, two)
-    for j in range(3):
-        up[:, j * TILE : (j + 1) * TILE] = ups[j * up_rows : (j + 1) * up_rows]
-    down[...] = pick(first, two, one)
     total = smalls_in[...] + after[size:].astype(F32)
     owned = scale.shape[0]
     count = 2 * size
     who = total[13:14, :count] * 64.0 + total[14:15, :count]
-    wanted = lax.broadcasted_iota(jnp.int32, (owned, count), 0) + spot[1] * owned
+    wanted = lax.broadcasted_iota(jnp.int32, (owned, count), 0) + place[0] * owned
     hit = who == wanted.astype(F32)
     kind = (lax.broadcasted_iota(jnp.int32, (owned, count), 1) >> 2) & 1
     for k, out in enumerate((scale, shift)):
         out[...] = dot(jnp.where(hit & (kind == k), 1.0, 0.0).astype(BF16), rows_of[...], NN)
-    width = total.shape[1]
-    lanes = width // BLOCKS
-    turn = lax.rem(BLOCKS - spot[1], BLOCKS)
+    lanes = total.shape[1] // BLOCKS
+    turn = lax.rem(BLOCKS - place[0], BLOCKS)
     cut = pltpu.roll(total, turn * lanes, 1)[:, :lanes]
     for k in range(7):
         taps[k] = cut[k : k + 1]
@@ -541,6 +538,15 @@
     gain[...] = cut[GAIN : GAIN + 1]
     line = jnp.concatenate([total[UPB + k : UPB + k + 1] for k in range(3)], axis=1)
     upb[...] = pltpu.roll(line, turn * 3 * lanes, 1)[:, : 3 * lanes]
+
+
+def finish_body(sec, mine, got, up, down):
+    first = sec[0] == 0
+    rows = up.shape[0]
+    ups = pick(first, mine[...], got[...])
+    for j in range(3):
+        up[:, j * TILE : (j + 1) * TILE] = ups[j * rows : (j + 1) * rows]
+    down[...] = pick(first, got[...], mine[...])
 
 
 def struct(shape, dtype):
@@ -690,8 +696,7 @@
             cost_estimate=cost(2 * count * product, 12 << 20),
         )(sec, gpre0, up_own, up_got, normed0, inv0, small0, gin1, tokens, sums, *others)
 
-    gin_own, gin_send, sums0 = last(0, 1, sums0)
-    gin_own, gin_send, sums0 = last(1, half - 1, sums0, gin_own, gin_send)
+    gin_own, gin_send, sums0 = last(0, half, sums0)
     got_gin = lax.ppermute(gin_send, "section", swap)
     got_sums = lax.ppermute(pick(first_section, sums1, sums0), "section", swap)
 
@@ -722,86 +727,113 @@
     _, share, width = pairs[0][0].shape
     pairs = [[piece.reshape(-1, width) for piece in pair] for pair in pairs]
     spot = (sec[0], place[0])
-    rows = 8 * share
+    half_rows = 8 * share
 
     def split(b):
         return pl.pallas_call(
             functools.partial(split_body, share),
-            out_shape=struct((rows, width), BF16),
-            in_specs=[SMEM, SMEM, HBM, ANY],
+            out_shape=struct((half_rows, width), BF16),
+            in_specs=[SMEM, SMEM, HBM, HBM],
             out_specs=VMEM,
             scratch_shapes=[
-                pltpu.VMEM((rows, width), BF16),
-                pltpu.VMEM((rows, width), BF16),
+                pltpu.VMEM((half_rows, width), BF16),
+                pltpu.VMEM((half_rows, width), BF16),
                 pltpu.SemaphoreType.DMA((4, 2)),
             ],
-            compiler_params=params(6),
+            compiler_params=params(),
             cost_estimate=cost(0, 4 << 20),
         )(sec, place, *pairs[b])
 
     def part(array, first, count):
         return lax.dynamic_slice_in_dim(array, first, count, 0).astype(F32)
 
-    latest, totals = [None, None], [None, None]
     for b in (1, 0):
         packet = split(b)
-        latest[b] = exchanged(packet, 0)
-    for b in (1, 0):
-        totals[b] = sum(part(piece, bit_of(spot, 0) * rows, rows) for piece in pairs[b])
-
-    def pack(step, extra_in):
-        count = 8 >> step
-        length = 2 * count * share + (8 << step) + 16
-        outs = [struct((length, width), BF16), struct((SCALE, width), F32)]
-        if step == 4:
-            outs += [struct((share, width), F32)] * 2
-        operands = list(totals) + (latest if step == 1 else []) + extra_in
+        pairs[b].append(exchanged(packet, 0))
+
+    def small_call(body, outs, scalars, operands, scratch=(), specs=None, limit=8):
         return pl.pallas_call(
-            functools.partial(pack_body, step, share),
+            body,
             out_shape=outs,
-            in_specs=[SMEM, SMEM, SMEM] + [VMEM] * len(operands),
+            in_specs=[SMEM] * len(scalars) + (specs or [VMEM] * len(operands)),
             out_specs=[VMEM] * len(outs),
-            compiler_params=params(8),
+            scratch_shapes=scratch,
+            compiler_params=params(limit),
             cost_estimate=cost(0, 2 << 20),
-        )(sec, place, speaker, *operands)
-
-    packet, smalls = pack(1, [sums0, sums1, got_sums])
-    for step in range(1, 4):
-        got = exchanged(packet, step)
-        rows = (8 >> step) * share
-        first = bit_of(spot, step) * rows
-        bases = (0, 0) if step == 1 else (0, 2 * rows)
-        totals = [
-            part(totals[b], first, rows) + part(latest[b], bases[b] + first, rows) for b in range(2)
-        ]
-        latest = [got, got]
-        packet, smalls, *shares = pack(step + 1, [got, packet, smalls])
-    mine, away = shares
-    got = exchanged(packet, 0)
-    got_share = lax.ppermute(away, "section", [(0, 1), (1, 0)])
+        )(*scalars, *operands)
+
+    def row_outs(hop):
+        return [struct(((16 << hop) + 16, width), BF16), struct((SCALE, width), F32)]
+
+    rows_packet, smalls = small_call(begin_rows_body, row_outs(0), [sec, place, speaker], [sums0, sums1, got_sums])
+    for hop in range(len(GATHER)):
+        more = lax.ppermute(
+            rows_packet, "dp", [(i, i ^ (1 << GATHER[hop])) for i in range(BLOCKS)]
+        )
+        operands = [rows_packet, more, smalls]
+        if hop + 1 < len(GATHER):
+            rows_packet, smalls = small_call(
+                functools.partial(more_rows_body, hop + 1), row_outs(hop + 1), [place],
+                operands,
+            )
     owned = table_rows // BLOCKS
-    up_rows = width // BLOCKS
     lanes = width // BLOCKS
     one = struct((1, lanes), F32)
-    scale, shift, up, down, taps, conv, upb, downb, gain = pl.pallas_call(
-        finish_body,
-        out_shape=[
+    scale, shift, taps, conv, upb, downb, gain = small_call(
+        tables_body,
+        [
             struct((owned, width), F32),
             struct((owned, width), F32),
-            struct((up_rows, 3 * TILE), F32),
-            struct((share, width), F32),
             struct((7, 1, lanes), F32),
             one,
             struct((1, 3 * lanes), F32),
             one,
             one,
         ],
-        in_specs=[SMEM, SMEM] + [VMEM] * 5,
-        out_specs=[VMEM] * 9,
-        scratch_shapes=[pltpu.VMEM((16 * BLOCKS, width), BF16)],
-        compiler_params=params(8),
-        name="finish",
-    )(sec, place, packet, got, smalls, mine, got_share)
+        [place],
+        operands,
+        [pltpu.VMEM((16 * BLOCKS, width), BF16)],
+    )
+
+    totals, latest = None, None
+    for step in range(1, 4):
+        rows = (8 >> step) * share
+        first = bit_of(spot, step) * rows
+        packet_struct = [struct((2 * rows, width), BF16)]
+        if step == 1:
+            (packet,) = small_call(
+                functools.partial(second_body, share), packet_struct, [sec, place],
+                pairs[0] + pairs[1],
+                [pltpu.VMEM((6, rows, width), BF16), pltpu.SemaphoreType.DMA((6,))],
+                [HBM] * 6,
+                None,
+            )
+        else:
+            (packet,) = small_call(
+                functools.partial(pack_body, step, share), packet_struct, [sec, place],
+                totals + [latest],
+            )
+        got = exchanged(packet, step)
+        if step == 1:
+            start = bit_of(spot, 0) * 2 * rows + first
+            totals = [
+                part(keep, start, rows) + part(swapped, start, rows) + part(came, first, rows)
+                for keep, swapped, came in pairs
+            ]
+        else:
+            totals = [
+                part(totals[b], first, rows) + part(latest, 2 * b * rows + first, rows)
+                for b in range(2)
+            ]
+        latest = got
+    mine, away = small_call(
+        functools.partial(share_body, share), [struct((share, width), F32)] * 2, [sec],
+        totals + [latest],
+    )
+    got_share = lax.ppermute(away, "section", [(0, 1), (1, 0)])
+    up, down = small_call(
+        finish_body, [struct((width // BLOCKS, 3 * TILE), F32), struct((share, width), F32)], [sec], [mine, got_share]
+    )
     return (
         taps.transpose(1, 0, 2), conv, scale[None], shift[None], up[None], upb, down[None], downb, gain
     )

time: 122 us -> 126 us (1.033)
  waiting for transfers between devices: 29.4 us -> 38.7 us
  Pallas kernels: 64.3 us -> 59.5 us
  other arithmetic: 7.87 us -> 4.92 us
  starting transfers between devices: 14.4 us -> 15.8 us
  local copies, waits for them, and re-layouts: 4.26 us -> 5.58 us
    ppermute x0 -> x4, waiting for transfers between devices: none -> 10.6 us  [halved(): lax.ppermute(rows_packet, 'dp', [(i, i ^ 1 << GATHER[hop]) for i in range...]
    ppermute x6 -> x5, waiting for transfers between devices: 26.7 us -> 20.8 us  [exchanged(): return lax.ppermute(packet, PAIR, moves)]
    ppermute x0 -> x4, starting transfers between devices: none -> 5.57 us  [halved(): lax.ppermute(rows_packet, 'dp', [(i, i ^ 1 << GATHER[hop]) for i in range...]
    ppermute x6 -> x5, starting transfers between devices: 11.8 us -> 8.11 us  [exchanged(): return lax.ppermute(packet, PAIR, moves)]
    pallas_call x2 -> x1, Pallas kernels: 13.5 us -> 9.84 us  [last(): pl.pallas_call(functools.partial(last_body, first), grid_spec=pltpu.Prefe...]
    ppermute x1, waiting for transfers between devices: 0.01 us -> 3.3 us  [local(): got0 = lax.ppermute(send0, 'section', swap)]
    add x6 -> x4, other arithmetic: 7.05 us -> 4.1 us  [the longest x2 2.75 us: halved(): part(keep, start, rows) + part(swapped, start, rows)]
    unnamed x22 -> x14, local copies, waits for them, and re-layouts: 1.45 us -> 2.77 us
  transfers between devices with their start and end apart: 15 -> 18, of which waited for: 6 -> 9; matrix products, arithmetic and copies ran while one was open for 9% -> 6% of each run, Pallas kernels for 20% -> 18%
where the time goes in v5:
time: 126 us; the launch traced here: 125 us
  Pallas kernels  59.5 us (47%)
  waiting for transfers between devices  38.7 us (31%)
  starting transfers between devices  15.8 us (13%)
  local copies, waits for them, and re-layouts  5.58 us (4%)
  other arithmetic  4.92 us (4%)
    pallas_call x1, Pallas kernels, local(): pl.pallas_call(main_body, out_shape=[small_struct, small_struct, half_str...  35.9 us
    ppermute x5, waiting for transfers between devices, exchanged(): return lax.ppermute(packet, PAIR, moves)  20.8 us
    ppermute x4, waiting for transfers between devices, halved(): lax.ppermute(rows_packet, 'dp', [(i, i ^ 1 << GATHER[hop]) for i in range...  10.6 us
    pallas_call x1, Pallas kernels, last(): pl.pallas_call(functools.partial(last_body, first), grid_spec=pltpu.Prefe...  9.84 us
    ppermute x5, starting transfers between devices, exchanged(): return lax.ppermute(packet, PAIR, moves)  8.11 us
    pallas_call x10, Pallas kernels, small_call(): pl.pallas_call(body, out_shape=outs, in_specs=[SMEM] * len(scalars) + (sp...  6.46 us
    ppermute x4, starting transfers between devices, halved(): lax.ppermute(rows_packet, 'dp', [(i, i ^ 1 << GATHER[hop]) for i in range...  5.57 us
    pallas_call x2, Pallas kernels, split(): pl.pallas_call(functools.partial(split_body, share), out_shape=struct((ha...  4.94 us
  transfers between devices with their start and end apart: 18, of which 9 were waited for; matrix products, arithmetic and copies ran while one was open for 6% of the time, Pallas kernels for 18%

profile of v5, /device:TPU:0, one launch (start us, length us, event | category | flops | bytes accessed | tf_op | source)
XLA Modules:
  0.0 125.5 jit_solution(5467298600800463786)
XLA Ops:
  0.6 0.6 collective-permute-start.1
  1.2 0.1 collective-permute-start.2
  1.3 2.4 %prep.1 = (f32[24,512]{1,0:T(8,128)}, f32[24,512]{1,0:T(8,128)}) custom-call(s32[1]{0:T(128)} %bitcast.sec, s32[8]{0:T(128)} %speaker.3, f32[7,1,512]{2,1,0:T(1,128)} %bitcast.26, f32[1,512]{1,0:T(1,128)} %conv.1, f32[1,1536]{1,0:T(1,128)} %upb.1, f32[1,512]{1,0:T(1,128)} %downb.1, f32[1,512]{1,0:T(1,128)} %gain.1, f32[1,2560,512]{2,1,0:T(8,128)} %scale_hbm.1, ...), custom_call_target="tpu_custom_call" | custom-call | tf_op jit(solution)/shard_map/prep/pallas_call | solution.py:580
  3.7 0.5 collective-permute-start
  4.2 2.7 %collective-permute-done.got_small = f32[24,512]{1,0:T(8,128)} collective-permute-done((f32[24,512]{1,0:T(8,128)}, f32[24,512]{1,0:T(8,128)}, u32[]{:S(2)}, u32[]{:S(2)}) %collective-permute-start) | collective-permute-done | bytes 49184 | tf_op jit(solution)/shard_map/ppermute | solution.py:592
  6.9 35.9 %main.1 = (f32[24,512]{1,0:T(8,128)}, f32[24,512]{1,0:T(8,128)}, bf16[4,256,512]{2,1,0:T(8,128)(2,1)}, bf16[1024,512]{1,0:T(8,128)(2,1)}, f32[1024,128]{1,0:T(8,...) custom-call(s32[1]{0:T(128)} %bitcast.sec, ...), custom_call_target="tpu_custom_call" | custom-call | flops 17716740096 | bytes 25165824 | tf_op jit(solution)/shard_map/main/pallas_call | solution.py:611
  42.8 0.6 collective-permute-start.10
  43.4 0.1 collective-permute-start.12
  43.5 3.3 %collective-permute-done.10 = bf16[16,96,512]{2,1,0:T(8,128)(2,1)} collective-permute-done((bf16[16,96,512]{2,1,0:T(8,128)(2,1)}, bf16[16,96,512]{2,1,0:T(8,128)(2,1)}, u32[]{:S(2)}, u32[]{:S(2)}) %collective-permute-start.10) | collective-permute-done | bytes 1572896 | tf_op jit(solution)/shard_map/ppermute | solution.py:658
  46.8 2.5 %shard_map.218 = bf16[768,512]{1,0:T(8,128)(2,1)} custom-call(s32[1]{0:T(128)} %bitcast.sec, s32[1]{0:T(128)} %bitcast.8.place, bf16[1536,512]{1,0:T(8,128)(2,1)} %bitcast.23, bf16[1536,512]{1,0:T(8,128)(2,1)} %bitcast.13.got.refs_1_), custom_call_target="tpu_custom_call" | custom-call | bytes 4194304 | tf_op jit(solution)/shard_map/pallas_call | solution.py:733
  49.3 2.7 %collective-permute-start.11 = (bf16[768,512]{1,0:T(8,128)(2,1)}, bf16[768,512]{1,0:T(8,128)(2,1)}, u32[]{:S(2)}, u32[]{:S(2)}) collective-permute-start(bf16[768,512]{1,0:T(8,128)(2,1)} %shard_map.218), channel_id=1, source_target_pairs={{0,1},{1,0},{2,3},{3,2},{4,5},{5,4},{6,7},{7,6},{8,9},{9,8},{10,11... | collective-permute-start | bytes 2359304 | tf_op jit(solution)/shard_map/ppermute | solution.py:723
  52.0 2.5 %shard_map.219 = bf16[768,512]{1,0:T(8,128)(2,1)} custom-call(s32[1]{0:T(128)} %bitcast.sec, s32[1]{0:T(128)} %bitcast.8.place, bf16[1536,512]{1,0:T(8,128)(2,1)} %bitcast.20, bf16[1536,512]{1,0:T(8,128)(2,1)} %bitcast.15.got.refs_4_), custom_call_target="tpu_custom_call" | custom-call | bytes 4194304 | tf_op jit(solution)/shard_map/pallas_call | solution.py:733
  54.5 0.1 collective-permute-start.13
  54.6 0.2 collective-permute-start.3
  54.7 7.5 %collective-permute-done.11.refs_2_ = bf16[768,512]{1,0:T(8,128)(2,1)} collective-permute-done((bf16[768,512]{1,0:T(8,128)(2,1)}, bf16[768,512]{1,0:T(8,128)(2,1)}, u32[]{:S(2)}, u32[]{:S(2)}) %collective-permute-start.11) | collective-permute-done | bytes 786464 | tf_op jit(solution)/shard_map/ppermute | solution.py:723
  62.3 8.4 %collective-permute-done.13.refs_5_ = bf16[768,512]{1,0:T(8,128)(2,1)} collective-permute-done((bf16[768,512]{1,0:T(8,128)(2,1)}, bf16[768,512]{1,0:T(8,128)(2,1)}, u32[]{:S(2)}, u32[]{:S(2)}) %collective-permute-start.13) | collective-permute-done | bytes 786464 | tf_op jit(solution)/shard_map/ppermute | solution.py:723
  70.7 2.6 %shard_map.220 = bf16[768,512]{1,0:T(8,128)(2,1)} custom-call(s32[1]{0:T(128)} %bitcast.sec, s32[1]{0:T(128)} %bitcast.8.place, bf16[1536,512]{1,0:T(8,128)(2,1)} %bitcast.24, bf16[1536,512]{1,0:T(8,128)(2,1)} %bitcast.13.got.refs_1_, bf16[768,512]{1,0:T(8,128)(2,1)} %collective-permute-done.11.refs_2_, bf16[1536,512]{1,0:T(8,128)(2,1)} %bitcast.21, ...), custom_call_target="tpu_custom_call" | custom-call | bytes 2097152 | tf_op jit(solution)/shard_map/pallas_call | solution.py:755
  73.3 2.1 %collective-permute-start.14 = (bf16[768,512]{1,0:T(8,128)(2,1)}, bf16[768,512]{1,0:T(8,128)(2,1)}, u32[]{:S(2)}, u32[]{:S(2)}) collective-permute-start(bf16[768,512]{1,0:T(8,128)(2,1)} %shard_map.220), channel_id=1, source_target_pairs={{0,2},{1,3},{2,0},{3,1},{4,6},{5,7},{6,4},{7,5},{8,10},{9,11},{10,... | collective-permute-start | bytes 2359304 | tf_op jit(solution)/shard_map/ppermute | solution.py:723
  75.4 9.8 %shard_map.212 = (bf16[8,256,512]{2,1,0:T(8,128)(2,1)}, bf16[4,256,512]{2,1,0:T(8,128)(2,1)}, f32[24,512]{1,0:T(8,128)}) custom-call(s32[1]{0:T(128)} %bitcast.sec, bf16[3,1024,512]{2,1,0:T(8,128)(2,1)} %get-tuple-element.52.gpre, bf16[512,1536]{1,0:T(8,128)(2,1)} %bitcast.33, bf16[512,1536]{1,0:T(8,128)(2,1)} %collective-permute-done.1.up_got, ...), custom_call_target="tpu_custom_call" | custom-call | flops 12884901888 | bytes 12582912 | tf_op jit(solution)/shard_map/pallas_call | solution.py:665
  85.3 0.8 broadcast_select_fusion
  86.1 0.1 collective-permute-start.5
  86.2 1.2 collective-permute-done.5.got
  87.4 0.8 copy-done
  88.2 0.8 copy-done.1
  89.0 0.7 copy-done.2
  89.6 0.6 shard_map.213
  90.2 2.7 %collective-permute-start.6 = (bf16[32,512]{1,0:T(8,128)(2,1)S(1)}, bf16[32,512]{1,0:T(8,128)(2,1)S(1)}, u32[]{:S(2)}, u32[]{:S(2)}) collective-permute-start(bf16[32,512]{1,0:T(8,128)(2,1)S(1)} %get-tuple-element.62.before), channel_id=1, source_target_pairs={{0,8},{1,9},{2,10},{3,11},{4,12},{5,13},{6,14},{7,15},{8,0},{9,1},... | collective-permute-start | bytes 98312 | tf_op jit(solution)/shard_map/ppermute | solution.py:770
  92.9 2.6 %collective-permute-done.6.after = bf16[32,512]{1,0:T(8,128)(2,1)S(1)} collective-permute-done((bf16[32,512]{1,0:T(8,128)(2,1)S(1)}, bf16[32,512]{1,0:T(8,128)(2,1)S(1)}, u32[]{:S(2)}, u32[]{:S(2)}) %collective-permute-start.6) | collective-permute-done | bytes 32800 | tf_op jit(solution)/shard_map/ppermute | solution.py:770
  95.5 1.3 %collective-permute-start.7 = (bf16[48,512]{1,0:T(8,128)(2,1)S(1)}, bf16[48,512]{1,0:T(8,128)(2,1)S(1)}, u32[]{:S(2)}, u32[]{:S(2)}) collective-permute-start(bf16[48,512]{1,0:T(8,128)(2,1)S(1)} %get-tuple-element.64.before), channel_id=1, source_target_pairs={{0,4},{1,5},{2,6},{3,7},{4,0},{5,1},{6,2},{7,3},{8,12},{9,13},{10,... | collective-permute-start | bytes 147464 | tf_op jit(solution)/shard_map/ppermute | solution.py:770
  96.8 1.4 %convert_add_fusion.1.total0 = f32[384,512]{1,0:T(8,128)S(1)} fusion(bf16[768,512]{1,0:T(8,128)(2,1)} %collective-permute-done.11.refs_2_, s32[]{:T(128)S(6)} %select_n.58, bf16[1536,512]{1,0:T(8,128)(2,1)} %bitcast.13.got.refs_1_, s32[]{:T(128)S(6)} %select_n.57, bf16[1536,512]{1,0:T(8,128)(2,1)} %bitcast.25), kind=kLoop, calls=%fused_computation.3 | loop fusion | flops 983040 | bytes 1966088 | tf_op jit(solution)/shard_map/add | solution.py:820
  98.1 1.4 %convert_add_fusion.total1 = f32[384,512]{1,0:T(8,128)S(1)} fusion(bf16[768,512]{1,0:T(8,128)(2,1)} %collective-permute-done.13.refs_5_, s32[]{:T(128)S(6)} %select_n.58, bf16[1536,512]{1,0:T(8,128)(2,1)} %bitcast.15.got.refs_4_, s32[]{:T(128)S(6)} %select_n.57, bf16[1536,512]{1,0:T(8,128)(2,1)} %bitcast.22), kind=kLoop, calls=%fused_computation.2 | loop fusion | flops 983040 | bytes 1966088 | tf_op jit(solution)/shard_map/add | solution.py:820
  99.5 1.2 shard_map.221
  100.7 0.9 collective-permute-start.15
  101.6 1.6 %collective-permute-start.8 = (bf16[80,512]{1,0:T(8,128)(2,1)S(1)}, bf16[80,512]{1,0:T(8,128)(2,1)S(1)}, u32[]{:S(2)}, u32[]{:S(2)}) collective-permute-start(bf16[80,512]{1,0:T(8,128)(2,1)S(1)} %get-tuple-element.66.before), channel_id=1, source_target_pairs={{0,1},{1,0},{2,3},{3,2},{4,5},{5,4},{6,7},{7,6},{8,9},{9,8},{10,11... | collective-permute-start | bytes 245768 | tf_op jit(solution)/shard_map/ppermute | solution.py:770
  103.2 3.0 %collective-permute-done.8.after = bf16[80,512]{1,0:T(8,128)(2,1)S(1)} collective-permute-done((bf16[80,512]{1,0:T(8,128)(2,1)S(1)}, bf16[80,512]{1,0:T(8,128)(2,1)S(1)}, u32[]{:S(2)}, u32[]{:S(2)}) %collective-permute-start.8) | collective-permute-done | bytes 81952 | tf_op jit(solution)/shard_map/ppermute | solution.py:770
  106.1 0.1 collective-permute-start.9
  106.2 5.1 %collective-permute-done.9.after = bf16[144,512]{1,0:T(8,128)(2,1)S(1)} collective-permute-done((bf16[144,512]{1,0:T(8,128)(2,1)S(1)}, bf16[144,512]{1,0:T(8,128)(2,1)S(1)}, u32[]{:S(2)}, u32[]{:S(2)}) %collective-permute-start.9) | collective-permute-done | bytes 147488 | tf_op jit(solution)/shard_map/ppermute | solution.py:770
  111.4 1.1 shard_map.217
  112.4 1.3 %convert_add_fusion.2 = (f32[192,512]{1,0:T(8,128)S(1)}, f32[192,512]{1,0:T(8,128)S(1)}) fusion(f32[384,512]{1,0:T(8,128)S(1)} %convert_add_fusion.total1, s32[]{:T(128)S(6)} %select_n.60, bf16[768,512]{1,0:T(8,128)(2,1)} %collective-permute-done.14.came, s32[]{:T(128)S(6)} %select_n.64, s32[]{:T(128)S(6)} %select_n.61, ...), kind=kLoop, calls=%fused_computation.4 | loop fusion | flops 393216 | bytes 1966092 | tf_op jit(solution)/shard_map/add | solution.py:825
  113.8 2.3 %collective-permute-start.16 = (bf16[192,512]{1,0:T(8,128)(2,1)S(1)}, bf16[192,512]{1,0:T(8,128)(2,1)S(1)}, u32[]{:S(2)}, u32[]{:S(2)}) collective-permute-start(bf16[192,512]{1,0:T(8,128)(2,1)S(1)} %shard_map.222), channel_id=1, source_target_pairs={{0,8},{1,9},{2,10},{3,11},{4,12},{5,13},{6,14},{7,15},{8,0},{9,1},... | collective-permute-start | bytes 589832 | tf_op jit(solution)/shard_map/ppermute | solution.py:723
  116.1 1.5 %bitcast_dynamic-update-slice_fusion.1 = bf16[1,8,256,512]{3,2,1,0:T(8,128)(2,1)S(1)} fusion(bf16[1,8,256,512]{3,2,1,0:T(8,128)(2,1)S(1)} %bitcast.27, s32[]{:T(128)S(6)} %select_n.52, bf16[4,256,512]{2,1,0:T(8,128)(2,1)} %collective-permute-done.3), kind=kLoop, calls=%fused_computation.1 | loop fusion | bytes 2097156 | tf_op jit(solution)/shard_map/dynamic_update_slice | solution.py:704
  117.6 0.1 convert_add_fusion.4
  117.6 4.9 %collective-permute-done.16.came = bf16[192,512]{1,0:T(8,128)(2,1)S(1)} collective-permute-done((bf16[192,512]{1,0:T(8,128)(2,1)S(1)}, bf16[192,512]{1,0:T(8,128)(2,1)S(1)}, u32[]{:S(2)}, u32[]{:S(2)}) %collective-permute-start.16) | collective-permute-done | bytes 196640 | tf_op jit(solution)/shard_map/ppermute | solution.py:723
  122.5 0.1 shard_map.223
  122.6 0.1 collective-permute-start.17
  122.7 1.3 %bitcast_dynamic-update-slice_fusion = bf16[1,8,256,512]{3,2,1,0:T(8,128)(2,1)S(1)} fusion(bf16[1,8,256,512]{3,2,1,0:T(8,128)(2,1)S(1)} %bitcast.28, s32[]{:T(128)S(6)} %select_n.52, bf16[4,256,512]{2,1,0:T(8,128)(2,1)} %collective-permute-done.4), kind=kLoop, calls=%fused_computation | loop fusion | bytes 2097156 | tf_op jit(solution)/shard_map/dynamic_update_slice | solution.py:704
  124.1 0.9 shard_map.224
  125.0 0.5 copy-done.6
  (24 shorter events, 0.2 us)
Async XLA Ops:
  0.6 6.3 %collective-permute-start.1 = (bf16[512,1536]{1,0:T(8,128)(2,1)}, bf16[512,1536]{1,0:T(8,128)(2,1)}, u32[]{:S(2)}, u32[]{:S(2)}) collective-permute-start(bf16[512,1536]{1,0:T(8,128)(2,1)} %bitcast.31), channel_id=1, source_target_pairs={{0,16},{16,0},{1,17},{17,1},{2,18},{18,2},{3,19},{19,3},{4,20},{20... | collective-permute-start | bytes 4718600 | tf_op jit(solution)/shard_map/ppermute | solution.py:594
  1.2 5.7 %collective-permute-start.2 = (bf16[1536,512]{1,0:T(8,128)(2,1)}, bf16[1536,512]{1,0:T(8,128)(2,1)}, u32[]{:S(2)}, u32[]{:S(2)}) collective-permute-start(bf16[1536,512]{1,0:T(8,128)(2,1)} %bitcast.29), channel_id=1, source_target_pairs={{0,16},{16,0},{1,17},{17,1},{2,18},{18,2},{3,19},{19,3},{4,20},{20... | collective-permute-start | bytes 4718600 | tf_op jit(solution)/shard_map/ppermute | solution.py:595
  3.7 3.2 %collective-permute-start = (f32[24,512]{1,0:T(8,128)}, f32[24,512]{1,0:T(8,128)}, u32[]{:S(2)}, u32[]{:S(2)}) collective-permute-start(f32[24,512]{1,0:T(8,128)} %get-tuple-element.49), channel_id=1, source_target_pairs={{0,16},{16,0},{1,17},{17,1},{2,18},{18,2},{3,19},{19,3},{4,20},{20... | collective-permute-start | bytes 147464 | tf_op jit(solution)/shard_map/ppermute | solution.py:592
  42.8 4.0 %collective-permute-start.10 = (bf16[16,96,512]{2,1,0:T(8,128)(2,1)}, bf16[16,96,512]{2,1,0:T(8,128)(2,1)}, u32[]{:S(2)}, u32[]{:S(2)}) collective-permute-start(bf16[16,96,512]{2,1,0:T(8,128)(2,1)} %get-tuple-element.75), channel_id=1, source_target_pairs={{0,16},{16,0},{1,17},{17,1},{2,18},{18,2},{3,19},{19,3},{4,20},{20... | collective-permute-start | bytes 4718600 | tf_op jit(solution)/shard_map/ppermute | solution.py:658
  43.4 8.6 %collective-permute-start.12 = (bf16[16,96,512]{2,1,0:T(8,128)(2,1)}, bf16[16,96,512]{2,1,0:T(8,128)(2,1)}, u32[]{:S(2)}, u32[]{:S(2)}) collective-permute-start(bf16[16,96,512]{2,1,0:T(8,128)(2,1)} %get-tuple-element.77), channel_id=1, source_target_pairs={{0,16},{16,0},{1,17},{17,1},{2,18},{18,2},{3,19},{19,3},{4,20},{20... | collective-permute-start | bytes 4718600 | tf_op jit(solution)/shard_map/ppermute | solution.py:657
  49.3 13.0 %collective-permute-start.11 = (bf16[768,512]{1,0:T(8,128)(2,1)}, bf16[768,512]{1,0:T(8,128)(2,1)}, u32[]{:S(2)}, u32[]{:S(2)}) collective-permute-start(bf16[768,512]{1,0:T(8,128)(2,1)} %shard_map.218), channel_id=1, source_target_pairs={{0,1},{1,0},{2,3},{3,2},{4,5},{5,4},{6,7},{7,6},{8,9},{9,8},{10,11... | collective-permute-start | bytes 2359304 | tf_op jit(solution)/shard_map/ppermute | solution.py:723
  54.5 16.2 %collective-permute-start.13 = (bf16[768,512]{1,0:T(8,128)(2,1)}, bf16[768,512]{1,0:T(8,128)(2,1)}, u32[]{:S(2)}, u32[]{:S(2)}) collective-permute-start(bf16[768,512]{1,0:T(8,128)(2,1)} %shard_map.219), channel_id=1, source_target_pairs={{0,1},{1,0},{2,3},{3,2},{4,5},{5,4},{6,7},{7,6},{8,9},{9,8},{10,11... | collective-permute-start | bytes 2359304 | tf_op jit(solution)/shard_map/ppermute | solution.py:723
  54.6 61.5 %collective-permute-start.3 = (bf16[4,256,512]{2,1,0:T(8,128)(2,1)}, bf16[4,256,512]{2,1,0:T(8,128)(2,1)}, u32[]{:S(2)}, u32[]{:S(2)}) collective-permute-start(bf16[4,256,512]{2,1,0:T(8,128)(2,1)} %get-tuple-element.51), channel_id=1, source_target_pairs={{0,16},{16,0},{1,17},{17,1},{2,18},{18,2},{3,19},{19,3},{4,20},{20... | collective-permute-start | bytes 3145736 | tf_op jit(solution)/shard_map/ppermute | solution.py:659
  73.3 26.2 %collective-permute-start.14 = (bf16[768,512]{1,0:T(8,128)(2,1)}, bf16[768,512]{1,0:T(8,128)(2,1)}, u32[]{:S(2)}, u32[]{:S(2)}) collective-permute-start(bf16[768,512]{1,0:T(8,128)(2,1)} %shard_map.220), channel_id=1, source_target_pairs={{0,2},{1,3},{2,0},{3,1},{4,6},{5,7},{6,4},{7,5},{8,10},{9,11},{10,... | collective-permute-start | bytes 2359304 | tf_op jit(solution)/shard_map/ppermute | solution.py:723
  86.1 1.3 %collective-permute-start.5 = (f32[24,512]{1,0:T(8,128)S(1)}, f32[24,512]{1,0:T(8,128)S(1)}, u32[]{:S(2)}, u32[]{:S(2)}) collective-permute-start(f32[24,512]{1,0:T(8,128)S(1)} %broadcast_select_fusion), channel_id=1, source_target_pairs={{0,16},{16,0},{1,17},{17,1},{2,18},{18,2},{3,19},{19,3},{4,20},{20... | collective-permute-start | bytes 147464 | tf_op jit(solution)/shard_map/ppermute | solution.py:701
  87.4 0.8 copy-start
  88.2 0.8 copy-start.1
  89.0 0.7 copy-start.2
  90.2 5.2 %collective-permute-start.6 = (bf16[32,512]{1,0:T(8,128)(2,1)S(1)}, bf16[32,512]{1,0:T(8,128)(2,1)S(1)}, u32[]{:S(2)}, u32[]{:S(2)}) collective-permute-start(bf16[32,512]{1,0:T(8,128)(2,1)S(1)} %get-tuple-element.62.before), channel_id=1, source_target_pairs={{0,8},{1,9},{2,10},{3,11},{4,12},{5,13},{6,14},{7,15},{8,0},{9,1},... | collective-permute-start | bytes 98312 | tf_op jit(solution)/shard_map/ppermute | solution.py:770
  92.9 29.8 %collective-permute-start.4 = (bf16[4,256,512]{2,1,0:T(8,128)(2,1)}, bf16[4,256,512]{2,1,0:T(8,128)(2,1)}, u32[]{:S(2)}, u32[]{:S(2)}) collective-permute-start(bf16[4,256,512]{2,1,0:T(8,128)(2,1)} %get-tuple-element.59), channel_id=1, source_target_pairs={{0,16},{16,0},{1,17},{17,1},{2,18},{18,2},{3,19},{19,3},{4,20},{20... | collective-permute-start | bytes 3145736 | tf_op jit(solution)/shard_map/ppermute | solution.py:700
  95.5 6.1 %collective-permute-start.7 = (bf16[48,512]{1,0:T(8,128)(2,1)S(1)}, bf16[48,512]{1,0:T(8,128)(2,1)S(1)}, u32[]{:S(2)}, u32[]{:S(2)}) collective-permute-start(bf16[48,512]{1,0:T(8,128)(2,1)S(1)} %get-tuple-element.64.before), channel_id=1, source_target_pairs={{0,4},{1,5},{2,6},{3,7},{4,0},{5,1},{6,2},{7,3},{8,12},{9,13},{10,... | collective-permute-start | bytes 147464 | tf_op jit(solution)/shard_map/ppermute | solution.py:770
  100.7 13.0 %collective-permute-start.15 = (bf16[384,512]{1,0:T(8,128)(2,1)S(1)}, bf16[384,512]{1,0:T(8,128)(2,1)S(1)}, u32[]{:S(2)}, u32[]{:S(2)}) collective-permute-start(bf16[384,512]{1,0:T(8,128)(2,1)S(1)} %shard_map.221), channel_id=1, source_target_pairs={{0,4},{1,5},{2,6},{3,7},{4,0},{5,1},{6,2},{7,3},{8,12},{9,13},{10,... | collective-permute-start | bytes 1179656 | tf_op jit(solution)/shard_map/ppermute | solution.py:723
  101.6 4.5 %collective-permute-start.8 = (bf16[80,512]{1,0:T(8,128)(2,1)S(1)}, bf16[80,512]{1,0:T(8,128)(2,1)S(1)}, u32[]{:S(2)}, u32[]{:S(2)}) collective-permute-start(bf16[80,512]{1,0:T(8,128)(2,1)S(1)} %get-tuple-element.66.before), channel_id=1, source_target_pairs={{0,1},{1,0},{2,3},{3,2},{4,5},{5,4},{6,7},{7,6},{8,9},{9,8},{10,11... | collective-permute-start | bytes 245768 | tf_op jit(solution)/shard_map/ppermute | solution.py:770
  106.1 5.2 %collective-permute-start.9 = (bf16[144,512]{1,0:T(8,128)(2,1)S(1)}, bf16[144,512]{1,0:T(8,128)(2,1)S(1)}, u32[]{:S(2)}, u32[]{:S(2)}) collective-permute-start(bf16[144,512]{1,0:T(8,128)(2,1)S(1)} %get-tuple-element.68.before), channel_id=1, source_target_pairs={{0,2},{1,3},{2,0},{3,1},{4,6},{5,7},{6,4},{7,5},{8,10},{9,11},{10,... | collective-permute-start | bytes 442376 | tf_op jit(solution)/shard_map/ppermute | solution.py:770
  112.4 3.7 %copy-start.3 = (bf16[8,256,512]{2,1,0:T(8,128)(2,1)S(1)}, bf16[8,256,512]{2,1,0:T(8,128)(2,1)}, u32[]{:S(2)}) copy-start(bf16[8,256,512]{2,1,0:T(8,128)(2,1)} %get-tuple-element.50) | copy-start | bytes 6291460
  113.8 8.7 %collective-permute-start.16 = (bf16[192,512]{1,0:T(8,128)(2,1)S(1)}, bf16[192,512]{1,0:T(8,128)(2,1)S(1)}, u32[]{:S(2)}, u32[]{:S(2)}) collective-permute-start(bf16[192,512]{1,0:T(8,128)(2,1)S(1)} %shard_map.222), channel_id=1, source_target_pairs={{0,8},{1,9},{2,10},{3,11},{4,12},{5,13},{6,14},{7,15},{8,0},{9,1},... | collective-permute-start | bytes 589832 | tf_op jit(solution)/shard_map/ppermute | solution.py:723
  116.1 6.6 %copy-start.5 = (bf16[8,256,512]{2,1,0:T(8,128)(2,1)S(1)}, bf16[8,256,512]{2,1,0:T(8,128)(2,1)}, u32[]{:S(2)}) copy-start(bf16[8,256,512]{2,1,0:T(8,128)(2,1)} %get-tuple-element.58) | copy-start | bytes 6291460
  117.6 6.5 %copy-start.4 = (bf16[1,8,256,512]{3,2,1,0:T(8,128)(2,1)}, bf16[1,8,256,512]{3,2,1,0:T(8,128)(2,1)S(1)}, u32[]{:S(2)}) copy-start(bf16[1,8,256,512]{3,2,1,0:T(8,128)(2,1)S(1)} %bitcast_dynamic-update-slice_fusion.1) | copy-start | bytes 6291460
  122.6 1.5 %collective-permute-start.17 = (f32[96,512]{1,0:T(8,128)S(1)}, f32[96,512]{1,0:T(8,128)S(1)}, u32[]{:S(2)}, u32[]{:S(2)}) collective-permute-start(f32[96,512]{1,0:T(8,128)S(1)} %get-tuple-element.79), channel_id=1, source_target_pairs={{0,16},{16,0},{1,17},{17,1},{2,18},{18,2},{3,19},{19,3},{4,20},{20... | collective-permute-start | bytes 589832 | tf_op jit(solution)/shard_map/ppermute | solution.py:833
  124.0 1.4 %copy-start.6 = (bf16[1,8,256,512]{3,2,1,0:T(8,128)(2,1)}, bf16[1,8,256,512]{3,2,1,0:T(8,128)(2,1)S(1)}, u32[]{:S(2)}) copy-start(bf16[1,8,256,512]{3,2,1,0:T(8,128)(2,1)S(1)} %bitcast_dynamic-update-slice_fusion) | copy-start | bytes 6291460

commit v6 on v5

--- a/solution.py
+++ b/solution.py
@@ -205,31 +205,89 @@
         go(up_got, down_got)
 
 
-def route_tile(sec, j, upd, dnd, keep, send, sems, start):
+def leaving(sec, place):
+    low, high = ORDERS[0][0], ORDERS[1][0]
+    return 1 - ((place[0] >> pick(sec[0] == 0, high, low)) & 1)
+
+
+def route_tile(sec, place, j, upd, dnd, keep, passed, stays, sems, start):
     share = TILE // BLOCKS
-
-    def go(up_to, down_to):
-        part = pl.ds(j * share, share)
-        copies = [pltpu.make_async_copy(upd.at[:, part], up_to.at[:, part], sems.at[j, 0])]
+    part = pl.ds(j * share, share)
+    half = BLOCKS // 2
+    goes = leaving(sec, place)
+
+    def run(copy):
+        copy.start() if start else copy.wait()
+
+    def up_copies(first, second):
+        for n, (source, target) in enumerate(((goes, first), (1 - goes, second))):
+            run(
+                pltpu.make_async_copy(
+                    upd.at[pl.ds(source * half, half), part], target.at[:, part], sems.at[j, n]
+                )
+            )
+
+    def down_copies(pick_target):
         for n, (block, first, rows, _) in enumerate(down_pieces(j)):
-            part = pl.ds(first, rows)
-            copies.append(
-                pltpu.make_async_copy(dnd.at[block, part], down_to.at[block, part], sems.at[j, 1 + n])
-            )
-        for copy in copies:
-            copy.start() if start else copy.wait()
+            pick_target(n, block, pl.ds(first, rows))
+
+    def down_to(target, n, source, block, rows):
+        run(pltpu.make_async_copy(dnd.at[source, rows], target.at[block, rows], sems.at[j, 2 + n]))
+
+    def down_kept(n, block, rows):
+        down_to(keep, n, block, block, rows)
+
+    def down_sent(n, block, rows):
+        @pl.when(goes == block // half)
+        def _():
+            down_to(passed, n, block, block % half, rows)
+
+        @pl.when(goes != block // half)
+        def _():
+            down_to(stays, n, block, block % half, rows)
 
     if not start:
-        go(keep, send)
+        up_copies(passed, stays)
+        down_copies(down_kept)
         return
 
     @pl.when(sec[0] == 0)
     def _():
-        go(keep, send)
+        up_copies(keep.at[pl.ds(goes * half, half)], keep.at[pl.ds((1 - goes) * half, half)])
+        down_copies(down_sent)
 
     @pl.when(sec[0] != 0)
     def _():
-        go(send, keep)
+        up_copies(passed, stays)
+        down_copies(down_kept)
+
+
+def route_halves(sec, place, upd, dnd, keep, passed, stays, sems, start):
+    half = BLOCKS // 2
+    goes = leaving(sec, place)
+
+    def go(kept, sent):
+        for n, (source, target) in enumerate(
+            (
+                (kept, keep),
+                (sent.at[pl.ds(goes * half, half)], passed),
+                (sent.at[pl.ds((1 - goes) * half, half)], stays),
+            )
+        ):
+            copy = pltpu.make_async_copy(source, target, sems.at[n])
+            copy.start() if start else copy.wait()
+
+    if not start:
+        go(upd, dnd)
+        return
+
+    @pl.when(sec[0] == 0)
+    def _():
+        go(upd, dnd)
+
+    @pl.when(sec[0] != 0)
+    def _():
+        go(dnd, upd)
 
 
 def route(sec, upd, dnd, keep, send, sems, start):
@@ -252,11 +310,11 @@
 
 
 def main_body(
-    sec, valid, own_small, got_small, tokens, cot, up_own, up_got, down_own, down_got,
-    sums0, sums1, gin1, normed_hbm, inv_hbm, out_own, out_send, gpre_hbm, keep1, send1, keep0, send0,
-    small0_out,
+    sec, place, valid, own_small, got_small, tokens, cot, up_own, up_got, down_own, down_got,
+    sums0, sums1, gin1, normed_hbm, inv_hbm, out_own, out_send, gpre_hbm, keep1, passed1, stays1, keep0, passed0,
+    stays0, small0_out,
     up0, down0, up1, down1, act0, slope0, act1, slope1, acc, adapted0, normed, inv, adapted1, branch0,
-    gb, v, grad, out0, out1, small0, small1, shifts, upd, dnd, upd0, dnd0, sems, pieces, parts,
+    gb, v, grad, out0, out1, small0, small1, shifts, upd, dnd, upd0, dnd0, sems, pieces, parts, halves,
 ):
     clips = acc.shape[0] // 256
     mine = pl.ds(sec[0] * clips, clips)
@@ -330,7 +388,7 @@
             part = dot(slope1[j, rows], up1[:, j * TILE : (j + 1) * TILE], NT)
             acc[rows] = part if j == 0 else acc[rows] + part
         weight_tile(j, gb, adapted1, act1[j], slope1[j], upd, dnd)
-    route(sec, upd, dnd, keep1, send1, sems.at[3], True)
+    route_halves(sec, place, upd, dnd, keep1, passed1, stays1, halves, True)
 
     def move(r):
         return pltpu.make_async_copy(grad.at[r], gin1.at[r], pieces.at[r])
@@ -359,25 +417,24 @@
         tiles.append(pltpu.make_async_copy(slope0.at[j], gpre_hbm.at[j], sems.at[5 + j // 2 * 3, j % 2]))
         tiles[-1].start()
         weight_tile(j, gb, adapted0, act0[j], slope0[j], upd0, dnd0)
-        route_tile(sec, j, upd0, dnd0, keep0, send0, parts, True)
+        route_tile(sec, place, j, upd0, dnd0, keep0, passed0, stays0, parts, True)
     route(sec, out0, out1, half_own, out_send, sems.at[4], False)
-    route(sec, upd, dnd, keep1, send1, sems.at[3], False)
+    route_halves(sec, place, upd, dnd, keep1, passed1, stays1, halves, False)
     for copy in tiles + [move(r) for r in range(clips)]:
         copy.wait()
     for j in range(3):
-        route_tile(sec, j, upd0, dnd0, keep0, send0, parts, False)
+        route_tile(sec, place, j, upd0, dnd0, keep0, passed0, stays0, parts, False)
 
 
 def last_body(
-    first, sec, gpre, up_own, up_got, normed, inv, small, grad_out, tokens, sums_in, *rest
+    sec, gpre, up_own, up_got, normed, inv, small, grad_out, tokens, sums0, sums1, gin, away, own, send,
+    up, shifts, sums, sem,
 ):
-    gin, away, sums, up, shifts, sem = rest[-6:]
-    step = pl.program_id(0)
-    clip = first + step
-
-    @pl.when(step == 0)
+    clip = pl.program_id(0)
+
+    @pl.when(clip == 0)
     def _():
-        sums[...] = sums_in[...]
+        sums[...] = sums0[...]
 
         @pl.when(sec[0] == 0)
         def _():
@@ -403,6 +460,11 @@
     sums[pl.ds(SCALE + clip, 1)] = g_scale
     sums[pl.ds(SHIFT + clip, 1)] = g_shift
 
+    @pl.when(clip == pl.num_programs(0) - 1)
+    def _():
+        own[...] = pick(sec[0] == 0, sums[...], sums1[...])
+        send[...] = pick(sec[0] == 0, sums1[...], sums[...])
+
 
 def pick(first, a, b):
     return jnp.where(first, a, b)
@@ -432,46 +494,22 @@
     copies[-1].start()
 
 
-def split_body(share, sec, place, keep, got, packet, kept, came, sems):
-    rows = 8 * share
-    first = pl.multiple_of((1 - bit_of((sec[0], place[0]), 0)) * rows, rows)
-    pieces = 4
-    size = rows // pieces
-    copies = []
-    for n in range(pieces):
-        for m, (source, target) in enumerate(((keep, kept), (got, came))):
-            fetch(
-                copies, source, first + n * size, size, target.at[pl.ds(n * size, size)], sems.at[n, m]
-            )
-    for n in range(pieces):
-        copies[2 * n].wait()
-        copies[2 * n + 1].wait()
-        part = slice(n * size, (n + 1) * size)
-        packet[part] = (kept[part].astype(F32) + came[part].astype(F32)).astype(BF16)
-
-
-def second_body(share, sec, place, *refs):
-    spot = (sec[0], place[0])
-    sources, (packet, buffer, sems) = refs[:6], refs[6:]
-    rows = 4 * share
-    away = (1 - bit_of(spot, 1)) * rows
-    copies = []
-    for n, source in enumerate(sources):
-        first = away if n % 3 == 2 else away + bit_of(spot, 0) * 2 * rows
-        fetch(copies, source, pl.multiple_of(first, 32), rows, buffer.at[n], sems.at[n])
-    for b in range(2):
-        total = 0.0
-        for n in range(3 * b, 3 * b + 3):
-            copies[n].wait()
-            total = total + buffer[n].astype(F32)
-        packet[b * rows : (b + 1) * rows] = total.astype(BF16)
-
-
-def pack_body(step, share, sec, place, total0, total1, came, packet):
+def pack_body(step, share, sec, place, total0, total1, *refs):
     rows = (8 >> step) * share
     first = pl.multiple_of((1 - bit_of((sec[0], place[0]), step)) * rows, 32)
+    if step == 1:
+        came, (packet, buffer, sems) = refs[:2], refs[2:]
+        copies = []
+        for b in range(2):
+            fetch(copies, came[b], first, rows, buffer.at[b], sems.at[b])
+    else:
+        came, packet = refs
     for b, total in enumerate((total0, total1)):
-        latest = came[pl.ds(b * 2 * rows + first, rows)]
+        if step == 1:
+            copies[b].wait()
+            latest = buffer[b]
+        else:
+            latest = came[pl.ds(b * 2 * rows + first, rows)]
         packet[b * rows : (b + 1) * rows] = (total[pl.ds(first, rows)] + latest.astype(F32)).astype(BF16)
 
 
@@ -485,11 +523,15 @@
                 target[...] = whole
 
 
-def begin_rows_body(sec, place, speaker, sums0, sums1, got, packet, smalls):
+def begin_rows_body(sec, place, speaker, own_sums, got_sums, packet, smalls, held, sems):
     spot = (sec[0], place[0])
     first = spot[0] == 0
-    own = pick(first, sums0[...], sums1[...])
-    other = got[...]
+    copies = []
+    for n, source in enumerate((own_sums, got_sums)):
+        fetch(copies, source, 0, SMALL, held.at[n], sems.at[n])
+    for copy in copies:
+        copy.wait()
+    own, other = held[0], held[1]
     low = pick(first, own[SCALE:], other[SCALE:])
     high = pick(first, other[SCALE:], own[SCALE:])
     packet[:16] = jnp.concatenate([low, high], axis=0).astype(BF16)
@@ -568,7 +610,6 @@
     section = lax.axis_index("section").astype(jnp.int32)
     place = lax.axis_index("dp").astype(jnp.int32)
     devices = lax.axis_size("dp")
-    first_section = section == 0
     clips, frames, width = tokens.shape
     hidden = up_weight.shape[2]
     table_rows = scale_table.shape[1]
@@ -604,19 +645,21 @@
     share = hidden // BLOCKS
     gradient = (BLOCKS, share, width)
     gradient_struct = struct(gradient, BF16)
+    piece_struct = struct((BLOCKS // 2, share, width), BF16)
     product = 2 * rows * width * hidden
 
     (
-        sums0, sums1, gin1, normed0, inv0, out_own, out_send, gpre0, keep1, send1, keep0, send0, small0,
+        sums0, sums1, gin1, normed0, inv0, out_own, out_send, gpre0, keep1, passed1,
+        stays1, keep0, passed0, stays0, small0,
     ) = pl.pallas_call(
         main_body,
         out_shape=[
             small_struct, small_struct, half_struct, flat_struct, struct((rows, 128), F32),
-            whole_struct, half_struct, struct(tiled, BF16), gradient_struct, gradient_struct,
-            gradient_struct, gradient_struct, small_struct,
+            whole_struct, half_struct, struct(tiled, BF16), gradient_struct, piece_struct, piece_struct,
+            gradient_struct, piece_struct, piece_struct, small_struct,
         ],
-        in_specs=[SMEM, SMEM, VMEM, VMEM, HBM, HBM, HBM, ANY, HBM, ANY],
-        out_specs=[VMEM, VMEM] + [HBM] * 10 + [VMEM],
+        in_specs=[SMEM, SMEM, SMEM, VMEM, VMEM, HBM, HBM, HBM, ANY, HBM, ANY],
+        out_specs=[VMEM, VMEM] + [HBM] * 12 + [VMEM],
         scratch_shapes=[
             pltpu.VMEM((width, hidden), BF16),
             pltpu.VMEM((hidden, width), BF16),
@@ -646,70 +689,68 @@
             pltpu.VMEM(gradient, BF16),
             pltpu.SemaphoreType.DMA((9, 2)),
             pltpu.SemaphoreType.DMA((half,)),
-            pltpu.SemaphoreType.DMA((3, 8)),
+            pltpu.SemaphoreType.DMA((3, 9)),
+            pltpu.SemaphoreType.DMA((3,)),
         ],
         compiler_params=params(),
         cost_estimate=cost(11 * product, 24 << 20),
         name="main",
     )(
-        sec, valid, own_small, got_small, tokens, out_cotangent, up_own, up_got, down_own, down_got
-    )
-    got1 = lax.ppermute(send1, "section", swap)
-    got0 = lax.ppermute(send0, "section", swap)
+        sec, place[None], valid, own_small, got_small, tokens, out_cotangent, up_own, up_got, down_own, down_got
+    )
+    swapped = []
+    for piece in (passed1, passed0, stays1, stays0):
+        swapped.append(lax.ppermute(piece, "section", swap))
+    pairs = [[keep0, swapped[1], swapped[3]], [keep1, swapped[0], swapped[2]]]
     got_out = lax.ppermute(out_send, "section", swap)
 
-    def last(first, count, sums, *others):
-        def at(c):
-            return first + c
-
-        return pl.pallas_call(
-            functools.partial(last_body, first),
-            grid_spec=pltpu.PrefetchScalarGridSpec(
-                num_scalar_prefetch=1,
-                grid=(count,),
-                in_specs=[
-                    pl.BlockSpec((tiles, frames, TILE), lambda c, sec: (0, at(c), 0)),
-                    HBM,
-                    ANY,
-                    pl.BlockSpec((frames, width), lambda c, sec: (at(c), 0)),
-                    pl.BlockSpec((frames, 128), lambda c, sec: (at(c), 0)),
-                    whole_small,
-                    pl.BlockSpec(clip_block, lambda c, sec: (at(c), 0, 0)),
-                    pl.BlockSpec(clip_block, lambda c, sec: (sec[0] * half + at(c), 0, 0)),
-                    whole_small,
-                ]
-                + [ANY] * len(others),
-                out_specs=[
-                    pl.BlockSpec(clip_block, lambda c, sec: (sec[0] * half + at(c), 0, 0)),
-                    pl.BlockSpec(clip_block, lambda c, sec: (at(c), 0, 0)),
-                    whole_small,
-                ],
-                scratch_shapes=[
-                    pltpu.VMEM((width, hidden), BF16),
-                    pltpu.VMEM((len(OFFSETS) * frames, frames), BF16),
-                    pltpu.SemaphoreType.DMA,
-                ],
-            ),
-            out_shape=[whole_struct, half_struct, small_struct],
-            input_output_aliases={10 + i: i for i in range(len(others))},
-            compiler_params=params(),
-            cost_estimate=cost(2 * count * product, 12 << 20),
-        )(sec, gpre0, up_own, up_got, normed0, inv0, small0, gin1, tokens, sums, *others)
-
-    gin_own, gin_send, sums0 = last(0, half, sums0)
+    gin_own, gin_send, own_sums, sums_send = pl.pallas_call(
+        last_body,
+        grid_spec=pltpu.PrefetchScalarGridSpec(
+            num_scalar_prefetch=1,
+            grid=(half,),
+            in_specs=[
+                pl.BlockSpec((tiles, frames, TILE), lambda c, sec: (0, c, 0)),
+                HBM,
+                ANY,
+                pl.BlockSpec((frames, width), lambda c, sec: (c, 0)),
+                pl.BlockSpec((frames, 128), lambda c, sec: (c, 0)),
+                whole_small,
+                pl.BlockSpec(clip_block, lambda c, sec: (c, 0, 0)),
+                pl.BlockSpec(clip_block, lambda c, sec: (sec[0] * half + c, 0, 0)),
+                whole_small,
+                whole_small,
+            ],
+            out_specs=[
+                pl.BlockSpec(clip_block, lambda c, sec: (sec[0] * half + c, 0, 0)),
+                pl.BlockSpec(clip_block, lambda c, sec: (c, 0, 0)),
+                whole_small,
+                whole_small,
+            ],
+            scratch_shapes=[
+                pltpu.VMEM((width, hidden), BF16),
+                pltpu.VMEM((len(OFFSETS) * frames, frames), BF16),
+                pltpu.VMEM((SMALL, width), F32),
+                pltpu.SemaphoreType.DMA,
+            ],
+        ),
+        out_shape=[whole_struct, half_struct, small_struct, small_struct],
+        compiler_params=params(),
+        cost_estimate=cost(2 * half * product, 12 << 20),
+        name="last",
+    )(sec, gpre0, up_own, up_got, normed0, inv0, small0, gin1, tokens, sums0, sums1)
     got_gin = lax.ppermute(gin_send, "section", swap)
-    got_sums = lax.ppermute(pick(first_section, sums1, sums0), "section", swap)
+    got_sums = lax.ppermute(sums_send, "section", swap)
 
     def joined(whole, got):
         return lax.dynamic_update_slice(whole, got, ((1 - section) * half, 0, 0))[None]
 
     block_outputs = joined(out_own, got_out)
     input_grads = joined(gin_own, got_gin)
-    pairs = [[keep0, got0], [keep1, got1]]
     if devices == BLOCKS:
-        outs = halved(sec, place[None], speaker, pairs, sums0, sums1, got_sums, table_rows)
+        outs = halved(sec, place[None], speaker, pairs, own_sums, got_sums, table_rows)
     else:
-        outs = scattered(section, place, devices, speaker, pairs, sums0, sums1, got_sums, table_rows)
+        outs = scattered(section, place, devices, speaker, pairs, own_sums, got_sums, table_rows)
     return (block_outputs, input_grads) + outs
 
 
@@ -723,33 +764,23 @@
     return lax.ppermute(packet, PAIR, moves)
 
 
-def halved(sec, place, speaker, pairs, sums0, sums1, got_sums, table_rows):
+def halved(sec, place, speaker, pairs, own_sums, got_sums, table_rows):
     _, share, width = pairs[0][0].shape
     pairs = [[piece.reshape(-1, width) for piece in pair] for pair in pairs]
     spot = (sec[0], place[0])
     half_rows = 8 * share
 
-    def split(b):
-        return pl.pallas_call(
-            functools.partial(split_body, share),
-            out_shape=struct((half_rows, width), BF16),
-            in_specs=[SMEM, SMEM, HBM, HBM],
-            out_specs=VMEM,
-            scratch_shapes=[
-                pltpu.VMEM((half_rows, width), BF16),
-                pltpu.VMEM((half_rows, width), BF16),
-                pltpu.SemaphoreType.DMA((4, 2)),
-            ],
-            compiler_params=params(),
-            cost_estimate=cost(0, 4 << 20),
-        )(sec, place, *pairs[b])
-
     def part(array, first, count):
         return lax.dynamic_slice_in_dim(array, first, count, 0).astype(F32)
 
+    bit = bit_of(spot, 0)
+    latest, totals = [None, None], [None, None]
     for b in (1, 0):
-        packet = split(b)
-        pairs[b].append(exchanged(packet, 0))
+        keep, passed, stays = pairs[b]
+        packet = (part(keep, (1 - bit) * half_rows, half_rows) + passed.astype(F32)).astype(BF16)
+        latest[b] = exchanged(packet, 0)
+        keep, stays, _ = lax.optimization_barrier((keep, stays, own_sums))
+        totals[b] = part(keep, bit * half_rows, half_rows) + stays.astype(F32)
 
     def small_call(body, outs, scalars, operands, scratch=(), specs=None, limit=8):
         return pl.pallas_call(
@@ -765,7 +796,11 @@
     def row_outs(hop):
         return [struct(((16 << hop) + 16, width), BF16), struct((SCALE, width), F32)]
 
-    rows_packet, smalls = small_call(begin_rows_body, row_outs(0), [sec, place, speaker], [sums0, sums1, got_sums])
+    rows_packet, smalls = small_call(
+        begin_rows_body, row_outs(0), [sec, place, speaker],
+        [own_sums, got_sums],
+        [pltpu.VMEM((2, SMALL, width), F32), pltpu.SemaphoreType.DMA((2,))], [HBM] * 2,
+    )
     for hop in range(len(GATHER)):
         more = lax.ppermute(
             rows_packet, "dp", [(i, i ^ (1 << GATHER[hop])) for i in range(BLOCKS)]
@@ -795,40 +830,31 @@
         [pltpu.VMEM((16 * BLOCKS, width), BF16)],
     )
 
-    totals, latest = None, None
     for step in range(1, 4):
         rows = (8 >> step) * share
         first = bit_of(spot, step) * rows
         packet_struct = [struct((2 * rows, width), BF16)]
         if step == 1:
             (packet,) = small_call(
-                functools.partial(second_body, share), packet_struct, [sec, place],
-                pairs[0] + pairs[1],
-                [pltpu.VMEM((6, rows, width), BF16), pltpu.SemaphoreType.DMA((6,))],
-                [HBM] * 6,
-                None,
+                functools.partial(pack_body, step, share), packet_struct, [sec, place],
+                totals + latest,
+                [pltpu.VMEM((2, rows, width), BF16), pltpu.SemaphoreType.DMA((2,))],
+                [VMEM] * 2 + [ANY] * 2,
             )
         else:
             (packet,) = small_call(
                 functools.partial(pack_body, step, share), packet_struct, [sec, place],
-                totals + [latest],
+                totals + latest[:1],
             )
         got = exchanged(packet, step)
-        if step == 1:
-            start = bit_of(spot, 0) * 2 * rows + first
-            totals = [
-                part(keep, start, rows) + part(swapped, start, rows) + part(came, first, rows)
-                for keep, swapped, came in pairs
-            ]
-        else:
-            totals = [
-                part(totals[b], first, rows) + part(latest, 2 * b * rows + first, rows)
-                for b in range(2)
-            ]
-        latest = got
+        bases = (0, 0) if step == 1 else (0, 2 * rows)
+        totals = [
+            part(totals[b], first, rows) + part(latest[b], bases[b] + first, rows) for b in range(2)
+        ]
+        latest = [got, got]
     mine, away = small_call(
         functools.partial(share_body, share), [struct((share, width), F32)] * 2, [sec],
-        totals + [latest],
+        totals + latest[:1],
     )
     got_share = lax.ppermute(away, "section", [(0, 1), (1, 0)])
     up, down = small_call(
@@ -839,9 +865,8 @@
     )
 
 
-def scattered(section, place, devices, speaker, pairs, sums0, sums1, got_sums, table_rows):
+def scattered(section, place, devices, speaker, pairs, own_sums, got_sums, table_rows):
     first_section = section == 0
-    own_sums = pick(first_section, sums0, sums1)
     smalls = lax.psum(own_sums[:SCALE] + got_sums[:SCALE], "dp")
     clip_rows = jnp.stack([own_sums[SCALE:], got_sums[SCALE:]])
     clip_rows = pick(first_section, clip_rows, clip_rows[::-1]).astype(BF16)
@@ -854,15 +879,16 @@
     wanted = place * owned + jnp.arange(owned, dtype=jnp.int32)
     chosen = (who[None, :] == wanted[:, None]).astype(BF16)
     tables = [jnp.dot(chosen, gathered[k], preferred_element_type=F32) for k in range(2)]
+    low, high = ORDERS[0][0], ORDERS[1][0]
+    leaves = 1 - ((place >> pick(first_section, low, high)) & 1)
+    whole = []
+    for keep, gone, stay in pairs:
+        other = pick(leaves == 0, jnp.concatenate([gone, stay]), jnp.concatenate([stay, gone]))
+        whole.append(keep.astype(F32) + other.astype(F32))
     natural = []
     for order in ORDERS:
         natural.append(
-            jnp.stack(
-                [
-                    jnp.stack([pair[0][position(i, order)].astype(F32) + pair[1][position(i, order)].astype(F32) for i in range(BLOCKS)])
-                    for pair in pairs
-                ]
-            )
+            jnp.stack([jnp.stack([total[position(i, order)] for i in range(BLOCKS)]) for total in whole])
         )
     blocks, _, rows, width = natural[0].shape
     tiles = rows * BLOCKS // TILE

time: 126 us -> 113 us (0.90)
  waiting for transfers between devices: 38.7 us -> 27.2 us
  Pallas kernels: 59.5 us -> 54.4 us
  other arithmetic: 4.92 us -> 9.77 us
  local copies, waits for them, and re-layouts: 5.58 us -> 3.35 us
    ppermute x5, waiting for transfers between devices: 20.8 us -> 10 us  [exchanged(): return lax.ppermute(packet, PAIR, moves)]
    pallas_call x3 -> x1, Pallas kernels: 14.8 us -> 9.96 us  [local(): pl.pallas_call(last_body, grid_spec=pltpu.PrefetchScalarGridSpec(num_scal...]
    convert_element_type x0 -> x2, other arithmetic: none -> 3.46 us  [halved(): (part(keep, (1 - bit) * half_rows, half_rows) + passed.astype(F32)).astyp...]
    unnamed x14 -> x18, local copies, waits for them, and re-layouts: 2.77 us -> 0.54 us
    add x4 -> x5, other arithmetic: 4.1 us -> 6.31 us  [the longest x4 3.97 us: halved(): part(totals[b], first, rows) + part(latest[b], bases[b] + first, rows)]
    ppermute x3 -> x5, waiting for transfers between devices: 4.52 us -> 4.03 us  [the longest x1 2.49 us: local(): got_sums = lax.ppermute(sums_send, 'section', swap)]
  transfers between devices with their start and end apart: 18 -> 20, of which waited for: 9 -> 8; matrix products, arithmetic and copies ran while one was open for 6% -> 11% of each run, Pallas kernels for 18% -> 14%
where the time goes in v6:
time: 113 us; the launch traced here: 112 us
  Pallas kernels  54.4 us (48%)
  waiting for transfers between devices  27.2 us (24%)
  starting transfers between devices  16.7 us (15%)
  other arithmetic  9.77 us (9%)
  local copies, waits for them, and re-layouts  3.35 us (3%)
    pallas_call x1, Pallas kernels, local(): pl.pallas_call(main_body, out_shape=[small_struct, small_struct, half_str...  35.9 us
    ppermute x4, waiting for transfers between devices, halved(): lax.ppermute(rows_packet, 'dp', [(i, i ^ 1 << GATHER[hop]) for i in range...  10.4 us
    ppermute x5, waiting for transfers between devices, exchanged(): return lax.ppermute(packet, PAIR, moves)  10 us
    pallas_call x1, Pallas kernels, local(): pl.pallas_call(last_body, grid_spec=pltpu.PrefetchScalarGridSpec(num_scal...  9.96 us
    ppermute x5, starting transfers between devices, exchanged(): return lax.ppermute(packet, PAIR, moves)  7.99 us
    pallas_call x10, Pallas kernels, small_call(): pl.pallas_call(body, out_shape=outs, in_specs=[SMEM] * len(scalars) + (sp...  6.11 us
    ppermute x4, starting transfers between devices, halved(): lax.ppermute(rows_packet, 'dp', [(i, i ^ 1 << GATHER[hop]) for i in range...  5.79 us
    add x4, other arithmetic, halved(): part(totals[b], first, rows) + part(latest[b], bases[b] + first, rows)  3.97 us
  transfers between devices with their start and end apart: 20, of which 8 were waited for; matrix products, arithmetic and copies ran while one was open for 11% of the time, Pallas kernels for 14%

profile of v6, /device:TPU:0, one launch (start us, length us, event | category | flops | bytes accessed | tf_op | source)
XLA Modules:
  0.0 112.4 jit_solution(17607418840178591299)
XLA Ops:
  0.6 0.6 collective-permute-start.1
  1.2 0.1 collective-permute-start.2
  1.3 2.4 %prep.1 = (f32[24,512]{1,0:T(8,128)}, f32[24,512]{1,0:T(8,128)}) custom-call(s32[1]{0:T(128)} %bitcast.sec, s32[8]{0:T(128)} %speaker.3, f32[7,1,512]{2,1,0:T(1,128)} %bitcast.30, f32[1,512]{1,0:T(1,128)} %conv.1, f32[1,1536]{1,0:T(1,128)} %upb.1, f32[1,512]{1,0:T(1,128)} %downb.1, f32[1,512]{1,0:T(1,128)} %gain.1, f32[1,2560,512]{2,1,0:T(8,128)} %scale_hbm.1, ...), custom_call_target="tpu_custom_call" | custom-call | tf_op jit(solution)/shard_map/prep/pallas_call | solution.py:621
  3.7 0.5 collective-permute-start
  4.2 2.7 %collective-permute-done.got_small = f32[24,512]{1,0:T(8,128)} collective-permute-done((f32[24,512]{1,0:T(8,128)}, f32[24,512]{1,0:T(8,128)}, u32[]{:S(2)}, u32[]{:S(2)}) %collective-permute-start) | collective-permute-done | bytes 49184 | tf_op jit(solution)/shard_map/ppermute | solution.py:633
  6.9 35.9 %main.1 = (f32[24,512]{1,0:T(8,128)}, f32[24,512]{1,0:T(8,128)}, bf16[4,256,512]{2,1,0:T(8,128)(2,1)}, bf16[1024,512]{1,0:T(8,128)(2,1)}, f32[1024,128]{1,0:T(8,...) custom-call(s32[1]{0:T(128)} %bitcast.sec, ...), custom_call_target="tpu_custom_call" | custom-call | flops 17716740096 | bytes 25165824 | tf_op jit(solution)/shard_map/main/pallas_call | solution.py:654
  42.8 0.6 collective-permute-start.14
  43.5 0.1 collective-permute-start.11
  43.6 0.4 collective-permute-start.13
  44.0 0.1 collective-permute-start.10
  44.1 1.5 %collective-permute-done.14 = bf16[8,96,512]{2,1,0:T(8,128)(2,1)S(1)} collective-permute-done((bf16[8,96,512]{2,1,0:T(8,128)(2,1)}, bf16[8,96,512]{2,1,0:T(8,128)(2,1)S(1)}, u32[]{:S(2)}, u32[]{:S(2)}) %collective-permute-start.14) | collective-permute-done | bytes 786464 | tf_op jit(solution)/shard_map/ppermute | solution.py:703
  45.6 2.3 %fusion = bf16[768,512]{1,0:T(8,128)(2,1)} fusion(bf16[8,96,512]{2,1,0:T(8,128)(2,1)S(1)} %collective-permute-done.14, bf16[1536,512]{1,0:T(8,128)(2,1)} %bitcast.26, s32[]{:T(128)S(6)} %select_n.53), kind=kLoop, calls=%fused_computation.1 | loop fusion | flops 1572864 | bytes 2359300 | tf_op jit(solution)/shard_map/convert_element_type | solution.py:780
  47.9 2.6 %collective-permute-start.15 = (bf16[768,512]{1,0:T(8,128)(2,1)}, bf16[768,512]{1,0:T(8,128)(2,1)}, u32[]{:S(2)}, u32[]{:S(2)}) collective-permute-start(bf16[768,512]{1,0:T(8,128)(2,1)} %fusion), channel_id=1, source_target_pairs={{0,1},{1,0},{2,3},{3,2},{4,5},{5,4},{6,7},{7,6},{8,9},{9,8},{10,11... | collective-permute-start | bytes 2359304 | tf_op jit(solution)/shard_map/ppermute | solution.py:764
  50.6 1.1 %fusion.1 = bf16[768,512]{1,0:T(8,128)(2,1)} fusion(bf16[8,96,512]{2,1,0:T(8,128)(2,1)S(1)} %collective-permute-done.11, bf16[1536,512]{1,0:T(8,128)(2,1)S(1)} %bitcast.29, s32[]{:T(128)S(6)} %select_n.53), kind=kLoop, calls=%fused_computation.3 | loop fusion | flops 1572864 | bytes 2359300 | tf_op jit(solution)/shard_map/convert_element_type | solution.py:780
  51.7 0.0 collective-permute-start.12
  51.7 10.0 %last.1 = (bf16[8,256,512]{2,1,0:T(8,128)(2,1)}, bf16[4,256,512]{2,1,0:T(8,128)(2,1)}, f32[24,512]{1,0:T(8,128)}, f32[24,512]{1,0:T(8,128)}) custom-call(s32[1]{0:T(128)} %bitcast.sec, bf16[3,1024,512]{2,1,0:T(8,128)(2,1)} %get-tuple-element.59.gpre, bf16[512,1536]{1,0:T(8,128)(2,1)} %bitcast.37, bf16[512,1536]{1,0:T(8,128)(2,1)} %collective-permute-done.1.up_got, ...), custom_call_target="tpu_custom_call" | custom-call | flops 12884901888 | bytes 12582912 | tf_op jit(solution)/shard_map/last/pallas_call | solution.py:707
  61.7 2.3 %convert_add_fusion.2 = (f32[768,512]{1,0:T(8,128)S(1)}, f32[768,512]{1,0:T(8,128)S(1)}) fusion(bf16[768,512]{1,0:T(8,128)(2,1)} %bitcast.16, bf16[1536,512]{1,0:T(8,128)(2,1)} %bitcast.27, s32[]{:T(128)S(6)} %select_n.50, bf16[768,512]{1,0:T(8,128)(2,1)} %bitcast.13, bf16[1536,512]{1,0:T(8,128)(2,1)} %bitcast.28), kind=kLoop, calls=%fused_computation.4 | loop fusion | flops 2359296 | bytes 6291460 | tf_op jit(solution)/shard_map/add | solution.py:783
  64.1 5.2 %collective-permute-done.12.refs_0_ = bf16[768,512]{1,0:T(8,128)(2,1)} collective-permute-done((bf16[768,512]{1,0:T(8,128)(2,1)}, bf16[768,512]{1,0:T(8,128)(2,1)}, u32[]{:S(2)}, u32[]{:S(2)}) %collective-permute-start.12) | collective-permute-done | bytes 786464 | tf_op jit(solution)/shard_map/ppermute | solution.py:764
  69.3 2.1 %shard_map.217 = bf16[768,512]{1,0:T(8,128)(2,1)} custom-call(s32[1]{0:T(128)} %bitcast.sec, s32[1]{0:T(128)} %bitcast.1.place, f32[768,512]{1,0:T(8,128)S(1)} %get-tuple-element.104.total0, f32[768,512]{1,0:T(8,128)S(1)} %get-tuple-element.103.total1, bf16[768,512]{1,0:T(8,128)(2,1)} %collective-permute-done.12.refs_0_, ...), custom_call_target="tpu_custom_call" | custom-call | bytes 2097152 | tf_op jit(solution)/shard_map/pallas_call | solution.py:786
  71.4 2.1 %collective-permute-start.16 = (bf16[768,512]{1,0:T(8,128)(2,1)}, bf16[768,512]{1,0:T(8,128)(2,1)}, u32[]{:S(2)}, u32[]{:S(2)}) collective-permute-start(bf16[768,512]{1,0:T(8,128)(2,1)} %shard_map.217), channel_id=1, source_target_pairs={{0,2},{1,3},{2,0},{3,1},{4,6},{5,7},{6,4},{7,5},{8,10},{9,11},{10,... | collective-permute-start | bytes 2359304 | tf_op jit(solution)/shard_map/ppermute | solution.py:764
  73.5 0.5 collective-permute-start.5
  74.0 2.5 %collective-permute-done.5.got_sums = f32[24,512]{1,0:T(8,128)S(1)} collective-permute-done((f32[24,512]{1,0:T(8,128)S(1)}, f32[24,512]{1,0:T(8,128)S(1)}, u32[]{:S(2)}, u32[]{:S(2)}) %collective-permute-start.5) | collective-permute-done | bytes 49184 | tf_op jit(solution)/shard_map/ppermute | solution.py:743
  76.5 0.7 shard_map.212
  77.3 2.7 %collective-permute-start.6 = (bf16[32,512]{1,0:T(8,128)(2,1)S(1)}, bf16[32,512]{1,0:T(8,128)(2,1)S(1)}, u32[]{:S(2)}, u32[]{:S(2)}) collective-permute-start(bf16[32,512]{1,0:T(8,128)(2,1)S(1)} %get-tuple-element.70.before), channel_id=1, source_target_pairs={{0,8},{1,9},{2,10},{3,11},{4,12},{5,13},{6,14},{7,15},{8,0},{9,1},... | collective-permute-start | bytes 98312 | tf_op jit(solution)/shard_map/ppermute | solution.py:805
  79.9 2.6 %collective-permute-done.6.after = bf16[32,512]{1,0:T(8,128)(2,1)S(1)} collective-permute-done((bf16[32,512]{1,0:T(8,128)(2,1)S(1)}, bf16[32,512]{1,0:T(8,128)(2,1)S(1)}, u32[]{:S(2)}, u32[]{:S(2)}) %collective-permute-start.6) | collective-permute-done | bytes 32800 | tf_op jit(solution)/shard_map/ppermute | solution.py:805
  82.5 1.3 %collective-permute-start.7 = (bf16[48,512]{1,0:T(8,128)(2,1)S(1)}, bf16[48,512]{1,0:T(8,128)(2,1)S(1)}, u32[]{:S(2)}, u32[]{:S(2)}) collective-permute-start(bf16[48,512]{1,0:T(8,128)(2,1)S(1)} %get-tuple-element.72.before), channel_id=1, source_target_pairs={{0,4},{1,5},{2,6},{3,7},{4,0},{5,1},{6,2},{7,3},{8,12},{9,13},{10,... | collective-permute-start | bytes 147464 | tf_op jit(solution)/shard_map/ppermute | solution.py:805
  83.8 1.1 convert_add_fusion.4.total1
  84.9 0.0 copy-start
  84.9 1.4 %convert_add_fusion.5.total0 = f32[384,512]{1,0:T(8,128)S(1)} fusion(f32[768,512]{1,0:T(8,128)S(1)} %get-tuple-element.104.total0, s32[]{:T(128)S(6)} %select_n.52, bf16[768,512]{1,0:T(8,128)(2,1)} %collective-permute-done.12.refs_0_), kind=kLoop, calls=%fused_computation.9 | loop fusion | flops 393216 | bytes 1966084 | tf_op jit(solution)/shard_map/add | solution.py:852
  86.3 1.2 %shard_map.218 = bf16[384,512]{1,0:T(8,128)(2,1)S(1)} custom-call(s32[1]{0:T(128)} %bitcast.sec, s32[1]{0:T(128)} %bitcast.1.place, f32[384,512]{1,0:T(8,128)S(1)} %convert_add_fusion.5.total0, f32[384,512]{1,0:T(8,128)S(1)} %convert_add_fusion.4.total1, bf16[768,512]{1,0:T(8,128)(2,1)} %collective-permute-done.16.refs_0_), custom_call_target="tpu_custom_call" | custom-call | bytes 2097152 | tf_op jit(solution)/shard_map/pallas_call | solution.py:786
  87.5 0.9 collective-permute-start.17
  88.4 1.6 %collective-permute-start.8 = (bf16[80,512]{1,0:T(8,128)(2,1)S(1)}, bf16[80,512]{1,0:T(8,128)(2,1)S(1)}, u32[]{:S(2)}, u32[]{:S(2)}) collective-permute-start(bf16[80,512]{1,0:T(8,128)(2,1)S(1)} %get-tuple-element.74.before), channel_id=1, source_target_pairs={{0,1},{1,0},{2,3},{3,2},{4,5},{5,4},{6,7},{7,6},{8,9},{9,8},{10,11... | collective-permute-start | bytes 245768 | tf_op jit(solution)/shard_map/ppermute | solution.py:805
  90.0 3.0 %collective-permute-done.8.after = bf16[80,512]{1,0:T(8,128)(2,1)S(1)} collective-permute-done((bf16[80,512]{1,0:T(8,128)(2,1)S(1)}, bf16[80,512]{1,0:T(8,128)(2,1)S(1)}, u32[]{:S(2)}, u32[]{:S(2)}) %collective-permute-start.8) | collective-permute-done | bytes 81952 | tf_op jit(solution)/shard_map/ppermute | solution.py:805
  92.9 0.3 collective-permute-start.9
  93.3 4.9 %collective-permute-done.9.after = bf16[144,512]{1,0:T(8,128)(2,1)S(1)} collective-permute-done((bf16[144,512]{1,0:T(8,128)(2,1)S(1)}, bf16[144,512]{1,0:T(8,128)(2,1)S(1)}, u32[]{:S(2)}, u32[]{:S(2)}) %collective-permute-start.9) | collective-permute-done | bytes 147488 | tf_op jit(solution)/shard_map/ppermute | solution.py:805
  98.2 1.1 shard_map.216
  99.2 1.4 %convert_add_fusion.6 = (f32[192,512]{1,0:T(8,128)S(1)}, f32[192,512]{1,0:T(8,128)S(1)}) fusion(f32[384,512]{1,0:T(8,128)} %copy-done, s32[]{:T(128)S(6)} %select_n.55, bf16[768,512]{1,0:T(8,128)(2,1)} %collective-permute-done.16.refs_0_, s32[]{:T(128)S(6)} %select_n.59, s32[]{:T(128)S(6)} %select_n.56, f32[384,512]{1,0:T(8,128)S(1)} %convert_add_fusion.5.total0), kind=kLoop, calls=%fused_computation.10 | loop fusion | flops 393216 | bytes 1966092 | tf_op jit(solution)/shard_map/add | solution.py:852
  100.7 2.3 %collective-permute-start.18 = (bf16[192,512]{1,0:T(8,128)(2,1)S(1)}, bf16[192,512]{1,0:T(8,128)(2,1)S(1)}, u32[]{:S(2)}, u32[]{:S(2)}) collective-permute-start(bf16[192,512]{1,0:T(8,128)(2,1)S(1)} %shard_map.219), channel_id=1, source_target_pairs={{0,8},{1,9},{2,10},{3,11},{4,12},{5,13},{6,14},{7,15},{8,0},{9,1},... | collective-permute-start | bytes 589832 | tf_op jit(solution)/shard_map/ppermute | solution.py:764
  103.0 1.5 %bitcast_dynamic-update-slice_fusion.1 = bf16[1,8,256,512]{3,2,1,0:T(8,128)(2,1)S(1)} fusion(bf16[1,8,256,512]{3,2,1,0:T(8,128)(2,1)S(1)} %bitcast.31, s32[]{:T(128)S(6)} %select_n.48, bf16[4,256,512]{2,1,0:T(8,128)(2,1)} %collective-permute-done.3), kind=kLoop, calls=%fused_computation.7 | loop fusion | bytes 2097156 | tf_op jit(solution)/shard_map/dynamic_update_slice | solution.py:746
  104.5 0.0 copy-start.5
  104.5 0.1 convert_add_fusion.8
  104.6 4.8 %collective-permute-done.18.came = bf16[192,512]{1,0:T(8,128)(2,1)S(1)} collective-permute-done((bf16[192,512]{1,0:T(8,128)(2,1)S(1)}, bf16[192,512]{1,0:T(8,128)(2,1)S(1)}, u32[]{:S(2)}, u32[]{:S(2)}) %collective-permute-start.18) | collective-permute-done | bytes 196640 | tf_op jit(solution)/shard_map/ppermute | solution.py:764
  109.4 0.1 shard_map.220
  109.5 0.1 collective-permute-start.19
  109.6 1.3 %bitcast_dynamic-update-slice_fusion = bf16[1,8,256,512]{3,2,1,0:T(8,128)(2,1)S(1)} fusion(bf16[1,8,256,512]{3,2,1,0:T(8,128)(2,1)S(1)} %bitcast.32, s32[]{:T(128)S(6)} %select_n.48, bf16[4,256,512]{2,1,0:T(8,128)(2,1)} %collective-permute-done.4), kind=kLoop, calls=%fused_computation.6 | loop fusion | bytes 2097156 | tf_op jit(solution)/shard_map/dynamic_update_slice | solution.py:746
  111.0 0.0 collective-permute-done.19.got
  111.0 0.9 shard_map.221
  111.9 0.5 copy-done.7
  (32 shorter events, 0.1 us)
Async XLA Ops:
  0.6 6.3 %collective-permute-start.1 = (bf16[512,1536]{1,0:T(8,128)(2,1)}, bf16[512,1536]{1,0:T(8,128)(2,1)}, u32[]{:S(2)}, u32[]{:S(2)}) collective-permute-start(bf16[512,1536]{1,0:T(8,128)(2,1)} %bitcast.35), channel_id=1, source_target_pairs={{0,16},{16,0},{1,17},{17,1},{2,18},{18,2},{3,19},{19,3},{4,20},{20... | collective-permute-start | bytes 4718600 | tf_op jit(solution)/shard_map/ppermute | solution.py:635
  1.2 5.7 %collective-permute-start.2 = (bf16[1536,512]{1,0:T(8,128)(2,1)}, bf16[1536,512]{1,0:T(8,128)(2,1)}, u32[]{:S(2)}, u32[]{:S(2)}) collective-permute-start(bf16[1536,512]{1,0:T(8,128)(2,1)} %bitcast.33), channel_id=1, source_target_pairs={{0,16},{16,0},{1,17},{17,1},{2,18},{18,2},{3,19},{19,3},{4,20},{20... | collective-permute-start | bytes 4718600 | tf_op jit(solution)/shard_map/ppermute | solution.py:636
  3.7 3.2 %collective-permute-start = (f32[24,512]{1,0:T(8,128)}, f32[24,512]{1,0:T(8,128)}, u32[]{:S(2)}, u32[]{:S(2)}) collective-permute-start(f32[24,512]{1,0:T(8,128)} %get-tuple-element.56), channel_id=1, source_target_pairs={{0,16},{16,0},{1,17},{17,1},{2,18},{18,2},{3,19},{19,3},{4,20},{20... | collective-permute-start | bytes 147464 | tf_op jit(solution)/shard_map/ppermute | solution.py:633
  42.8 7.7 %copy-start.3 = (bf16[16,96,512]{2,1,0:T(8,128)(2,1)S(1)}, bf16[16,96,512]{2,1,0:T(8,128)(2,1)}, u32[]{:S(2)}) copy-start(bf16[16,96,512]{2,1,0:T(8,128)(2,1)} %get-tuple-element.82) | copy-start | bytes 4718596
  42.8 2.8 %collective-permute-start.14 = (bf16[8,96,512]{2,1,0:T(8,128)(2,1)}, bf16[8,96,512]{2,1,0:T(8,128)(2,1)S(1)}, u32[]{:S(2)}, u32[]{:S(2)}) collective-permute-start(bf16[8,96,512]{2,1,0:T(8,128)(2,1)} %get-tuple-element.91), channel_id=1, source_target_pairs={{0,16},{16,0},{1,17},{17,1},{2,18},{18,2},{3,19},{19,3},{4,20},{20... | collective-permute-start | bytes 2359304 | tf_op jit(solution)/shard_map/ppermute | solution.py:703
  43.5 7.1 %collective-permute-start.11 = (bf16[8,96,512]{2,1,0:T(8,128)(2,1)}, bf16[8,96,512]{2,1,0:T(8,128)(2,1)S(1)}, u32[]{:S(2)}, u32[]{:S(2)}) collective-permute-start(bf16[8,96,512]{2,1,0:T(8,128)(2,1)} %get-tuple-element.86), channel_id=1, source_target_pairs={{0,16},{16,0},{1,17},{17,1},{2,18},{18,2},{3,19},{19,3},{4,20},{20... | collective-permute-start | bytes 2359304 | tf_op jit(solution)/shard_map/ppermute | solution.py:703
  43.6 18.1 %collective-permute-start.13 = (bf16[8,96,512]{2,1,0:T(8,128)(2,1)}, bf16[8,96,512]{2,1,0:T(8,128)(2,1)}, u32[]{:S(2)}, u32[]{:S(2)}) collective-permute-start(bf16[8,96,512]{2,1,0:T(8,128)(2,1)} %get-tuple-element.88), channel_id=1, source_target_pairs={{0,16},{16,0},{1,17},{17,1},{2,18},{18,2},{3,19},{19,3},{4,20},{20... | collective-permute-start | bytes 2359304 | tf_op jit(solution)/shard_map/ppermute | solution.py:703
  44.0 17.7 %collective-permute-start.10 = (bf16[8,96,512]{2,1,0:T(8,128)(2,1)}, bf16[8,96,512]{2,1,0:T(8,128)(2,1)}, u32[]{:S(2)}, u32[]{:S(2)}) collective-permute-start(bf16[8,96,512]{2,1,0:T(8,128)(2,1)} %get-tuple-element.83), channel_id=1, source_target_pairs={{0,16},{16,0},{1,17},{17,1},{2,18},{18,2},{3,19},{19,3},{4,20},{20... | collective-permute-start | bytes 2359304 | tf_op jit(solution)/shard_map/ppermute | solution.py:703
  47.9 16.2 %collective-permute-start.15 = (bf16[768,512]{1,0:T(8,128)(2,1)}, bf16[768,512]{1,0:T(8,128)(2,1)}, u32[]{:S(2)}, u32[]{:S(2)}) collective-permute-start(bf16[768,512]{1,0:T(8,128)(2,1)} %fusion), channel_id=1, source_target_pairs={{0,1},{1,0},{2,3},{3,2},{4,5},{5,4},{6,7},{7,6},{8,9},{9,8},{10,11... | collective-permute-start | bytes 2359304 | tf_op jit(solution)/shard_map/ppermute | solution.py:764
  51.7 17.6 %collective-permute-start.12 = (bf16[768,512]{1,0:T(8,128)(2,1)}, bf16[768,512]{1,0:T(8,128)(2,1)}, u32[]{:S(2)}, u32[]{:S(2)}) collective-permute-start(bf16[768,512]{1,0:T(8,128)(2,1)} %fusion.1), channel_id=1, source_target_pairs={{0,1},{1,0},{2,3},{3,2},{4,5},{5,4},{6,7},{7,6},{8,9},{9,8},{10,11... | collective-permute-start | bytes 2359304 | tf_op jit(solution)/shard_map/ppermute | solution.py:764
  69.3 4.2 %copy-start.8 = (f32[24,512]{1,0:T(8,128)S(1)}, f32[24,512]{1,0:T(8,128)}, u32[]{:S(2)}) copy-start(f32[24,512]{1,0:T(8,128)} %get-tuple-element.69) | copy-start | bytes 147460
  69.3 7.2 %copy-start.1 = (f32[24,512]{1,0:T(8,128)S(1)}, f32[24,512]{1,0:T(8,128)}, u32[]{:S(2)}) copy-start(f32[24,512]{1,0:T(8,128)} %get-tuple-element.68.own_sums) | copy-start | bytes 147460
  69.3 7.2 %copy-start.2 = (s32[8]{0:T(128)S(1)}, s32[8]{0:T(128)}, u32[]{:S(2)}) copy-start(s32[8]{0:T(128)} %speaker.3) | copy-start | bytes 100
  71.4 14.9 %collective-permute-start.16 = (bf16[768,512]{1,0:T(8,128)(2,1)}, bf16[768,512]{1,0:T(8,128)(2,1)}, u32[]{:S(2)}, u32[]{:S(2)}) collective-permute-start(bf16[768,512]{1,0:T(8,128)(2,1)} %shard_map.217), channel_id=1, source_target_pairs={{0,2},{1,3},{2,0},{3,1},{4,6},{5,7},{6,4},{7,5},{8,10},{9,11},{10,... | collective-permute-start | bytes 2359304 | tf_op jit(solution)/shard_map/ppermute | solution.py:764
  73.5 29.5 %collective-permute-start.3 = (bf16[4,256,512]{2,1,0:T(8,128)(2,1)}, bf16[4,256,512]{2,1,0:T(8,128)(2,1)}, u32[]{:S(2)}, u32[]{:S(2)}) collective-permute-start(bf16[4,256,512]{2,1,0:T(8,128)(2,1)} %get-tuple-element.58), channel_id=1, source_target_pairs={{0,16},{16,0},{1,17},{17,1},{2,18},{18,2},{3,19},{19,3},{4,20},{20... | collective-permute-start | bytes 3145736 | tf_op jit(solution)/shard_map/ppermute | solution.py:705
  73.5 3.0 %collective-permute-start.5 = (f32[24,512]{1,0:T(8,128)S(1)}, f32[24,512]{1,0:T(8,128)S(1)}, u32[]{:S(2)}, u32[]{:S(2)}) collective-permute-start(f32[24,512]{1,0:T(8,128)S(1)} %copy-done.8), channel_id=1, source_target_pairs={{0,16},{16,0},{1,17},{17,1},{2,18},{18,2},{3,19},{19,3},{4,20},{20... | collective-permute-start | bytes 147464 | tf_op jit(solution)/shard_map/ppermute | solution.py:743
  77.3 5.2 %collective-permute-start.6 = (bf16[32,512]{1,0:T(8,128)(2,1)S(1)}, bf16[32,512]{1,0:T(8,128)(2,1)S(1)}, u32[]{:S(2)}, u32[]{:S(2)}) collective-permute-start(bf16[32,512]{1,0:T(8,128)(2,1)S(1)} %get-tuple-element.70.before), channel_id=1, source_target_pairs={{0,8},{1,9},{2,10},{3,11},{4,12},{5,13},{6,14},{7,15},{8,0},{9,1},... | collective-permute-start | bytes 98312 | tf_op jit(solution)/shard_map/ppermute | solution.py:805
  79.9 29.7 %collective-permute-start.4 = (bf16[4,256,512]{2,1,0:T(8,128)(2,1)}, bf16[4,256,512]{2,1,0:T(8,128)(2,1)}, u32[]{:S(2)}, u32[]{:S(2)}) collective-permute-start(bf16[4,256,512]{2,1,0:T(8,128)(2,1)} %get-tuple-element.67), channel_id=1, source_target_pairs={{0,16},{16,0},{1,17},{17,1},{2,18},{18,2},{3,19},{19,3},{4,20},{20... | collective-permute-start | bytes 3145736 | tf_op jit(solution)/shard_map/ppermute | solution.py:742
  82.5 5.9 %collective-permute-start.7 = (bf16[48,512]{1,0:T(8,128)(2,1)S(1)}, bf16[48,512]{1,0:T(8,128)(2,1)S(1)}, u32[]{:S(2)}, u32[]{:S(2)}) collective-permute-start(bf16[48,512]{1,0:T(8,128)(2,1)S(1)} %get-tuple-element.72.before), channel_id=1, source_target_pairs={{0,4},{1,5},{2,6},{3,7},{4,0},{5,1},{6,2},{7,3},{8,12},{9,13},{10,... | collective-permute-start | bytes 147464 | tf_op jit(solution)/shard_map/ppermute | solution.py:805
  84.9 2.6 %copy-start = (f32[384,512]{1,0:T(8,128)}, f32[384,512]{1,0:T(8,128)S(1)}, u32[]{:S(2)}) copy-start(f32[384,512]{1,0:T(8,128)S(1)} %convert_add_fusion.4.total1) | copy-start | bytes 2359300
  87.5 13.1 %collective-permute-start.17 = (bf16[384,512]{1,0:T(8,128)(2,1)S(1)}, bf16[384,512]{1,0:T(8,128)(2,1)S(1)}, u32[]{:S(2)}, u32[]{:S(2)}) collective-permute-start(bf16[384,512]{1,0:T(8,128)(2,1)S(1)} %shard_map.218), channel_id=1, source_target_pairs={{0,4},{1,5},{2,6},{3,7},{4,0},{5,1},{6,2},{7,3},{8,12},{9,13},{10,... | collective-permute-start | bytes 1179656 | tf_op jit(solution)/shard_map/ppermute | solution.py:764
  88.4 4.5 %collective-permute-start.8 = (bf16[80,512]{1,0:T(8,128)(2,1)S(1)}, bf16[80,512]{1,0:T(8,128)(2,1)S(1)}, u32[]{:S(2)}, u32[]{:S(2)}) collective-permute-start(bf16[80,512]{1,0:T(8,128)(2,1)S(1)} %get-tuple-element.74.before), channel_id=1, source_target_pairs={{0,1},{1,0},{2,3},{3,2},{4,5},{5,4},{6,7},{7,6},{8,9},{9,8},{10,11... | collective-permute-start | bytes 245768 | tf_op jit(solution)/shard_map/ppermute | solution.py:805
  92.9 5.2 %collective-permute-start.9 = (bf16[144,512]{1,0:T(8,128)(2,1)S(1)}, bf16[144,512]{1,0:T(8,128)(2,1)S(1)}, u32[]{:S(2)}, u32[]{:S(2)}) collective-permute-start(bf16[144,512]{1,0:T(8,128)(2,1)S(1)} %get-tuple-element.76.before), channel_id=1, source_target_pairs={{0,2},{1,3},{2,0},{3,1},{4,6},{5,7},{6,4},{7,5},{8,10},{9,11},{10,... | collective-permute-start | bytes 442376 | tf_op jit(solution)/shard_map/ppermute | solution.py:805
  99.2 3.8 %copy-start.4 = (bf16[8,256,512]{2,1,0:T(8,128)(2,1)S(1)}, bf16[8,256,512]{2,1,0:T(8,128)(2,1)}, u32[]{:S(2)}) copy-start(bf16[8,256,512]{2,1,0:T(8,128)(2,1)} %get-tuple-element.57) | copy-start | bytes 6291460
  100.7 8.7 %collective-permute-start.18 = (bf16[192,512]{1,0:T(8,128)(2,1)S(1)}, bf16[192,512]{1,0:T(8,128)(2,1)S(1)}, u32[]{:S(2)}, u32[]{:S(2)}) collective-permute-start(bf16[192,512]{1,0:T(8,128)(2,1)S(1)} %shard_map.219), channel_id=1, source_target_pairs={{0,8},{1,9},{2,10},{3,11},{4,12},{5,13},{6,14},{7,15},{8,0},{9,1},... | collective-permute-start | bytes 589832 | tf_op jit(solution)/shard_map/ppermute | solution.py:764
  103.0 6.6 %copy-start.6 = (bf16[8,256,512]{2,1,0:T(8,128)(2,1)S(1)}, bf16[8,256,512]{2,1,0:T(8,128)(2,1)}, u32[]{:S(2)}) copy-start(bf16[8,256,512]{2,1,0:T(8,128)(2,1)} %get-tuple-element.66) | copy-start | bytes 6291460
  104.5 6.4 %copy-start.5 = (bf16[1,8,256,512]{3,2,1,0:T(8,128)(2,1)}, bf16[1,8,256,512]{3,2,1,0:T(8,128)(2,1)S(1)}, u32[]{:S(2)}) copy-start(bf16[1,8,256,512]{3,2,1,0:T(8,128)(2,1)S(1)} %bitcast_dynamic-update-slice_fusion.1) | copy-start | bytes 6291460
  109.5 1.5 %collective-permute-start.19 = (f32[96,512]{1,0:T(8,128)S(1)}, f32[96,512]{1,0:T(8,128)S(1)}, u32[]{:S(2)}, u32[]{:S(2)}) collective-permute-start(f32[96,512]{1,0:T(8,128)S(1)} %get-tuple-element.93), channel_id=1, source_target_pairs={{0,16},{16,0},{1,17},{17,1},{2,18},{18,2},{3,19},{19,3},{4,20},{20... | collective-permute-start | bytes 589832 | tf_op jit(solution)/shard_map/ppermute | solution.py:859
  111.0 1.4 %copy-start.7 = (bf16[1,8,256,512]{3,2,1,0:T(8,128)(2,1)}, bf16[1,8,256,512]{3,2,1,0:T(8,128)(2,1)S(1)}, u32[]{:S(2)}) copy-start(bf16[1,8,256,512]{3,2,1,0:T(8,128)(2,1)S(1)} %bitcast_dynamic-update-slice_fusion) | copy-start | bytes 6291460
